TPU v7x, 32 devices: a whole 2x2x4 slice. The times are simulated.
32 devices in a mesh: seq: 16 (over z, y, x), pair: 2 (over core).
Axes of the slice: x: 2, y: 2, z: 4, core: 2. Of those that a mesh axis runs over, the one named last changes fastest.
Arguments:
- tokens_in: bfloat16 [4096, 1024], P(('seq', 'pair')), may hold values from -6 to 6
- queries: bfloat16 [4096, 1024], P(('seq', 'pair')), may hold values from -500 to 500
- key_value: bfloat16 [4096, 128], P(('seq', 'pair')), may hold values from -6 to 6
- out_grad: bfloat16 [4096, 1024], P(('seq', 'pair')), may hold values from -4 to 4
- cluster_of: int32 [4096, 16], P(('seq', 'pair')), may hold values from 0 to 127, as said below
- slot_of: int32 [4096, 16], P(('seq', 'pair')), may hold values from 0 to 1023, as said below
Outputs:
- weight_grad: float32 [1024, 1024], P(('seq', 'pair'))
Inputs may be any that keep to these rules, and one draw needn't show every extreme that they name: `cluster_of`: cluster c belongs to owner group c // 8. Of the 2048 rows of one aligned block of 128 tokens, at most 256 name clusters of one owner group; in every draw some owner group receives exactly 256 rows from every block of even index and some from every block of odd index. No two rows share a cluster and a slot. Rows of the k-th aligned block of 128 tokens take slots of half k % 2, that is slot_of // 512 == k % 2. Half of all slots have a member in all; single clusters hold more or fewer.
All inputs are finite; a program needn't handle non-finite values.
Results may differ from a plain program's by a relative error of at most 0.0041.
Values may be sent and summed in bfloat16 or wider, within the bound.
No kernel may reach another device: no remote copies, remote signals or barrier semaphores. Data moves between devices by JAX's collectives and lax.ppermute only.
A program may use at most 64 MiB of HBM per device.

v0:
```python
import jax
import jax.numpy as jnp
from jax import lax
from jax.sharding import PartitionSpec as P

H = 16
HD = 64
HALF = 512
CL_DEV = 8


def cluster_grad(query_part, key_part, live_keys):
    score_scale = HD ** (-0.5)
    query_rows = query_part[:, :HD]
    grad_rows = query_part[:, HD:]
    key_rows = key_part[:, :HD]
    value_rows = key_part[:, HD:]
    scores = jnp.dot(query_rows, key_rows.T, preferred_element_type=jnp.float32) * score_scale
    scores = jnp.where(live_keys[None, :] > 0, scores, jnp.float32(-1e30))
    row_max = jnp.max(scores, axis=1, keepdims=True)
    weights = jnp.exp(scores - row_max)
    probs = weights / jnp.sum(weights, axis=1, keepdims=True)
    prob_grad = jnp.dot(grad_rows, value_rows.T, preferred_element_type=jnp.float32)
    row_dot = jnp.sum(probs * prob_grad, axis=1, keepdims=True)
    score_grad = (probs * (prob_grad - row_dot) * score_scale).astype(jnp.bfloat16)
    return jnp.dot(score_grad, key_rows, preferred_element_type=jnp.float32).astype(jnp.bfloat16)


def on_device(tokens_in, queries, key_value, out_grad, cluster_of, slot_of):
    groups = lax.axis_size("seq")
    tok_count = queries.shape[0]
    row_count = tok_count * H
    bound_rows = 2 * row_count // groups
    slot_count = CL_DEV * HALF
    owners = (cluster_of // CL_DEV).reshape(row_count)
    local_slot = (cluster_of % CL_DEV * HALF + slot_of % HALF).reshape(row_count)
    picked = (owners[:, None] == jnp.arange(groups, dtype=jnp.int32)[None, :]).astype(jnp.int32)
    ranked = jnp.sum(jnp.cumsum(picked, axis=0) * picked, axis=1) - 1
    cell_index = owners * bound_rows + ranked
    paired_rows = jnp.concatenate(
        [queries.reshape(row_count, HD), out_grad.reshape(row_count, HD)], axis=1
    )
    packed = jnp.concatenate([paired_rows, jnp.repeat(key_value, H, axis=0)], axis=1)
    outgoing = jnp.zeros((groups * bound_rows, 4 * HD), jnp.bfloat16).at[cell_index].set(packed)
    labels = jnp.full((groups * bound_rows,), -1, jnp.int32).at[cell_index].set(local_slot)
    incoming, labels_in = (
        lax.all_to_all(
            outgoing.reshape(groups, bound_rows, 4 * HD),
            "seq",
            split_axis=0,
            concat_axis=0,
            tiled=True,
        ),
        lax.all_to_all(
            labels.reshape(groups, bound_rows), "seq", split_axis=0, concat_axis=0, tiled=True
        ),
    )
    target = labels_in.reshape(groups * bound_rows)
    target_safe = jnp.where(target >= 0, target, slot_count)
    arranged = (
        jnp.zeros((slot_count, 4 * HD), jnp.bfloat16)
        .at[target_safe]
        .set(incoming.reshape(groups * bound_rows, 4 * HD), mode="drop")
    )
    live_slot = (
        jnp.zeros((slot_count,), jnp.bfloat16)
        .at[target_safe]
        .set(jnp.ones((groups * bound_rows,), jnp.bfloat16), mode="drop")
    )
    arranged = arranged.reshape(CL_DEV, HALF, 4 * HD)
    keys_all, live_all = (
        lax.all_gather(arranged[:, :, 2 * HD :], "pair", axis=1, tiled=True),
        lax.all_gather(live_slot.reshape(CL_DEV, HALF), "pair", axis=1, tiled=True),
    )

    def per_cluster(operands):
        return cluster_grad(operands[0], operands[1], operands[2])

    cluster_grads = lax.map(per_cluster, (arranged[:, :, : 2 * HD], keys_all, live_all))
    slot_grads = cluster_grads.reshape(slot_count, HD)
    going_back = jnp.where(
        target[:, None] >= 0,
        slot_grads[jnp.minimum(target_safe, slot_count - 1)],
        jnp.zeros((), jnp.bfloat16),
    )
    returned = lax.all_to_all(
        going_back.reshape(groups, bound_rows // 2, 2 * HD),
        "seq",
        split_axis=0,
        concat_axis=0,
        tiled=True,
    )
    query_grad = returned.reshape(groups * bound_rows, HD)[cell_index].reshape(tok_count, H * HD)
    partial_rows = lax.psum_scatter(
        lax.dot_general(
            tokens_in, query_grad, (((0,), (0,)), ((), ())), preferred_element_type=jnp.float32
        ),
        "seq",
        scatter_dimension=0,
        tiled=True,
    )
    result = lax.psum_scatter(partial_rows, "pair", scatter_dimension=0, tiled=True)
    return result


def solution(mesh):
    return jax.shard_map(
        on_device,
        mesh=mesh,
        in_specs=(
            P(("seq", "pair"), None),
            P(("seq", "pair"), None),
            P(("seq", "pair"), None),
            P(("seq", "pair"), None),
            P(("seq", "pair"), None),
            P(("seq", "pair"), None),
        ),
        out_specs=P(("seq", "pair"), None),
        check_vma=False,
    )
```

profile of v0, /device:TPU:0, one launch (start us, length us, event | category | flops | bytes accessed | tf_op | source)
XLA Modules:
  0.0 343.1 jit_solution(14554870113099850528)
XLA Ops:
  6.5 0.8 broadcast_multiply_fusion
  8.0 4.5 %reduce-window.6 = s32[16,16,128]{2,1,0:T(8,128)S(1)} reduce-window(s32[16,16,128]{2,1,0:T(8,128)S(1)} %fusion.27, s32[]{:T(128)} %copy.66), window={size=1x1x128 pad=0_0x0_0x127_0}, to_apply=%region_0.1 | reduce-window | flops 4161536 | bytes 262148 | tf_op jit(solution)/shard_map/reduce-window
  13.4 8.6 %scatter_custom_fusion = s32[4096]{0:T(1024)} fusion(s32[2048]{0:T(1024)S(1)} %bitcast.60, s32[2048]{0:T(1024)S(1)} %reshape.186, s32[]{:T(128)} %constant.76.clone.1), kind=kCustom, calls=%fused_computation.66 | custom fusion | bytes 16388 | tf_op jit(solution)/shard_map/scatter | solution.py:45
  22.0 8.3 %all-to-all-start = ((s32[16,1,256]{2,1,0:T(1,128)}), s32[16,1,256]{2,1,0:T(1,128)S(1)}, u32[]{:S(2)}, u32[]{:S(2)}) async-start(s32[16,1,256]{2,1,0:T(1,128)} %bitcast.6), calls=%async_computation | async-start | bytes 32768 | tf_op jit(solution)/shard_map/all_to_all | solution.py:54
  30.3 1.3 reshape.157
  32.1 11.5 %scatter_custom_fusion.2 = bf16[4096,256]{1,0:T(8,128)(2,1)} fusion(s32[2048]{0:T(1024)S(1)} %bitcast.61, bf16[2048,128]{1,0:T(8,128)(2,1)S(1)} %bitcast.56, bf16[]{:T(256)} %constant.91, bf16[2048,64]{1,0:T(8,128)(2,1)S(1)} %reshape.158, bf16[2048,64]{1,0:T(8,128)(2,1)S(1)} %reshape.157, bf16[]{:T(256)} %constant.86.clone.1), kind=kCustom, calls=%fused_computation.30 | custom fusion | flops 3145728 | bytes 3670020 | tf_op jit(solution)/shard_map/scatter | solution.py:44
  43.7 6.9 %all-to-all-start.1 = ((bf16[16,256,256]{2,1,0:T(8,128)(2,1)}), bf16[16,256,256]{2,1,0:T(8,128)(2,1)S(1)}, u32[]{:S(2)}, u32[]{:S(2)}) async-start(bf16[16,256,256]{2,1,0:T(8,128)(2,1)} %bitcast.11), calls=%async_computation.1 | async-start | bytes 4194304 | tf_op jit(solution)/shard_map/all_to_all | solution.py:47
  50.7 42.6 %all-to-all-done.1 = bf16[16,256,256]{2,1,0:T(8,128)(2,1)S(1)} async-done(((bf16[16,256,256]{2,1,0:T(8,128)(2,1)}), bf16[16,256,256]{2,1,0:T(8,128)(2,1)S(1)}, u32[]{:S(2)}, u32[]{:S(2)}) %all-to-all-start.1) | async-done | bytes 2097184 | tf_op jit(solution)/shard_map/all_to_all | solution.py:47
  93.3 1.3 copy-done.1
  94.7 19.0 %scatter_custom_fusion.3 = bf16[4096,256]{1,0:T(8,128)(2,1)S(1)} fusion(s32[4096]{0:T(1024)S(1)} %bitcast.65, bf16[4096,256]{1,0:T(8,128)(2,1)} %bitcast.55, bf16[]{:T(256)} %constant.86.clone.1), kind=kCustom, calls=%fused_computation.36 | custom fusion | bytes 2097664 | tf_op jit(solution)/shard_map/scatter | solution.py:63
  113.7 1.5 fusion.37
  115.6 28.6 %scatter_custom_fusion.1 = bf16[4096]{0:T(1024)(128)(2,1)S(1)} fusion(s32[4096]{0:T(1024)S(1)} %bitcast.66, bf16[4096]{0:T(1024)(128)(2,1)S(1)} %broadcast.158, bf16[]{:T(256)} %constant.86.clone.1), kind=kCustom, calls=%fused_computation.71 | custom fusion | bytes 8194 | tf_op jit(solution)/shard_map/scatter | solution.py:68
  144.2 1.8 all_gather.6
  146.1 32.5 %while.10 = (s32[]{:T(128)}, bf16[8,512,64]{1,2,0:T(8,128)(2,1)S(1)}, bf16[8,1024]{1,0:T(8,128)(2,1)S(1)}, bf16[8,512,128]{2,1,0:T(8,128)(2,1)S(1)}, bf16[8,1024,128]{2,1,0:T(8,128)(2,1)}, /*index=5*/s32[]{:T(128)}) while((s32[]{:T(128)}, bf16[8,512,64]{1,2,0:T(8,128)(2,1)S(1)}, bf16[8,1024]{1,0:T(8,128)(2,1)S(1)}, ...), condition=%wide.region_11.12_spmd, body=%wide.region_7.11_spmd.sunk | while | flops 212370944 | bytes 14509149 | solution.py:79
  146.2 1.0 dynamic-slice_bitcast_fusion.4
  147.1 0.5 fusion.45
  147.7 0.6 fusion.46
  148.3 0.9 multiply_reduce_fusion.2
  149.1 1.0 fusion.47
  150.2 1.0 dynamic-slice_bitcast_fusion.4
  151.2 0.5 fusion.45
  151.7 0.6 fusion.46
  152.3 0.9 multiply_reduce_fusion.2
  153.2 1.0 fusion.47
  154.3 1.0 dynamic-slice_bitcast_fusion.4
  155.3 0.5 fusion.45
  155.8 0.6 fusion.46
  156.4 0.9 multiply_reduce_fusion.2
  157.2 1.0 fusion.47
  158.3 1.0 dynamic-slice_bitcast_fusion.4
  159.3 0.5 fusion.45
  159.8 0.6 fusion.46
  160.4 0.9 multiply_reduce_fusion.2
  161.3 1.0 fusion.47
  162.4 1.0 dynamic-slice_bitcast_fusion.4
  163.4 0.5 fusion.45
  163.9 0.6 fusion.46
  164.5 0.9 multiply_reduce_fusion.2
  165.3 1.0 fusion.47
  166.4 1.0 dynamic-slice_bitcast_fusion.4
  167.4 0.5 fusion.45
  167.9 0.6 fusion.46
  168.5 0.9 multiply_reduce_fusion.2
  169.4 1.0 fusion.47
  170.5 1.0 dynamic-slice_bitcast_fusion.4
  171.5 0.5 fusion.45
  172.0 0.6 fusion.46
  172.6 0.9 multiply_reduce_fusion.2
  173.5 1.0 fusion.47
  174.6 1.0 dynamic-slice_bitcast_fusion.4
  175.5 0.5 fusion.45
  176.1 0.6 fusion.46
  176.6 0.9 multiply_reduce_fusion.2
  177.5 1.0 fusion.47
  179.0 12.1 %gather_fusion = bf16[4096,64]{1,0:T(8,128)(2,1)S(1)} fusion(bf16[4096,64]{1,0:T(8,128)(2,1)S(1)} %bitcast.53, s32[4096]{0:T(1024)S(1)} %broadcast_clamp_fusion), kind=kCustom, calls=%fused_computation | custom fusion | bytes 1064960 | tf_op jit(solution)/shard_map/gather | solution.py:83
  191.2 0.5 gather.9
  192.0 0.8 bitcast_select_fusion
  192.8 9.8 %all-to-all-start.2 = ((bf16[16,128,128]{1,2,0:T(8,128)(2,1)}), bf16[16,128,128]{1,2,0:T(8,128)(2,1)S(1)}, u32[]{:S(2)}, u32[]{:S(2)}) async-start(bf16[16,128,128]{1,2,0:T(8,128)(2,1)} %bitcast_select_fusion), calls=%async_computation.2 | async-start | bytes 1048576 | tf_op jit(solution)/shard_map/all_to_all | solution.py:86
  202.7 15.3 %all-to-all-done.2 = bf16[16,128,128]{1,2,0:T(8,128)(2,1)S(1)} async-done(((bf16[16,128,128]{1,2,0:T(8,128)(2,1)}), bf16[16,128,128]{1,2,0:T(8,128)(2,1)S(1)}, u32[]{:S(2)}, u32[]{:S(2)}) %all-to-all-start.2) | async-done | bytes 524320 | tf_op jit(solution)/shard_map/all_to_all | solution.py:86
  218.7 6.2 %gather_fusion.1 = bf16[2048,64]{1,0:T(8,128)(2,1)S(1)} fusion(bf16[4096,64]{1,0:T(8,128)(2,1)S(1)} %reshape.164, s32[2048]{0:T(1024)S(1)} %broadcast_clamp_fusion.1), kind=kCustom, calls=%fused_computation.1 | custom fusion | bytes 532480 | tf_op jit(solution)/shard_map/gather | solution.py:93
  225.2 2.7 convolution_bitcast_fusion
  227.9 5.3 %copy.51 = f32[1024,1024]{1,0:T(8,128)} copy(f32[1024,1024]{0,1:T(8,128)} %convolution_bitcast_fusion) | data formatting | bytes 8388608
  233.3 93.7 %reduce-scatter.7.cloned.1.call-done = f32[64,1024]{1,0:T(8,128)} async-done(((f32[1024,1024]{1,0:T(8,128)}), f32[64,1024]{1,0:T(8,128)}) %reduce-scatter.7.cloned.1.call-update) | async-done | bytes 262160
  327.1 9.5 %reduce-scatter.9.cloned.1.call-done = f32[32,1024]{1,0:T(8,128)} async-done(((f32[64,1024]{1,0:T(8,128)}), f32[32,1024]{1,0:T(8,128)}) %reduce-scatter.9.cloned.1.call-update) | async-done | bytes 131088 | tf_op jit(solution)/shard_map/reduce_scatter | solution.py:102
  (62 shorter events, 4.6 us)
Async XLA Ops:
  6.5 218.7 %copy-start = (bf16[128,1024]{1,0:T(8,128)(2,1)S(1)}, bf16[128,1024]{1,0:T(8,128)(2,1)}, u32[]{:S(2)}) copy-start(bf16[128,1024]{1,0:T(8,128)(2,1)} %param.8) | copy-start | bytes 786436
  6.5 25.1 %copy-start.2 = (bf16[128,1024]{1,0:T(8,128)(2,1)S(1)}, bf16[128,1024]{1,0:T(8,128)(2,1)}, u32[]{:S(2)}) copy-start(bf16[128,1024]{1,0:T(8,128)(2,1)} %param.11) | copy-start | bytes 786436
  6.5 25.5 %copy-start.3 = (bf16[128,128]{1,0:T(8,128)(2,1)S(1)}, bf16[128,128]{1,0:T(8,128)(2,1)}, u32[]{:S(2)}) copy-start(bf16[128,128]{1,0:T(8,128)(2,1)} %param.10) | copy-start | bytes 98308
  22.0 21.7 %all-to-all-start = ((s32[16,1,256]{2,1,0:T(1,128)}), s32[16,1,256]{2,1,0:T(1,128)S(1)}, u32[]{:S(2)}, u32[]{:S(2)}) async-start(s32[16,1,256]{2,1,0:T(1,128)} %bitcast.6), calls=%async_computation | async-start | bytes 32768 | tf_op jit(solution)/shard_map/all_to_all | solution.py:54
  43.7 49.6 %all-to-all-start.1 = ((bf16[16,256,256]{2,1,0:T(8,128)(2,1)}), bf16[16,256,256]{2,1,0:T(8,128)(2,1)S(1)}, u32[]{:S(2)}, u32[]{:S(2)}) async-start(bf16[16,256,256]{2,1,0:T(8,128)(2,1)} %bitcast.11), calls=%async_computation.1 | async-start | bytes 4194304 | tf_op jit(solution)/shard_map/all_to_all | solution.py:47
  50.6 95.5 %all-gather.2.cloned.1.call-start = ((), (), s32[]{:S(2)}) async-start(), calls=%async_computation.5 | async-start | bytes 3145728 | tf_op jit(solution)/shard_map/all_gather | solution.py:72
  93.3 1.4 copy-start.1
  192.8 25.2 %all-to-all-start.2 = ((bf16[16,128,128]{1,2,0:T(8,128)(2,1)}), bf16[16,128,128]{1,2,0:T(8,128)(2,1)S(1)}, u32[]{:S(2)}, u32[]{:S(2)}) async-start(bf16[16,128,128]{1,2,0:T(8,128)(2,1)} %bitcast_select_fusion), calls=%async_computation.2 | async-start | bytes 1048576 | tf_op jit(solution)/shard_map/all_to_all | solution.py:86
  202.6 124.4 %reduce-scatter.7.cloned.1.call-start = ((), (), s32[]{:S(2)}) async-start(), calls=%async_computation.6 | async-start | bytes 4456448
  233.3 103.3 %reduce-scatter.9.cloned.1.call-start = ((), (), s32[]{:S(2)}) async-start(), calls=%async_computation.7 | async-start | bytes 393216 | tf_op jit(solution)/shard_map/reduce_scatter | solution.py:102
Sparse Core Ops, SparseCore 0:
  115.4 14.7 all-gather.1
  233.4 93.5 reduce-scatter.6
  329.3 7.2 reduce-scatter.8
where the time goes:
time: 344 us; the launch traced here: 343 us
  waiting for transfers between devices  161 us (47%)
  local copies, waits for them, and re-layouts  96.2 us (28%)
  starting transfers between devices  25.2 us (7%)
  other arithmetic  23 us (7%)
  matrix products  22.1 us (6%)
  between operations  13.4 us (4%)
    unnamed x4, waiting for transfers between devices  93.8 us
    all_to_all x1, waiting for transfers between devices, on_device(): lax.all_to_all(outgoing.reshape(groups, bound_rows, 4 * HD), 'seq', split...  42.6 us
    scatter x1, local copies, waits for them, and re-layouts, on_device(): live_slot = jnp.zeros((slot_count,), jnp.bfloat16).at[target_safe].set(jn...  28.6 us
    scatter x1, local copies, waits for them, and re-layouts, on_device(): arranged = jnp.zeros((slot_count, 4 * HD), jnp.bfloat16).at[target_safe]....  19 us
    all_to_all x1, waiting for transfers between devices, on_device(): lax.all_to_all(going_back.reshape(groups, bound_rows // 2, 2 * HD), 'seq'...  15.3 us
    gather x3, local copies, waits for them, and re-layouts, on_device(): slot_grads[jnp.minimum(target_safe, slot_count - 1)]  12.9 us
    scatter x1, other arithmetic, on_device(): jnp.zeros((groups * bound_rows, 4 * HD), jnp.bfloat16).at[cell_index]  11.5 us
    all_to_all x1, starting transfers between devices, on_device(): lax.all_to_all(going_back.reshape(groups, bound_rows // 2, 2 * HD), 'seq'...  9.79 us
  transfers between devices with their start and end apart: 6, of which 4 were waited for; matrix products, arithmetic and copies ran while one was open for 12% of the time, Pallas kernels for 0%

commit v1 on v0

v1 whole, which is shorter than its diff:
```python
import jax
import jax.numpy as jnp
from jax import lax
from jax.experimental import pallas as pl
from jax.experimental.pallas import tpu as pltpu
from jax.sharding import PartitionSpec as P

H = 16
HD = 64
HALF = 512
CL_DEV = 8
SCALE = HD ** (-0.5)
LOG2E = 1.4426950408889634
TILE = 512


def attend_kernel(q_ref, g_ref, cl_ref, *refs):
    kv_refs = refs[:-6]
    out_ref, rhs, val, key, sc, pg = refs[-6:]
    pair = pl.program_id(0)
    tok = q_ref.shape[0]
    lanes = 2 * HD
    clusters = (rhs.shape[0] - lanes) // 2
    total = rhs.shape[1]
    tiles = total // TILE

    @pl.when(pair == 0)
    def _():
        ids = lax.broadcasted_iota(jnp.int32, (clusters, tok), 0).astype(jnp.float32)
        at = 0
        for kv_ref in kv_refs:
            for j in range(kv_ref.shape[0]):
                cols = pl.ds(at, tok)
                kt = kv_ref[j, 0:HD, :]
                vt = kv_ref[j, HD : 2 * HD, :]
                cl = kv_ref[j, 2 * HD : 2 * HD + H, :].astype(jnp.float32)
                rhs[0:HD, cols] = kt
                rhs[HD : 2 * HD, cols] = kt
                val[0:HD, cols] = vt
                val[HD : 2 * HD, cols] = vt
                k2 = jnp.concatenate([kt, kt], axis=0).astype(jnp.float32)
                key[cols, :] = k2.T.astype(jnp.bfloat16)
                count = jnp.zeros((clusters, tok), jnp.float32)
                for h in range(H):
                    count += jnp.where(cl[h : h + 1, :] == ids, 1.0, 0.0)
                bias = jnp.where(
                    count > 0.0, jnp.log(jnp.maximum(count, 1.0)) * (1.0 / SCALE), -1e30
                )
                hi = bias.astype(jnp.bfloat16)
                lo = bias - hi.astype(jnp.float32)
                lo = jnp.where(count > 0.0, lo, 0.0).astype(jnp.bfloat16)
                rhs[lanes : lanes + clusters, cols] = hi
                rhs[lanes + clusters :, cols] = lo
                at += tok

    lane = lax.broadcasted_iota(jnp.int32, (tok, lanes), 1)
    low = lane < HD
    q2 = q_ref[...]
    g2 = g_ref[...]
    zero = jnp.zeros_like(q2)
    head = lax.broadcasted_iota(jnp.int32, (tok, H), 1)
    own = lax.broadcasted_iota(jnp.int32, (tok, clusters), 1)
    lhs = []
    for odd in range(2):
        mine = jnp.sum(jnp.where(head == 2 * pair + odd, cl_ref[...], 0), axis=1, keepdims=True)
        hot = jnp.where(own == mine, 1.0, 0.0).astype(jnp.bfloat16)
        part = jnp.where(low, q2, zero) if odd == 0 else jnp.where(low, zero, q2)
        lhs.append(jnp.concatenate([part, hot, hot], axis=1))
    lhs = jnp.concatenate(lhs, axis=0)
    grads = jnp.concatenate([jnp.where(low, g2, zero), jnp.where(low, zero, g2)], axis=0)
    rows = 2 * tok

    top = jnp.full((rows, lanes), -3e38, jnp.float32)
    for t in range(tiles):
        cols = slice(t * TILE, (t + 1) * TILE)
        s = jnp.dot(lhs, rhs[:, cols], preferred_element_type=jnp.float32)
        sc[:, cols] = s
        for b in range(TILE // lanes):
            top = jnp.maximum(top, s[:, b * lanes : (b + 1) * lanes])
    top = jnp.max(top, axis=1, keepdims=True)

    denom = jnp.zeros((rows, lanes), jnp.float32)
    dots = jnp.zeros((rows, lanes), jnp.float32)
    for t in range(tiles):
        cols = slice(t * TILE, (t + 1) * TILE)
        w = jnp.exp2((sc[:, cols] - top) * (SCALE * LOG2E))
        sc[:, cols] = w
        p = jnp.dot(grads, val[:, cols], preferred_element_type=jnp.float32)
        pg[:, cols] = p
        wp = w * p
        for b in range(TILE // lanes):
            denom += w[:, b * lanes : (b + 1) * lanes]
            dots += wp[:, b * lanes : (b + 1) * lanes]
    denom = jnp.sum(denom, axis=1, keepdims=True)
    inv = SCALE / denom
    dot = jnp.sum(dots, axis=1, keepdims=True) / denom

    acc = jnp.zeros((rows, lanes), jnp.float32)
    for t in range(tiles):
        cols = slice(t * TILE, (t + 1) * TILE)
        ds = ((sc[:, cols] * inv) * (pg[:, cols] - dot)).astype(jnp.bfloat16)
        acc += jnp.dot(ds, key[cols, :], preferred_element_type=jnp.float32)
    out_ref[...] = jnp.where(low, acc[:tok], acc[tok:]).astype(jnp.bfloat16)


def attend(queries, out_grad, cluster_of, gathered, clusters):
    tok, width = queries.shape
    total = sum(g.shape[0] for g in gathered) * tok
    lanes = 2 * HD
    specs = [
        pl.BlockSpec((tok, lanes), lambda i: (0, i)),
        pl.BlockSpec((tok, lanes), lambda i: (0, i)),
        pl.BlockSpec((tok, H), lambda i: (0, 0)),
    ] + [pl.BlockSpec(g.shape, lambda i: (0, 0, 0)) for g in gathered]
    return pl.pallas_call(
        attend_kernel,
        grid=(width // lanes,),
        in_specs=specs,
        out_specs=pl.BlockSpec((tok, lanes), lambda i: (0, i)),
        out_shape=jax.ShapeDtypeStruct((tok, width), jnp.bfloat16),
        scratch_shapes=[
            pltpu.VMEM((lanes + 2 * clusters, total), jnp.bfloat16),
            pltpu.VMEM((lanes, total), jnp.bfloat16),
            pltpu.VMEM((total, lanes), jnp.bfloat16),
            pltpu.VMEM((2 * tok, total), jnp.float32),
            pltpu.VMEM((2 * tok, total), jnp.float32),
        ],
        compiler_params=pltpu.CompilerParams(vmem_limit_bytes=40 * 1024 * 1024),
    )(queries, out_grad, cluster_of, *gathered)


def xor_permute(x, axis, mask):
    n = lax.axis_size(axis)
    return lax.ppermute(x, axis, [(i, i ^ mask) for i in range(n)])


def dense(tokens_in, queries, key_value, out_grad, cluster_of, slot_of):
    n = lax.axis_size("seq")
    tok, width = queries.shape
    me = lax.axis_index("pair")
    low = 1
    while low * low < n:
        low *= 2
    high = n // low
    own = jnp.concatenate([key_value.T, cluster_of.T.astype(jnp.bfloat16)], axis=0)[None]
    column = jnp.concatenate([own] + [xor_permute(own, "seq", low * k) for k in range(1, high)])
    parts = [column] + [xor_permute(column, "seq", k) for k in range(1, low)]
    parts = parts + [xor_permute(p, "pair", 1) for p in parts]

    depth = tokens_in.shape[1]
    x4 = tokens_in.reshape(tok, n, 2, depth // (2 * n))
    x_mine = lax.dynamic_index_in_dim(x4, me, 2, keepdims=False).reshape(tok, depth // 2)
    x_other = lax.dynamic_index_in_dim(x4, 1 - me, 2, keepdims=False).reshape(tok, depth // 2)
    x_got = xor_permute(x_other, "pair", 1)

    mine = attend(queries, out_grad, cluster_of, parts, n * CL_DEV)
    other = xor_permute(mine, "pair", 1)
    contract = (((0,), (0,)), ((), ()))
    block = lax.dot_general(
        x_mine, mine, contract, preferred_element_type=jnp.float32
    ) + lax.dot_general(x_got, other, contract, preferred_element_type=jnp.float32)
    block = block.astype(jnp.bfloat16).reshape(n, depth // (2 * n), width)
    got = lax.all_to_all(block, "seq", 0, 0, tiled=True)
    return jnp.sum(got.astype(jnp.float32), axis=0)


def cluster_grad(query_part, key_part, live_keys):
    query_rows = query_part[:, :HD]
    grad_rows = query_part[:, HD:]
    key_rows = key_part[:, :HD]
    value_rows = key_part[:, HD:]
    scores = jnp.dot(query_rows, key_rows.T, preferred_element_type=jnp.float32) * SCALE
    scores = jnp.where(live_keys[None, :] > 0, scores, jnp.float32(-1e30))
    row_max = jnp.max(scores, axis=1, keepdims=True)
    weights = jnp.exp(scores - row_max)
    probs = weights / jnp.sum(weights, axis=1, keepdims=True)
    prob_grad = jnp.dot(grad_rows, value_rows.T, preferred_element_type=jnp.float32)
    row_dot = jnp.sum(probs * prob_grad, axis=1, keepdims=True)
    score_grad = (probs * (prob_grad - row_dot) * SCALE).astype(jnp.bfloat16)
    return jnp.dot(score_grad, key_rows, preferred_element_type=jnp.float32).astype(jnp.bfloat16)


def routed(tokens_in, queries, key_value, out_grad, cluster_of, slot_of):
    groups = lax.axis_size("seq")
    tok_count = queries.shape[0]
    row_count = tok_count * H
    bound_rows = 2 * row_count // groups
    slot_count = CL_DEV * HALF
    owners = (cluster_of // CL_DEV).reshape(row_count)
    local_slot = (cluster_of % CL_DEV * HALF + slot_of % HALF).reshape(row_count)
    picked = (owners[:, None] == jnp.arange(groups, dtype=jnp.int32)[None, :]).astype(jnp.int32)
    ranked = jnp.sum(jnp.cumsum(picked, axis=0) * picked, axis=1) - 1
    cell_index = owners * bound_rows + ranked
    paired_rows = jnp.concatenate(
        [queries.reshape(row_count, HD), out_grad.reshape(row_count, HD)], axis=1
    )
    packed = jnp.concatenate([paired_rows, jnp.repeat(key_value, H, axis=0)], axis=1)
    outgoing = jnp.zeros((groups * bound_rows, 4 * HD), jnp.bfloat16).at[cell_index].set(packed)
    labels = jnp.full((groups * bound_rows,), -1, jnp.int32).at[cell_index].set(local_slot)
    incoming = lax.all_to_all(
        outgoing.reshape(groups, bound_rows, 4 * HD), "seq", 0, 0, tiled=True
    )
    labels_in = lax.all_to_all(labels.reshape(groups, bound_rows), "seq", 0, 0, tiled=True)
    target = labels_in.reshape(groups * bound_rows)
    target_safe = jnp.where(target >= 0, target, slot_count)
    arranged = (
        jnp.zeros((slot_count, 4 * HD), jnp.bfloat16)
        .at[target_safe]
        .set(incoming.reshape(groups * bound_rows, 4 * HD), mode="drop")
    )
    live_slot = (
        jnp.zeros((slot_count,), jnp.bfloat16)
        .at[target_safe]
        .set(jnp.ones((groups * bound_rows,), jnp.bfloat16), mode="drop")
    )
    arranged = arranged.reshape(CL_DEV, HALF, 4 * HD)
    keys_all = lax.all_gather(arranged[:, :, 2 * HD :], "pair", axis=1, tiled=True)
    live_all = lax.all_gather(live_slot.reshape(CL_DEV, HALF), "pair", axis=1, tiled=True)
    cluster_grads = lax.map(
        lambda ops: cluster_grad(*ops), (arranged[:, :, : 2 * HD], keys_all, live_all)
    )
    slot_grads = cluster_grads.reshape(slot_count, HD)
    going_back = jnp.where(
        target[:, None] >= 0,
        slot_grads[jnp.minimum(target_safe, slot_count - 1)],
        jnp.zeros((), jnp.bfloat16),
    )
    returned = lax.all_to_all(
        going_back.reshape(groups, bound_rows // 2, 2 * HD), "seq", 0, 0, tiled=True
    )
    query_grad = returned.reshape(groups * bound_rows, HD)[cell_index].reshape(tok_count, H * HD)
    partial_rows = lax.psum_scatter(
        lax.dot_general(
            tokens_in, query_grad, (((0,), (0,)), ((), ())), preferred_element_type=jnp.float32
        ),
        "seq",
        scatter_dimension=0,
        tiled=True,
    )
    return lax.psum_scatter(partial_rows, "pair", scatter_dimension=0, tiled=True)


def solution(mesh):
    n = mesh.shape["seq"]
    small = n * CL_DEV <= 128 and n & (n - 1) == 0
    spec = P(("seq", "pair"), None)
    return jax.shard_map(
        dense if small else routed,
        mesh=mesh,
        in_specs=(spec,) * 6,
        out_specs=spec,
        check_vma=False,
    )
```

time: 344 us -> 91.1 us (0.26)
  waiting for transfers between devices: 161 us -> 10.5 us
  local copies, waits for them, and re-layouts: 96.2 us -> 3.75 us
  Pallas kernels: 0 us -> 32.6 us
  blocking collectives: 1.82 us -> 30.9 us
  other arithmetic: 23 us -> 1.61 us
  matrix products: 22.1 us -> 0.84 us
  starting transfers between devices: 25.2 us -> 10.5 us
  between operations: 13.4 us -> 0.08 us
    unnamed x4 -> x0, waiting for transfers between devices: 93.8 us -> none
    all_to_all x3 -> x0, waiting for transfers between devices: 57.9 us -> none  [the longest x1 42.6 us: on_device(): lax.all_to_all(outgoing.reshape(groups, bound_rows, 4 * HD), 'seq', split...]
    scatter x3 -> x0, local copies, waits for them, and re-layouts: 56.2 us -> none  [the longest x1 28.6 us: on_device(): live_slot = jnp.zeros((slot_count,), jnp.bfloat16).at[target_safe].set(jn...]
    pallas_call x0 -> x1, Pallas kernels: none -> 32.6 us  [attend(): pl.pallas_call(attend_kernel, grid=(width // lanes,), in_specs=specs, out...]
    all_to_all x0 -> x1, blocking collectives: none -> 30.9 us  [dense(): got = lax.all_to_all(block, 'seq', 0, 0, tiled=True)]
    all_to_all x3 -> x0, starting transfers between devices: 25 us -> none  [the longest x1 9.79 us: on_device(): lax.all_to_all(going_back.reshape(groups, bound_rows // 2, 2 * HD), 'seq'...]
    dot_general x25 -> x2, matrix products: 22.1 us -> 0.84 us  [the longest x1 0.42 us: dense(): lax.dot_general(x_mine, mine, contract, preferred_element_type=jnp.float32)]
    gather x4 -> x0, local copies, waits for them, and re-layouts: 19.1 us -> none  [the longest x3 12.9 us: on_device(): slot_grads[jnp.minimum(target_safe, slot_count - 1)]]
  transfers between devices with their start and end apart: 6 -> 12, of which waited for: 4 -> 6; matrix products, arithmetic and copies ran while one was open for 12% -> 1% of each run, Pallas kernels for 0% -> 0%
where the time goes in v1:
time: 91.1 us; the launch traced here: 90.8 us
  Pallas kernels  32.6 us (36%)
  blocking collectives  30.9 us (34%)
  starting transfers between devices  10.5 us (12%)
  waiting for transfers between devices  10.5 us (12%)
  local copies, waits for them, and re-layouts  3.75 us (4%)
  other arithmetic  1.61 us (2%)
    pallas_call x1, Pallas kernels, attend(): pl.pallas_call(attend_kernel, grid=(width // lanes,), in_specs=specs, out...  32.6 us
    all_to_all x1, blocking collectives, dense(): got = lax.all_to_all(block, 'seq', 0, 0, tiled=True)  30.9 us
    ppermute x12, waiting for transfers between devices, xor_permute(): return lax.ppermute(x, axis, [(i, i ^ mask) for i in range(n)])  10.5 us
    ppermute x12, starting transfers between devices, xor_permute(): return lax.ppermute(x, axis, [(i, i ^ mask) for i in range(n)])  10.5 us
    unnamed x9, local copies, waits for them, and re-layouts  3.73 us
  transfers between devices with their start and end apart: 12, of which 6 were waited for; matrix products, arithmetic and copies ran while one was open for 1% of the time, Pallas kernels for 0%

profile of v1, /device:TPU:0, one launch (start us, length us, event | category | flops | bytes accessed | tf_op | source)
XLA Modules:
  0.0 90.8 jit_solution(7828346389373524242)
XLA Ops:
  0.0 0.0 copy-start.2
  0.0 0.7 convert_bitcast_fusion
  0.7 0.9 copy.9
  1.6 5.1 %collective-permute-start.2 = (bf16[1,144,128]{2,1,0:T(8,128)(2,1)S(1)}, bf16[1,144,128]{2,1,0:T(8,128)(2,1)S(1)}, u32[]{:S(2)}, u32[]{:S(2)}) collective-permute-start(bf16[1,144,128]{2,1,0:T(8,128)(2,1)S(1)} %maximum_bitcast_fusion), channel_id=1, source_target_pairs={{0,24},{2,26},{4,28},{6,30},{8,16},{10,18},{12,20},{14,22},{16,8},... | collective-permute-start | bytes 110600 | tf_op jit(solution)/shard_map/ppermute | solution.py:134
  6.8 0.0 collective-permute-start.1
  6.8 0.6 collective-permute-start
  7.4 1.3 %collective-permute-done.2 = bf16[1,144,128]{2,1,0:T(8,128)(2,1)S(1)} collective-permute-done((bf16[1,144,128]{2,1,0:T(8,128)(2,1)S(1)}, bf16[1,144,128]{2,1,0:T(8,128)(2,1)S(1)}, u32[]{:S(2)}, u32[]{:S(2)}) %collective-permute-start.2) | collective-permute-done | bytes 36896 | tf_op jit(solution)/shard_map/ppermute | solution.py:134
  8.7 2.9 %collective-permute-done.1 = bf16[1,144,128]{2,1,0:T(8,128)(2,1)S(1)} collective-permute-done((bf16[1,144,128]{2,1,0:T(8,128)(2,1)S(1)}, bf16[1,144,128]{2,1,0:T(8,128)(2,1)S(1)}, u32[]{:S(2)}, u32[]{:S(2)}) %collective-permute-start.1) | collective-permute-done | bytes 36896 | tf_op jit(solution)/shard_map/ppermute | solution.py:134
  11.6 0.0 collective-permute-done
  11.7 2.5 %collective-permute-start.5 = (bf16[4,144,128]{2,1,0:T(8,128)(2,1)S(1)}, bf16[4,144,128]{2,1,0:T(8,128)(2,1)S(1)}, u32[]{:S(2)}, u32[]{:S(2)}) collective-permute-start(bf16[4,144,128]{2,1,0:T(8,128)(2,1)S(1)} %pad_maximum_fusion.refs_0_), channel_id=1, source_target_pairs={{0,6},{2,4},{4,2},{6,0},{8,14},{10,12},{12,10},{14,8},{16,22},{18,... | collective-permute-start | bytes 442376 | tf_op jit(solution)/shard_map/ppermute | solution.py:134
  14.2 0.5 collective-permute-start.4
  14.7 0.5 collective-permute-start.3
  15.2 0.0 collective-permute-start.6
  15.2 4.1 %collective-permute-done.5.refs_3_ = bf16[4,144,128]{2,1,0:T(8,128)(2,1)S(1)} collective-permute-done((bf16[4,144,128]{2,1,0:T(8,128)(2,1)S(1)}, bf16[4,144,128]{2,1,0:T(8,128)(2,1)S(1)}, u32[]{:S(2)}, u32[]{:S(2)}) %collective-permute-start.5) | collective-permute-done | bytes 147488 | tf_op jit(solution)/shard_map/ppermute | solution.py:134
  19.3 0.0 collective-permute-start.9
  19.3 0.8 collective-permute-done.4.refs_2_
  20.1 0.0 collective-permute-start.8
  20.1 0.0 collective-permute-done.3.refs_1_
  20.1 0.5 collective-permute-start.7
  20.6 0.8 copy.10.cl_ref
  21.4 0.0 collective-permute-done.6.refs_4_
  21.4 0.0 collective-permute-done.9.refs_7_
  21.4 0.0 collective-permute-done.8.refs_6_
  21.5 0.2 collective-permute-done.7.refs_5_
  21.7 0.0 copy-start
  21.7 0.9 %copy-done = bf16[128,1024]{1,0:T(8,128)(2,1)S(1)} copy-done((bf16[128,1024]{1,0:T(8,128)(2,1)S(1)}, bf16[128,1024]{1,0:T(8,128)(2,1)}, u32[]{:S(2)}) %copy-start) | copy-done | bytes 262168
  22.7 0.0 copy-start.1
  22.7 0.9 %copy-done.1 = bf16[128,1024]{1,0:T(8,128)(2,1)S(1)} copy-done((bf16[128,1024]{1,0:T(8,128)(2,1)S(1)}, bf16[128,1024]{1,0:T(8,128)(2,1)}, u32[]{:S(2)}) %copy-start.1) | copy-done | bytes 262168
  23.6 32.6 %shard_map.55 = bf16[128,1024]{1,0:T(8,128)(2,1)S(1)} custom-call(bf16[128,1024]{1,0:T(8,128)(2,1)S(1)} %copy-done, bf16[128,1024]{1,0:T(8,128)(2,1)S(1)} %copy-done.1, s32[128,16]{1,0:T(8,128)S(1)} %copy.10.cl_ref, bf16[4,144,128]{2,1,0:T(8,128)(2,1)S(1)} %pad_maximum_fusion.refs_0_, bf16[4,144,128]{2,1,0:T(8,128)(2,1)S(1)} %collective-permute-done.3.refs_1_, ...), custom_call_target="tpu_custom_call" | custom-call | tf_op jit(solution)/shard_map/pallas_call | solution.py:115
  56.2 0.4 collective-permute-start.11
  56.5 0.0 copy-done.2
  56.6 0.2 copy.8
  56.8 0.3 collective-permute-start.10
  57.0 1.1 %collective-permute-done.10 = bf16[128,512]{0,1:T(8,128)(2,1)S(1)} collective-permute-done((bf16[128,512]{0,1:T(8,128)(2,1)S(1)}, bf16[128,512]{0,1:T(8,128)(2,1)S(1)}, u32[]{:S(2)}, u32[]{:S(2)}) %collective-permute-start.10) | collective-permute-done | bytes 131104 | tf_op jit(solution)/shard_map/ppermute | solution.py:134
  58.2 0.0 collective-permute-done.11
  58.2 0.4 fusion
  58.6 0.4 add_convert_fusion
  59.0 30.9 %all_to_all.5 = bf16[16,32,1024]{2,1,0:T(8,128)(2,1)S(1)} all-to-all(bf16[16,32,1024]{2,1,0:T(8,128)(2,1)S(1)} %bitcast.13), channel_id=1, replica_groups=mesh['seq'=16,'pair'=2] {'seq'}, dimensions={0} | all-to-all | bytes 2097152 | tf_op jit(solution)/shard_map/all_to_all | solution.py:163
  89.9 0.8 convert_reduce_fusion
  (3 shorter events, 0.1 us)
Async XLA Ops:
  0.0 56.6 %copy-start.2 = (bf16[128,1024]{1,0:T(8,128)(2,1)S(1)}, bf16[128,1024]{1,0:T(8,128)(2,1)}, u32[]{:S(2)}) copy-start(bf16[128,1024]{1,0:T(8,128)(2,1)} %param.6) | copy-start | bytes 786436
  1.6 7.1 %collective-permute-start.2 = (bf16[1,144,128]{2,1,0:T(8,128)(2,1)S(1)}, bf16[1,144,128]{2,1,0:T(8,128)(2,1)S(1)}, u32[]{:S(2)}, u32[]{:S(2)}) collective-permute-start(bf16[1,144,128]{2,1,0:T(8,128)(2,1)S(1)} %maximum_bitcast_fusion), channel_id=1, source_target_pairs={{0,24},{2,26},{4,28},{6,30},{8,16},{10,18},{12,20},{14,22},{16,8},... | collective-permute-start | bytes 110600 | tf_op jit(solution)/shard_map/ppermute | solution.py:134
  6.8 4.9 %collective-permute-start.1 = (bf16[1,144,128]{2,1,0:T(8,128)(2,1)S(1)}, bf16[1,144,128]{2,1,0:T(8,128)(2,1)S(1)}, u32[]{:S(2)}, u32[]{:S(2)}) collective-permute-start(bf16[1,144,128]{2,1,0:T(8,128)(2,1)S(1)} %maximum_bitcast_fusion), channel_id=1, source_target_pairs={{0,16},{2,18},{4,20},{6,22},{8,24},{10,26},{12,28},{14,30},{16,0},... | collective-permute-start | bytes 110600 | tf_op jit(solution)/shard_map/ppermute | solution.py:134
  6.8 4.9 %collective-permute-start = (bf16[1,144,128]{2,1,0:T(8,128)(2,1)S(1)}, bf16[1,144,128]{2,1,0:T(8,128)(2,1)S(1)}, u32[]{:S(2)}, u32[]{:S(2)}) collective-permute-start(bf16[1,144,128]{2,1,0:T(8,128)(2,1)S(1)} %maximum_bitcast_fusion), channel_id=1, source_target_pairs={{0,8},{2,10},{4,12},{6,14},{8,0},{10,2},{12,4},{14,6},{16,24},{18,... | collective-permute-start | bytes 110600 | tf_op jit(solution)/shard_map/ppermute | solution.py:134
  11.7 7.7 %collective-permute-start.5 = (bf16[4,144,128]{2,1,0:T(8,128)(2,1)S(1)}, bf16[4,144,128]{2,1,0:T(8,128)(2,1)S(1)}, u32[]{:S(2)}, u32[]{:S(2)}) collective-permute-start(bf16[4,144,128]{2,1,0:T(8,128)(2,1)S(1)} %pad_maximum_fusion.refs_0_), channel_id=1, source_target_pairs={{0,6},{2,4},{4,2},{6,0},{8,14},{10,12},{12,10},{14,8},{16,22},{18,... | collective-permute-start | bytes 442376 | tf_op jit(solution)/shard_map/ppermute | solution.py:134
  14.2 6.0 %collective-permute-start.4 = (bf16[4,144,128]{2,1,0:T(8,128)(2,1)S(1)}, bf16[4,144,128]{2,1,0:T(8,128)(2,1)S(1)}, u32[]{:S(2)}, u32[]{:S(2)}) collective-permute-start(bf16[4,144,128]{2,1,0:T(8,128)(2,1)S(1)} %pad_maximum_fusion.refs_0_), channel_id=1, source_target_pairs={{0,4},{2,6},{4,0},{6,2},{8,12},{10,14},{12,8},{14,10},{16,20},{18,... | collective-permute-start | bytes 442376 | tf_op jit(solution)/shard_map/ppermute | solution.py:134
  14.7 5.4 %collective-permute-start.3 = (bf16[4,144,128]{2,1,0:T(8,128)(2,1)S(1)}, bf16[4,144,128]{2,1,0:T(8,128)(2,1)S(1)}, u32[]{:S(2)}, u32[]{:S(2)}) collective-permute-start(bf16[4,144,128]{2,1,0:T(8,128)(2,1)S(1)} %pad_maximum_fusion.refs_0_), channel_id=1, source_target_pairs={{0,2},{2,0},{4,6},{6,4},{8,10},{10,8},{12,14},{14,12},{16,18},{18,... | collective-permute-start | bytes 442376 | tf_op jit(solution)/shard_map/ppermute | solution.py:134
  15.2 6.2 %collective-permute-start.6 = (bf16[4,144,128]{2,1,0:T(8,128)(2,1)S(1)}, bf16[4,144,128]{2,1,0:T(8,128)(2,1)S(1)}, u32[]{:S(2)}, u32[]{:S(2)}) collective-permute-start(bf16[4,144,128]{2,1,0:T(8,128)(2,1)S(1)} %pad_maximum_fusion.refs_0_), channel_id=1, source_target_pairs={{0,1},{1,0},{2,3},{3,2},{4,5},{5,4},{6,7},{7,6},{8,9},{9,8},{10,11... | collective-permute-start | bytes 442376 | tf_op jit(solution)/shard_map/ppermute | solution.py:134
  19.3 2.1 %collective-permute-start.9 = (bf16[4,144,128]{2,1,0:T(8,128)(2,1)S(1)}, bf16[4,144,128]{2,1,0:T(8,128)(2,1)S(1)}, u32[]{:S(2)}, u32[]{:S(2)}) collective-permute-start(bf16[4,144,128]{2,1,0:T(8,128)(2,1)S(1)} %collective-permute-done.5.refs_3_), channel_id=1, source_target_pairs={{0,1},{1,0},{2,3},{3,2},{4,5},{5,4},{6,7},{7,6},{8,9},{9,8},{10,11... | collective-permute-start | bytes 442376 | tf_op jit(solution)/shard_map/ppermute | solution.py:134
  20.1 1.4 %collective-permute-start.8 = (bf16[4,144,128]{2,1,0:T(8,128)(2,1)S(1)}, bf16[4,144,128]{2,1,0:T(8,128)(2,1)S(1)}, u32[]{:S(2)}, u32[]{:S(2)}) collective-permute-start(bf16[4,144,128]{2,1,0:T(8,128)(2,1)S(1)} %collective-permute-done.4.refs_2_), channel_id=1, source_target_pairs={{0,1},{1,0},{2,3},{3,2},{4,5},{5,4},{6,7},{7,6},{8,9},{9,8},{10,11... | collective-permute-start | bytes 442376 | tf_op jit(solution)/shard_map/ppermute | solution.py:134
  20.1 1.6 %collective-permute-start.7 = (bf16[4,144,128]{2,1,0:T(8,128)(2,1)S(1)}, bf16[4,144,128]{2,1,0:T(8,128)(2,1)S(1)}, u32[]{:S(2)}, u32[]{:S(2)}) collective-permute-start(bf16[4,144,128]{2,1,0:T(8,128)(2,1)S(1)} %collective-permute-done.3.refs_1_), channel_id=1, source_target_pairs={{0,1},{1,0},{2,3},{3,2},{4,5},{5,4},{6,7},{7,6},{8,9},{9,8},{10,11... | collective-permute-start | bytes 442376 | tf_op jit(solution)/shard_map/ppermute | solution.py:134
  21.7 1.0 %copy-start = (bf16[128,1024]{1,0:T(8,128)(2,1)S(1)}, bf16[128,1024]{1,0:T(8,128)(2,1)}, u32[]{:S(2)}) copy-start(bf16[128,1024]{1,0:T(8,128)(2,1)} %q_ref.1) | copy-start | bytes 786436
  22.7 0.9 %copy-start.1 = (bf16[128,1024]{1,0:T(8,128)(2,1)S(1)}, bf16[128,1024]{1,0:T(8,128)(2,1)}, u32[]{:S(2)}) copy-start(bf16[128,1024]{1,0:T(8,128)(2,1)} %g_ref.1) | copy-start | bytes 786436
  56.2 2.0 %collective-permute-start.11 = (bf16[128,1024]{1,0:T(8,128)(2,1)S(1)}, bf16[128,1024]{1,0:T(8,128)(2,1)S(1)}, u32[]{:S(2)}, u32[]{:S(2)}) collective-permute-start(bf16[128,1024]{1,0:T(8,128)(2,1)S(1)} %shard_map.55), channel_id=1, source_target_pairs={{0,1},{1,0},{2,3},{3,2},{4,5},{5,4},{6,7},{7,6},{8,9},{9,8},{10,11... | collective-permute-start | bytes 786440 | tf_op jit(solution)/shard_map/ppermute | solution.py:134
  56.8 1.4 %collective-permute-start.10 = (bf16[128,512]{0,1:T(8,128)(2,1)S(1)}, bf16[128,512]{0,1:T(8,128)(2,1)S(1)}, u32[]{:S(2)}, u32[]{:S(2)}) collective-permute-start(bf16[128,512]{0,1:T(8,128)(2,1)S(1)} %bitcast.17), channel_id=1, source_target_pairs={{0,1},{1,0},{2,3},{3,2},{4,5},{5,4},{6,7},{7,6},{8,9},{9,8},{10,11... | collective-permute-start | bytes 393224 | tf_op jit(solution)/shard_map/ppermute | solution.py:134

commit v2 on v0

v2 whole, which is shorter than its diff:
```python
import jax
import jax.numpy as jnp
from jax import lax
from jax.experimental import pallas as pl
from jax.experimental.pallas import tpu as pltpu
from jax.sharding import PartitionSpec as P

H = 16
HD = 64
HALF = 512
CL_DEV = 8
SCALE = HD ** (-0.5)
LOG2E = 1.4426950408889634
TILE = 512


def prepare_rows_kernel(q_ref, g_ref, cl_ref, lhs, grd):
    tok, width = q_ref.shape
    lanes = 2 * HD
    lane = lax.broadcasted_iota(jnp.int32, (tok, lanes), 1)
    low = lane < HD
    head = lax.broadcasted_iota(jnp.int32, (tok, H), 1)
    for h in range(width // HD):
        at = slice(h * tok, (h + 1) * tok)
        two = slice((h // 2) * lanes, (h // 2 + 1) * lanes)
        q2 = q_ref[:, two].astype(jnp.float32) * SCALE
        g2 = g_ref[:, two].astype(jnp.float32)
        if h % 2:
            q2 = pltpu.roll(q2, HD, 1)
            g2 = pltpu.roll(g2, HD, 1)
        mine = jnp.sum(jnp.where(head == h, cl_ref[...], 0), axis=1, keepdims=True)
        same = jnp.where(mine >= HD, mine - HD, mine)
        first = jnp.where(lane - HD == mine, 1.0, 0.0)
        second = jnp.where(lane == jnp.where(low, mine - HD, same + HD), 1.0, 0.0)
        lhs[0, at, :] = jnp.where(low, q2, first).astype(jnp.bfloat16)
        lhs[1, at, :] = second.astype(jnp.bfloat16)
        grd[at, :] = g2[:, :HD].astype(jnp.bfloat16)


def prepare_rows(queries, out_grad, cluster_of):
    tok, width = queries.shape
    rows = width // HD * tok
    return pl.pallas_call(
        prepare_rows_kernel,
        out_shape=(
            jax.ShapeDtypeStruct((2, rows, 2 * HD), jnp.bfloat16),
            jax.ShapeDtypeStruct((rows, HD), jnp.bfloat16),
        ),
        cost_estimate=pl.CostEstimate(flops=10**7, bytes_accessed=2 * 10**6, transcendentals=0),
    )(queries, out_grad, cluster_of)


def prepare_keys_kernel(*refs):
    kv_refs = refs[:-3]
    rhs, val, key = refs[-3:]
    tok = rhs.shape[2]
    quarter = HD // 2
    ids = lax.broadcasted_iota(jnp.int32, (quarter, tok), 0)
    at = 0
    for kv_ref in kv_refs:
        for j in range(kv_ref.shape[0]):
            kv = kv_ref[j, 0:tok, :]
            turned = kv.astype(jnp.float32).T.astype(jnp.bfloat16)
            rhs[at, 0:HD, :] = turned[:HD]
            val[at, :, :] = turned[HD:]
            key[at * tok : (at + 1) * tok, :] = kv
            cl = kv_ref[j, tok : tok + H, :].astype(jnp.float32).astype(jnp.int32)
            group = jnp.bitwise_and(cl, quarter - 1)
            one = jnp.left_shift(1, 8 * jnp.right_shift(cl, 5))
            packed = jnp.zeros((quarter, tok), jnp.int32)
            for h in range(H):
                packed += jnp.where(group[h : h + 1, :] == ids, one[h : h + 1, :], 0)
            res = []
            for part in range(4):
                count = jnp.bitwise_and(jnp.right_shift(packed, 8 * part), 255)
                live = count > 0
                log = jnp.log(count.astype(jnp.float32))
                hi = jnp.where(live, log, -1e30).astype(jnp.bfloat16)
                rhs[at, HD + part * quarter : HD + (part + 1) * quarter, :] = hi
                res.append(jnp.where(live, log - hi.astype(jnp.float32), 0.0))
            for part in range(2):
                a, b = res[part], res[part + 2]
                both = jnp.where(a == 0.0, b, jnp.where(b == 0.0, a, 0.5 * (a + b)))
                start = 3 * HD + part * quarter
                rhs[at, start : start + quarter, :] = both.astype(jnp.bfloat16)
            at += 1


def prepare_keys(gathered):
    tok = gathered[0].shape[2]
    blocks = sum(g.shape[0] for g in gathered)
    return pl.pallas_call(
        prepare_keys_kernel,
        out_shape=(
            jax.ShapeDtypeStruct((blocks, 4 * HD, tok), jnp.bfloat16),
            jax.ShapeDtypeStruct((blocks, HD, tok), jnp.bfloat16),
            jax.ShapeDtypeStruct((blocks * tok, 2 * HD), jnp.bfloat16),
        ),
        cost_estimate=pl.CostEstimate(
            flops=blocks * 10**6, bytes_accessed=blocks * 10**5, transcendentals=0
        ),
    )(*gathered)


def attend_kernel(lhs, grd, *refs):
    count = (len(refs) - 9) // 3
    groups = [refs[3 * i : 3 * i + 3] for i in range(count)]
    out_ref, sc0, sc1, pg0, pg1, ds0, ds1, acc, tot = refs[3 * count :]
    sc, pg, ds = (sc0, sc1), (pg0, pg1), (ds0, ds1)
    lanes = 2 * HD
    tok = out_ref.shape[0]
    rows = sc0.shape[0]
    per = TILE // lanes
    places = [(g, j) for g, group in enumerate(groups) for j in range(group[0].shape[0] // per)]
    tiles = len(places)
    total = tiles * TILE
    steps = out_ref.shape[1] // HD * tok // rows
    block = rows // tiles
    chunks = [slice(c * lanes, (c + 1) * lanes) for c in range(total // lanes)]

    def gated(x, gate):
        if gate is None:
            return x
        tie = jnp.tile((gate * 0.0).astype(x.dtype), (1, x.shape[1] // gate.shape[1]))
        pieces = []
        for r in range(0, x.shape[0], 2 * lanes):
            pieces += [x[r : r + 16] + tie, x[r + 16 : r + 2 * lanes]]
        return jnp.concatenate(pieces, axis=0)

    def score(step, slot, t, gate=None):
        g, j = places[t]
        at = pl.ds(pl.multiple_of(step * rows, rows), rows)
        span = range(j * per, (j + 1) * per)
        right = jnp.concatenate([groups[g][0][b] for b in span], axis=1)
        left = jnp.concatenate([lhs[0, at, :], lhs[1, at, :]], axis=1)
        cols = slice(t * TILE, (t + 1) * TILE)
        sc[slot][:, cols] = jnp.dot(left, gated(right, gate), preferred_element_type=jnp.float32)
        right = jnp.concatenate([groups[g][1][b] for b in span], axis=1)
        pg[slot][:, cols] = jnp.dot(
            grd[at, :], gated(right, gate), preferred_element_type=jnp.float32
        )

    def soften(slot, t):
        at = slice(t * block, (t + 1) * block)
        top = sc[slot][at, chunks[0]]
        for c in chunks[1:]:
            top = jnp.maximum(top, sc[slot][at, c])
        top = jnp.broadcast_to(jnp.max(top, axis=1, keepdims=True), (block, lanes))
        denom = jnp.zeros((block, lanes), jnp.float32)
        dots = jnp.zeros((block, lanes), jnp.float32)
        for c in chunks:
            w = jnp.exp(sc[slot][at, c] - top)
            sc[slot][at, c] = w
            denom += w
            dots += w * pg[slot][at, c]
        denom = jnp.sum(denom, axis=1, keepdims=True)
        inv = jnp.broadcast_to(SCALE / denom, (block, lanes))
        dot = jnp.broadcast_to(jnp.sum(dots, axis=1, keepdims=True) / denom, (block, lanes))
        for i, c in enumerate(chunks):
            d = (sc[slot][at, c] * inv) * (pg[slot][at, c] - dot)
            ds[slot][i, at, :] = d.astype(jnp.bfloat16)
        return d[0:16, :]

    def collect(slot, t, gate=None):
        g, j = places[t]
        left = jnp.concatenate([ds[slot][t * per + b] for b in range(per)], axis=1)
        right = gated(groups[g][2][j * TILE : (j + 1) * TILE, :], gate)
        add = jnp.dot(left, right, preferred_element_type=jnp.float32)
        acc[...] = add if t == 0 else acc[...] + add

    def finish(step):
        low = lax.broadcasted_iota(jnp.int32, (tok, lanes), 1) < HD
        for j in range(rows // (2 * tok)):
            even = acc[2 * j * tok : (2 * j + 1) * tok, :]
            odd = pltpu.roll(acc[(2 * j + 1) * tok : (2 * j + 2) * tok, :], HD, 1)
            where = pl.multiple_of((step * (rows // (2 * tok)) + j) * lanes, lanes)
            out_ref[:, pl.ds(where, lanes)] = jnp.where(low, even, odd).astype(jnp.bfloat16)

    def stage(step, slot, following):
        gate = None
        for t in range(tiles):
            score(following, 1 - slot, t, gate)
            collect(1 - slot, t, gate)
            gate = soften(slot, t)

        @pl.when(step > 0)
        def _():
            finish(step - 1)

    for t in range(tiles):
        score(0, 0, t)

    def body(i, _):
        stage(2 * i, 0, 2 * i + 1)
        stage(2 * i + 1, 1, jnp.minimum(2 * i + 2, steps - 1))
        return 0

    lax.fori_loop(0, steps // 2, body, 0)
    for t in range(tiles):
        collect(1, t)
    finish(steps - 1)


def attend(left, groups, tok):
    lhs, grd = left
    heads = grd.shape[0] // tok
    total = sum(g[2].shape[0] for g in groups)
    lanes = 2 * HD
    rows = 2 * tok
    operands = [lhs, grd] + [x for g in groups for x in g]
    work = grd.shape[0] * total
    return pl.pallas_call(
        attend_kernel,
        in_specs=[pl.BlockSpec(memory_space=pltpu.VMEM)] * len(operands),
        out_specs=pl.BlockSpec(memory_space=pltpu.VMEM),
        out_shape=jax.ShapeDtypeStruct((tok, heads * HD), jnp.bfloat16),
        scratch_shapes=[pltpu.VMEM((rows, total), jnp.float32)] * 4
        + [pltpu.VMEM((total // lanes, rows, lanes), jnp.bfloat16)] * 2
        + [pltpu.VMEM((rows, lanes), jnp.float32)] * 2,
        compiler_params=pltpu.CompilerParams(vmem_limit_bytes=40 * 1024 * 1024),
        cost_estimate=pl.CostEstimate(
            flops=work * 6 * HD, bytes_accessed=10**7, transcendentals=work
        ),
    )(*operands)


def bench(q, g, c, *parts):
    groups = [prepare_keys(parts[:1]), prepare_keys(parts[1:4]), prepare_keys(parts[4:])]
    return attend(prepare_rows(q, g, c), groups, q.shape[0])


def xor_permute(x, axis, mask):
    n = lax.axis_size(axis)
    return lax.ppermute(x, axis, [(i, i ^ mask) for i in range(n)])


def dense(tokens_in, queries, key_value, out_grad, cluster_of, slot_of):
    n = lax.axis_size("seq")
    tok, width = queries.shape
    me = lax.axis_index("pair")
    low = 1
    while low * low < n:
        low *= 2
    high = n // low
    own = jnp.concatenate([key_value, cluster_of.T.astype(jnp.bfloat16)], axis=0)[None]
    column = jnp.concatenate([own] + [xor_permute(own, "seq", low * k) for k in range(1, high)])
    near = [xor_permute(column, "seq", k) for k in range(1, low)]
    left = prepare_rows(queries, out_grad, cluster_of)
    groups = [
        prepare_keys([column]),
        prepare_keys(near),
        prepare_keys([xor_permute(p, "pair", 1) for p in [column] + near]),
    ]

    depth = tokens_in.shape[1]
    x4 = tokens_in.reshape(tok, n, 2, depth // (2 * n))
    x_mine = lax.dynamic_index_in_dim(x4, me, 2, keepdims=False).reshape(tok, depth // 2)
    x_other = lax.dynamic_index_in_dim(x4, 1 - me, 2, keepdims=False).reshape(tok, depth // 2)
    x_got = xor_permute(x_other, "pair", 1)

    mine = attend(left, groups, tok)
    other = xor_permute(mine, "pair", 1)
    contract = (((0,), (0,)), ((), ()))
    block = lax.dot_general(
        x_mine, mine, contract, preferred_element_type=jnp.float32
    ) + lax.dot_general(x_got, other, contract, preferred_element_type=jnp.float32)
    block = block.astype(jnp.bfloat16).reshape(n, depth // (2 * n), width)
    got = lax.all_to_all(block, "seq", 0, 0, tiled=True)
    return jnp.sum(got.astype(jnp.float32), axis=0)


def cluster_grad(query_part, key_part, live_keys):
    query_rows = query_part[:, :HD]
    grad_rows = query_part[:, HD:]
    key_rows = key_part[:, :HD]
    value_rows = key_part[:, HD:]
    scores = jnp.dot(query_rows, key_rows.T, preferred_element_type=jnp.float32) * SCALE
    scores = jnp.where(live_keys[None, :] > 0, scores, jnp.float32(-1e30))
    row_max = jnp.max(scores, axis=1, keepdims=True)
    weights = jnp.exp(scores - row_max)
    probs = weights / jnp.sum(weights, axis=1, keepdims=True)
    prob_grad = jnp.dot(grad_rows, value_rows.T, preferred_element_type=jnp.float32)
    row_dot = jnp.sum(probs * prob_grad, axis=1, keepdims=True)
    score_grad = (probs * (prob_grad - row_dot) * SCALE).astype(jnp.bfloat16)
    return jnp.dot(score_grad, key_rows, preferred_element_type=jnp.float32).astype(jnp.bfloat16)


def routed(tokens_in, queries, key_value, out_grad, cluster_of, slot_of):
    groups = lax.axis_size("seq")
    tok_count = queries.shape[0]
    row_count = tok_count * H
    bound_rows = 2 * row_count // groups
    slot_count = CL_DEV * HALF
    owners = (cluster_of // CL_DEV).reshape(row_count)
    local_slot = (cluster_of % CL_DEV * HALF + slot_of % HALF).reshape(row_count)
    picked = (owners[:, None] == jnp.arange(groups, dtype=jnp.int32)[None, :]).astype(jnp.int32)
    ranked = jnp.sum(jnp.cumsum(picked, axis=0) * picked, axis=1) - 1
    cell_index = owners * bound_rows + ranked
    paired_rows = jnp.concatenate(
        [queries.reshape(row_count, HD), out_grad.reshape(row_count, HD)], axis=1
    )
    packed = jnp.concatenate([paired_rows, jnp.repeat(key_value, H, axis=0)], axis=1)
    outgoing = jnp.zeros((groups * bound_rows, 4 * HD), jnp.bfloat16).at[cell_index].set(packed)
    labels = jnp.full((groups * bound_rows,), -1, jnp.int32).at[cell_index].set(local_slot)
    incoming = lax.all_to_all(
        outgoing.reshape(groups, bound_rows, 4 * HD), "seq", 0, 0, tiled=True
    )
    labels_in = lax.all_to_all(labels.reshape(groups, bound_rows), "seq", 0, 0, tiled=True)
    target = labels_in.reshape(groups * bound_rows)
    target_safe = jnp.where(target >= 0, target, slot_count)
    arranged = (
        jnp.zeros((slot_count, 4 * HD), jnp.bfloat16)
        .at[target_safe]
        .set(incoming.reshape(groups * bound_rows, 4 * HD), mode="drop")
    )
    live_slot = (
        jnp.zeros((slot_count,), jnp.bfloat16)
        .at[target_safe]
        .set(jnp.ones((groups * bound_rows,), jnp.bfloat16), mode="drop")
    )
    arranged = arranged.reshape(CL_DEV, HALF, 4 * HD)
    keys_all = lax.all_gather(arranged[:, :, 2 * HD :], "pair", axis=1, tiled=True)
    live_all = lax.all_gather(live_slot.reshape(CL_DEV, HALF), "pair", axis=1, tiled=True)
    cluster_grads = lax.map(
        lambda ops: cluster_grad(*ops), (arranged[:, :, : 2 * HD], keys_all, live_all)
    )
    slot_grads = cluster_grads.reshape(slot_count, HD)
    going_back = jnp.where(
        target[:, None] >= 0,
        slot_grads[jnp.minimum(target_safe, slot_count - 1)],
        jnp.zeros((), jnp.bfloat16),
    )
    returned = lax.all_to_all(
        going_back.reshape(groups, bound_rows // 2, 2 * HD), "seq", 0, 0, tiled=True
    )
    query_grad = returned.reshape(groups * bound_rows, HD)[cell_index].reshape(tok_count, H * HD)
    partial_rows = lax.psum_scatter(
        lax.dot_general(
            tokens_in, query_grad, (((0,), (0,)), ((), ())), preferred_element_type=jnp.float32
        ),
        "seq",
        scatter_dimension=0,
        tiled=True,
    )
    return lax.psum_scatter(partial_rows, "pair", scatter_dimension=0, tiled=True)


def solution(mesh):
    n = mesh.shape["seq"]
    small = n * CL_DEV == 2 * HD and n & (n - 1) == 0
    spec = P(("seq", "pair"), None)
    return jax.shard_map(
        dense if small else routed,
        mesh=mesh,
        in_specs=(spec,) * 6,
        out_specs=spec,
        check_vma=False,
    )
```

time: 344 us -> 108 us (0.31)
  waiting for transfers between devices: 161 us -> 12.4 us
  local copies, waits for them, and re-layouts: 96.2 us -> 14.3 us
  Pallas kernels: 0 us -> 37.2 us
  blocking collectives: 1.82 us -> 29.3 us
  matrix products: 22.1 us -> 0.84 us
  other arithmetic: 23 us -> 2.32 us
  starting transfers between devices: 25.2 us -> 10.3 us
  between operations: 13.4 us -> 0.12 us
    unnamed x4 -> x0, waiting for transfers between devices: 93.8 us -> none
    all_to_all x3 -> x0, waiting for transfers between devices: 57.9 us -> none  [the longest x1 42.6 us: on_device(): lax.all_to_all(outgoing.reshape(groups, bound_rows, 4 * HD), 'seq', split...]
    scatter x3 -> x0, local copies, waits for them, and re-layouts: 56.2 us -> none  [the longest x1 28.6 us: on_device(): live_slot = jnp.zeros((slot_count,), jnp.bfloat16).at[target_safe].set(jn...]
    pallas_call x0 -> x5, Pallas kernels: none -> 37.2 us  [the longest x1 26 us: attend(): pl.pallas_call(attend_kernel, in_specs=[pl.BlockSpec(memory_space=pltpu.V...]
    all_to_all x0 -> x1, blocking collectives: none -> 29.3 us  [dense(): got = lax.all_to_all(block, 'seq', 0, 0, tiled=True)]
    all_to_all x3 -> x0, starting transfers between devices: 25 us -> none  [the longest x1 9.79 us: on_device(): lax.all_to_all(going_back.reshape(groups, bound_rows // 2, 2 * HD), 'seq'...]
    dot_general x25 -> x2, matrix products: 22.1 us -> 0.84 us  [the longest x1 0.42 us: dense(): lax.dot_general(x_mine, mine, contract, preferred_element_type=jnp.float32)]
    gather x4 -> x0, local copies, waits for them, and re-layouts: 19.1 us -> none  [the longest x3 12.9 us: on_device(): slot_grads[jnp.minimum(target_safe, slot_count - 1)]]
  transfers between devices with their start and end apart: 6 -> 12, of which waited for: 4 -> 5; matrix products, arithmetic and copies ran while one was open for 12% -> 2% of each run, Pallas kernels for 0% -> 7%
where the time goes in v2:
time: 108 us; the launch traced here: 107 us
  Pallas kernels  37.2 us (34%)
  blocking collectives  29.3 us (27%)
  local copies, waits for them, and re-layouts  14.3 us (13%)
  waiting for transfers between devices  12.4 us (11%)
  starting transfers between devices  10.3 us (10%)
  other arithmetic  2.32 us (2%)
    all_to_all x1, blocking collectives, dense(): got = lax.all_to_all(block, 'seq', 0, 0, tiled=True)  29.3 us
    pallas_call x1, Pallas kernels, attend(): pl.pallas_call(attend_kernel, in_specs=[pl.BlockSpec(memory_space=pltpu.V...  26 us
    unnamed x42, local copies, waits for them, and re-layouts  14.3 us
    ppermute x12, waiting for transfers between devices, xor_permute(): return lax.ppermute(x, axis, [(i, i ^ mask) for i in range(n)])  12.4 us
    ppermute x12, starting transfers between devices, xor_permute(): return lax.ppermute(x, axis, [(i, i ^ mask) for i in range(n)])  10.3 us
    pallas_call x3, Pallas kernels, prepare_keys(): pl.pallas_call(prepare_keys_kernel, out_shape=(jax.ShapeDtypeStruct((bloc...  7.96 us
    pallas_call x1, Pallas kernels, prepare_rows(): pl.pallas_call(prepare_rows_kernel, out_shape=(jax.ShapeDtypeStruct((2, r...  3.2 us
  transfers between devices with their start and end apart: 12, of which 5 were waited for; matrix products, arithmetic and copies ran while one was open for 2% of the time, Pallas kernels for 7%

profile of v2, /device:TPU:0, one launch (start us, length us, event | category | flops | bytes accessed | tf_op | source)
XLA Modules:
  0.0 106.9 jit_solution(1352602500216808683)
XLA Ops:
  0.0 0.7 convert_bitcast_fusion
  0.7 0.8 maximum_bitcast_fusion
  1.5 3.1 %collective-permute-start = (bf16[1,144,128]{2,1,0:T(8,128)(2,1)S(1)}, bf16[1,144,128]{2,1,0:T(8,128)(2,1)S(1)}, u32[]{:S(2)}, u32[]{:S(2)}) collective-permute-start(bf16[1,144,128]{2,1,0:T(8,128)(2,1)S(1)} %maximum_bitcast_fusion), channel_id=1, source_target_pairs={{0,8},{2,10},{4,12},{6,14},{8,0},{10,2},{12,4},{14,6},{16,24},{18,... | collective-permute-start | bytes 110600 | tf_op jit(solution)/shard_map/ppermute | solution.py:234
  4.5 2.6 %collective-permute-start.1 = (bf16[1,144,128]{2,1,0:T(8,128)(2,1)S(1)}, bf16[1,144,128]{2,1,0:T(8,128)(2,1)S(1)}, u32[]{:S(2)}, u32[]{:S(2)}) collective-permute-start(bf16[1,144,128]{2,1,0:T(8,128)(2,1)S(1)} %maximum_bitcast_fusion), channel_id=1, source_target_pairs={{0,16},{2,18},{4,20},{6,22},{8,24},{10,26},{12,28},{14,30},{16,0},... | collective-permute-start | bytes 110600 | tf_op jit(solution)/shard_map/ppermute | solution.py:234
  7.1 0.0 collective-permute-start.2
  7.1 0.0 collective-permute-done
  7.1 2.9 %collective-permute-done.1 = bf16[1,144,128]{2,1,0:T(8,128)(2,1)S(1)} collective-permute-done((bf16[1,144,128]{2,1,0:T(8,128)(2,1)S(1)}, bf16[1,144,128]{2,1,0:T(8,128)(2,1)S(1)}, u32[]{:S(2)}, u32[]{:S(2)}) %collective-permute-start.1) | collective-permute-done | bytes 36896 | tf_op jit(solution)/shard_map/ppermute | solution.py:234
  10.0 2.8 %collective-permute-done.2 = bf16[1,144,128]{2,1,0:T(8,128)(2,1)S(1)} collective-permute-done((bf16[1,144,128]{2,1,0:T(8,128)(2,1)S(1)}, bf16[1,144,128]{2,1,0:T(8,128)(2,1)S(1)}, u32[]{:S(2)}, u32[]{:S(2)}) %collective-permute-start.2) | collective-permute-done | bytes 36896 | tf_op jit(solution)/shard_map/ppermute | solution.py:234
  12.9 0.0 copy-start.11
  12.9 1.6 %collective-permute-start.3 = (bf16[4,144,128]{2,1,0:T(8,128)(2,1)S(1)}, bf16[4,144,128]{2,1,0:T(8,128)(2,1)S(1)}, u32[]{:S(2)}, u32[]{:S(2)}) collective-permute-start(bf16[4,144,128]{2,1,0:T(8,128)(2,1)S(1)} %pad_maximum_fusion.refs_0_), channel_id=1, source_target_pairs={{0,2},{2,0},{4,6},{6,4},{8,10},{10,8},{12,14},{14,12},{16,18},{18,... | collective-permute-start | bytes 442376 | tf_op jit(solution)/shard_map/ppermute | solution.py:234
  14.5 1.5 %collective-permute-start.4 = (bf16[4,144,128]{2,1,0:T(8,128)(2,1)S(1)}, bf16[4,144,128]{2,1,0:T(8,128)(2,1)S(1)}, u32[]{:S(2)}, u32[]{:S(2)}) collective-permute-start(bf16[4,144,128]{2,1,0:T(8,128)(2,1)S(1)} %pad_maximum_fusion.refs_0_), channel_id=1, source_target_pairs={{0,4},{2,6},{4,0},{6,2},{8,12},{10,14},{12,8},{14,10},{16,20},{18,... | collective-permute-start | bytes 442376 | tf_op jit(solution)/shard_map/ppermute | solution.py:234
  16.0 0.5 collective-permute-start.5
  16.4 0.0 collective-permute-start.6
  16.5 2.9 %collective-permute-done.3.refs_0_ = bf16[4,144,128]{2,1,0:T(8,128)(2,1)S(1)} collective-permute-done((bf16[4,144,128]{2,1,0:T(8,128)(2,1)S(1)}, bf16[4,144,128]{2,1,0:T(8,128)(2,1)S(1)}, u32[]{:S(2)}, u32[]{:S(2)}) %collective-permute-start.3) | collective-permute-done | bytes 147488 | tf_op jit(solution)/shard_map/ppermute | solution.py:234
  19.3 0.0 copy-start.13
  19.3 0.0 collective-permute-start.7
  19.3 2.8 %collective-permute-done.4.refs_1_ = bf16[4,144,128]{2,1,0:T(8,128)(2,1)S(1)} collective-permute-done((bf16[4,144,128]{2,1,0:T(8,128)(2,1)S(1)}, bf16[4,144,128]{2,1,0:T(8,128)(2,1)S(1)}, u32[]{:S(2)}, u32[]{:S(2)}) %collective-permute-start.4) | collective-permute-done | bytes 147488 | tf_op jit(solution)/shard_map/ppermute | solution.py:234
  22.1 0.0 copy-start.14
  22.1 0.0 collective-permute-start.8
  22.1 0.0 collective-permute-done.5.refs_2_
  22.2 0.0 copy-start.15
  22.2 0.5 collective-permute-start.9
  22.7 1.4 %copy.8.cl_ref = s32[128,16]{1,0:T(8,128)} copy(s32[128,16]{0,1:T(8,128)} %param.10) | data formatting | bytes 16384 | tf_op args[4]
  24.1 3.2 %shard_map.55 = (bf16[2,2048,128]{2,1,0:T(8,128)(2,1)}, bf16[2048,64]{1,0:T(8,128)(2,1)}) custom-call(bf16[128,1024]{1,0:T(8,128)(2,1)} %q_ref.1, bf16[128,1024]{1,0:T(8,128)(2,1)} %g_ref.1, s32[128,16]{1,0:T(8,128)} %copy.8.cl_ref), custom_call_target="tpu_custom_call" | custom-call | flops 10000000 | bytes 2000000 | tf_op jit(solution)/shard_map/pallas_call | solution.py:43
  27.3 0.0 copy-done.11
  27.3 1.9 %shard_map.56 = (bf16[4,256,128]{2,1,0:T(8,128)(2,1)}, bf16[4,64,128]{2,1,0:T(8,128)(2,1)}, bf16[512,128]{1,0:T(8,128)(2,1)}) custom-call(bf16[4,144,128]{2,1,0:T(8,128)(2,1)} %copy-done.11), custom_call_target="tpu_custom_call" | custom-call | flops 4000000 | bytes 400000 | tf_op jit(solution)/shard_map/pallas_call | solution.py:92
  29.2 0.0 copy-done.13
  29.2 0.0 copy-done.14
  29.2 0.0 copy-done.15
  29.2 2.8 %shard_map.57 = (bf16[12,256,128]{2,1,0:T(8,128)(2,1)}, bf16[12,64,128]{2,1,0:T(8,128)(2,1)}, bf16[1536,128]{1,0:T(8,128)(2,1)}) custom-call(bf16[4,144,128]{2,1,0:T(8,128)(2,1)} %copy-done.13, bf16[4,144,128]{2,1,0:T(8,128)(2,1)} %copy-done.14, bf16[4,144,128]{2,1,0:T(8,128)(2,1)} %copy-done.15), custom_call_target="tpu_custom_call" | custom-call | flops 12000000 | bytes 1200000 | tf_op jit(solution)/shard_map/pallas_call | solution.py:92
  32.0 0.0 collective-permute-done.6.refs_0_
  32.0 0.0 copy-start.16
  32.0 0.0 collective-permute-done.7.refs_1_
  32.0 0.0 copy-start.17
  32.0 0.0 collective-permute-done.8.refs_2_
  32.0 0.0 copy-start.18
  32.1 0.0 collective-permute-done.9.refs_3_
  32.1 0.6 copy-done.16
  32.7 0.0 copy-done.17
  32.7 0.1 copy-done.18
  32.8 0.7 copy-done.19
  33.5 3.2 %shard_map.58 = (bf16[16,256,128]{2,1,0:T(8,128)(2,1)}, bf16[16,64,128]{2,1,0:T(8,128)(2,1)}, bf16[2048,128]{1,0:T(8,128)(2,1)}) custom-call(bf16[4,144,128]{2,1,0:T(8,128)(2,1)} %copy-done.16, bf16[4,144,128]{2,1,0:T(8,128)(2,1)} %copy-done.17, bf16[4,144,128]{2,1,0:T(8,128)(2,1)} %copy-done.18, bf16[4,144,128]{2,1,0:T(8,128)(2,1)} %copy-done.19), custom_call_target="tpu_custom_call" | custom-call | flops 16000000 | bytes 1600000 | tf_op jit(solution)/shard_map/pallas_call | solution.py:92
  36.7 1.2 %copy-done = bf16[2,2048,128]{2,1,0:T(8,128)(2,1)S(1)} copy-done((bf16[2,2048,128]{2,1,0:T(8,128)(2,1)S(1)}, bf16[2,2048,128]{2,1,0:T(8,128)(2,1)}, u32[]{:S(2)}) %copy-start) | copy-done | bytes 1048600
  38.0 1.2 %copy-done.1 = bf16[16,256,128]{2,1,0:T(8,128)(2,1)S(1)} copy-done((bf16[16,256,128]{2,1,0:T(8,128)(2,1)S(1)}, bf16[16,256,128]{2,1,0:T(8,128)(2,1)}, u32[]{:S(2)}) %copy-start.1) | copy-done | bytes 1048600
  39.2 1.1 %copy-done.2 = bf16[12,256,128]{2,1,0:T(8,128)(2,1)S(1)} copy-done((bf16[12,256,128]{2,1,0:T(8,128)(2,1)S(1)}, bf16[12,256,128]{2,1,0:T(8,128)(2,1)}, u32[]{:S(2)}) %copy-start.2) | copy-done | bytes 786456
  40.3 1.0 copy-done.3
  41.4 1.0 copy-done.4
  42.4 1.0 copy-done.5
  43.4 0.9 copy-done.6
  44.3 0.9 copy-done.7
  45.3 0.9 copy-done.8
  46.2 0.9 copy-done.9
  47.1 0.8 copy-done.10
  48.0 26.0 %shard_map.59 = bf16[128,1024]{1,0:T(8,128)(2,1)S(1)} custom-call(bf16[2,2048,128]{2,1,0:T(8,128)(2,1)S(1)} %copy-done, bf16[2048,64]{1,0:T(8,128)(2,1)S(1)} %copy-done.3, bf16[4,256,128]{2,1,0:T(8,128)(2,1)S(1)} %copy-done.6, bf16[4,64,128]{2,1,0:T(8,128)(2,1)S(1)} %copy-done.10, bf16[512,128]{1,0:T(8,128)(2,1)S(1)} %copy-done.9, ...), custom_call_target="tpu_custom_call" | custom-call | flops 3221225472 | bytes 10000000 | tf_op jit(solution)/shard_map/pallas_call | solution.py:212
  74.0 0.1 collective-permute-start.11
  74.1 0.0 copy-done.12
  74.1 0.2 copy.7
  74.3 0.5 collective-permute-start.10
  74.8 1.0 collective-permute-done.10
  75.8 0.0 collective-permute-done.11
  75.8 0.4 fusion
  76.3 0.4 add_convert_fusion
  76.7 29.3 %all_to_all.5 = bf16[16,32,1024]{2,1,0:T(8,128)(2,1)S(1)} all-to-all(bf16[16,32,1024]{2,1,0:T(8,128)(2,1)S(1)} %bitcast.12), channel_id=1, replica_groups=mesh['seq'=16,'pair'=2] {'seq'}, dimensions={0} | all-to-all | bytes 2097152 | tf_op jit(solution)/shard_map/all_to_all | solution.py:268
  106.0 0.8 convert_reduce_fusion
  (15 shorter events, 0.1 us)
Async XLA Ops:
  1.5 5.6 %collective-permute-start = (bf16[1,144,128]{2,1,0:T(8,128)(2,1)S(1)}, bf16[1,144,128]{2,1,0:T(8,128)(2,1)S(1)}, u32[]{:S(2)}, u32[]{:S(2)}) collective-permute-start(bf16[1,144,128]{2,1,0:T(8,128)(2,1)S(1)} %maximum_bitcast_fusion), channel_id=1, source_target_pairs={{0,8},{2,10},{4,12},{6,14},{8,0},{10,2},{12,4},{14,6},{16,24},{18,... | collective-permute-start | bytes 110600 | tf_op jit(solution)/shard_map/ppermute | solution.py:234
  4.5 5.5 %collective-permute-start.1 = (bf16[1,144,128]{2,1,0:T(8,128)(2,1)S(1)}, bf16[1,144,128]{2,1,0:T(8,128)(2,1)S(1)}, u32[]{:S(2)}, u32[]{:S(2)}) collective-permute-start(bf16[1,144,128]{2,1,0:T(8,128)(2,1)S(1)} %maximum_bitcast_fusion), channel_id=1, source_target_pairs={{0,16},{2,18},{4,20},{6,22},{8,24},{10,26},{12,28},{14,30},{16,0},... | collective-permute-start | bytes 110600 | tf_op jit(solution)/shard_map/ppermute | solution.py:234
  7.1 5.8 %collective-permute-start.2 = (bf16[1,144,128]{2,1,0:T(8,128)(2,1)S(1)}, bf16[1,144,128]{2,1,0:T(8,128)(2,1)S(1)}, u32[]{:S(2)}, u32[]{:S(2)}) collective-permute-start(bf16[1,144,128]{2,1,0:T(8,128)(2,1)S(1)} %maximum_bitcast_fusion), channel_id=1, source_target_pairs={{0,24},{2,26},{4,28},{6,30},{8,16},{10,18},{12,20},{14,22},{16,8},... | collective-permute-start | bytes 110600 | tf_op jit(solution)/shard_map/ppermute | solution.py:234
  12.9 14.4 %copy-start.11 = (bf16[4,144,128]{2,1,0:T(8,128)(2,1)}, bf16[4,144,128]{2,1,0:T(8,128)(2,1)S(1)}, u32[]{:S(2)}) copy-start(bf16[4,144,128]{2,1,0:T(8,128)(2,1)S(1)} %pad_maximum_fusion.refs_0_) | copy-start | bytes 442372
  12.9 6.4 %collective-permute-start.3 = (bf16[4,144,128]{2,1,0:T(8,128)(2,1)S(1)}, bf16[4,144,128]{2,1,0:T(8,128)(2,1)S(1)}, u32[]{:S(2)}, u32[]{:S(2)}) collective-permute-start(bf16[4,144,128]{2,1,0:T(8,128)(2,1)S(1)} %pad_maximum_fusion.refs_0_), channel_id=1, source_target_pairs={{0,2},{2,0},{4,6},{6,4},{8,10},{10,8},{12,14},{14,12},{16,18},{18,... | collective-permute-start | bytes 442376 | tf_op jit(solution)/shard_map/ppermute | solution.py:234
  14.5 7.7 %collective-permute-start.4 = (bf16[4,144,128]{2,1,0:T(8,128)(2,1)S(1)}, bf16[4,144,128]{2,1,0:T(8,128)(2,1)S(1)}, u32[]{:S(2)}, u32[]{:S(2)}) collective-permute-start(bf16[4,144,128]{2,1,0:T(8,128)(2,1)S(1)} %pad_maximum_fusion.refs_0_), channel_id=1, source_target_pairs={{0,4},{2,6},{4,0},{6,2},{8,12},{10,14},{12,8},{14,10},{16,20},{18,... | collective-permute-start | bytes 442376 | tf_op jit(solution)/shard_map/ppermute | solution.py:234
  16.0 6.2 %collective-permute-start.5 = (bf16[4,144,128]{2,1,0:T(8,128)(2,1)S(1)}, bf16[4,144,128]{2,1,0:T(8,128)(2,1)S(1)}, u32[]{:S(2)}, u32[]{:S(2)}) collective-permute-start(bf16[4,144,128]{2,1,0:T(8,128)(2,1)S(1)} %pad_maximum_fusion.refs_0_), channel_id=1, source_target_pairs={{0,6},{2,4},{4,2},{6,0},{8,14},{10,12},{12,10},{14,8},{16,22},{18,... | collective-permute-start | bytes 442376 | tf_op jit(solution)/shard_map/ppermute | solution.py:234
  16.4 15.6 %collective-permute-start.6 = (bf16[4,144,128]{2,1,0:T(8,128)(2,1)S(1)}, bf16[4,144,128]{2,1,0:T(8,128)(2,1)S(1)}, u32[]{:S(2)}, u32[]{:S(2)}) collective-permute-start(bf16[4,144,128]{2,1,0:T(8,128)(2,1)S(1)} %pad_maximum_fusion.refs_0_), channel_id=1, source_target_pairs={{0,1},{1,0},{2,3},{3,2},{4,5},{5,4},{6,7},{7,6},{8,9},{9,8},{10,11... | collective-permute-start | bytes 442376 | tf_op jit(solution)/shard_map/ppermute | solution.py:234
  19.3 9.9 %copy-start.13 = (bf16[4,144,128]{2,1,0:T(8,128)(2,1)}, bf16[4,144,128]{2,1,0:T(8,128)(2,1)S(1)}, u32[]{:S(2)}) copy-start(bf16[4,144,128]{2,1,0:T(8,128)(2,1)S(1)} %collective-permute-done.3.refs_0_) | copy-start | bytes 442372
  19.3 12.7 %collective-permute-start.7 = (bf16[4,144,128]{2,1,0:T(8,128)(2,1)S(1)}, bf16[4,144,128]{2,1,0:T(8,128)(2,1)S(1)}, u32[]{:S(2)}, u32[]{:S(2)}) collective-permute-start(bf16[4,144,128]{2,1,0:T(8,128)(2,1)S(1)} %collective-permute-done.3.refs_0_), channel_id=1, source_target_pairs={{0,1},{1,0},{2,3},{3,2},{4,5},{5,4},{6,7},{7,6},{8,9},{9,8},{10,11... | collective-permute-start | bytes 442376 | tf_op jit(solution)/shard_map/ppermute | solution.py:234
  22.1 7.1 %copy-start.14 = (bf16[4,144,128]{2,1,0:T(8,128)(2,1)}, bf16[4,144,128]{2,1,0:T(8,128)(2,1)S(1)}, u32[]{:S(2)}) copy-start(bf16[4,144,128]{2,1,0:T(8,128)(2,1)S(1)} %collective-permute-done.4.refs_1_) | copy-start | bytes 442372
  22.1 9.9 %collective-permute-start.8 = (bf16[4,144,128]{2,1,0:T(8,128)(2,1)S(1)}, bf16[4,144,128]{2,1,0:T(8,128)(2,1)S(1)}, u32[]{:S(2)}, u32[]{:S(2)}) collective-permute-start(bf16[4,144,128]{2,1,0:T(8,128)(2,1)S(1)} %collective-permute-done.4.refs_1_), channel_id=1, source_target_pairs={{0,1},{1,0},{2,3},{3,2},{4,5},{5,4},{6,7},{7,6},{8,9},{9,8},{10,11... | collective-permute-start | bytes 442376 | tf_op jit(solution)/shard_map/ppermute | solution.py:234
  22.2 7.0 %copy-start.15 = (bf16[4,144,128]{2,1,0:T(8,128)(2,1)}, bf16[4,144,128]{2,1,0:T(8,128)(2,1)S(1)}, u32[]{:S(2)}) copy-start(bf16[4,144,128]{2,1,0:T(8,128)(2,1)S(1)} %collective-permute-done.5.refs_2_) | copy-start | bytes 442372
  22.2 9.9 %collective-permute-start.9 = (bf16[4,144,128]{2,1,0:T(8,128)(2,1)S(1)}, bf16[4,144,128]{2,1,0:T(8,128)(2,1)S(1)}, u32[]{:S(2)}, u32[]{:S(2)}) collective-permute-start(bf16[4,144,128]{2,1,0:T(8,128)(2,1)S(1)} %collective-permute-done.5.refs_2_), channel_id=1, source_target_pairs={{0,1},{1,0},{2,3},{3,2},{4,5},{5,4},{6,7},{7,6},{8,9},{9,8},{10,11... | collective-permute-start | bytes 442376 | tf_op jit(solution)/shard_map/ppermute | solution.py:234
  32.0 0.7 copy-start.16
  32.0 0.7 copy-start.17
  32.0 0.8 copy-start.18
  32.8 0.7 copy-start.19
  36.7 1.2 %copy-start = (bf16[2,2048,128]{2,1,0:T(8,128)(2,1)S(1)}, bf16[2,2048,128]{2,1,0:T(8,128)(2,1)}, u32[]{:S(2)}) copy-start(bf16[2,2048,128]{2,1,0:T(8,128)(2,1)} %get-tuple-element.16.lhs) | copy-start | bytes 3145732
  37.9 1.2 %copy-start.1 = (bf16[16,256,128]{2,1,0:T(8,128)(2,1)S(1)}, bf16[16,256,128]{2,1,0:T(8,128)(2,1)}, u32[]{:S(2)}) copy-start(bf16[16,256,128]{2,1,0:T(8,128)(2,1)} %get-tuple-element.24.refs_6_) | copy-start | bytes 3145732
  39.2 1.1 %copy-start.2 = (bf16[12,256,128]{2,1,0:T(8,128)(2,1)S(1)}, bf16[12,256,128]{2,1,0:T(8,128)(2,1)}, u32[]{:S(2)}) copy-start(bf16[12,256,128]{2,1,0:T(8,128)(2,1)} %get-tuple-element.21.refs_3_) | copy-start | bytes 2359300
  40.3 1.0 copy-start.3
  41.3 1.0 copy-start.4
  42.4 1.0 copy-start.5
  43.4 0.9 copy-start.6
  44.3 0.9 copy-start.7
  45.3 0.9 copy-start.8
  46.2 0.9 copy-start.9
  47.1 0.8 copy-start.10
  48.0 26.2 %copy-start.12 = (bf16[128,1024]{1,0:T(8,128)(2,1)S(1)}, bf16[128,1024]{1,0:T(8,128)(2,1)}, u32[]{:S(2)}) copy-start(bf16[128,1024]{1,0:T(8,128)(2,1)} %param.6) | copy-start | bytes 786436
  74.0 1.8 %collective-permute-start.11 = (bf16[128,1024]{1,0:T(8,128)(2,1)S(1)}, bf16[128,1024]{1,0:T(8,128)(2,1)S(1)}, u32[]{:S(2)}, u32[]{:S(2)}) collective-permute-start(bf16[128,1024]{1,0:T(8,128)(2,1)S(1)} %shard_map.59), channel_id=1, source_target_pairs={{0,1},{1,0},{2,3},{3,2},{4,5},{5,4},{6,7},{7,6},{8,9},{9,8},{10,11... | collective-permute-start | bytes 786440 | tf_op jit(solution)/shard_map/ppermute | solution.py:234
  74.3 1.5 %collective-permute-start.10 = (bf16[128,512]{0,1:T(8,128)(2,1)S(1)}, bf16[128,512]{0,1:T(8,128)(2,1)S(1)}, u32[]{:S(2)}, u32[]{:S(2)}) collective-permute-start(bf16[128,512]{0,1:T(8,128)(2,1)S(1)} %bitcast.15), channel_id=1, source_target_pairs={{0,1},{1,0},{2,3},{3,2},{4,5},{5,4},{6,7},{7,6},{8,9},{9,8},{10,11... | collective-permute-start | bytes 393224 | tf_op jit(solution)/shard_map/ppermute | solution.py:234

commit v3 on v2

--- a/solution.py
+++ b/solution.py
@@ -46,6 +46,7 @@
             jax.ShapeDtypeStruct((2, rows, 2 * HD), jnp.bfloat16),
             jax.ShapeDtypeStruct((rows, HD), jnp.bfloat16),
         ),
+        compiler_params=pltpu.CompilerParams(vmem_limit_bytes=8 * 1024 * 1024),
         cost_estimate=pl.CostEstimate(flops=10**7, bytes_accessed=2 * 10**6, transcendentals=0),
     )(queries, out_grad, cluster_of)
 
@@ -96,6 +97,7 @@
             jax.ShapeDtypeStruct((blocks, HD, tok), jnp.bfloat16),
             jax.ShapeDtypeStruct((blocks * tok, 2 * HD), jnp.bfloat16),
         ),
+        compiler_params=pltpu.CompilerParams(vmem_limit_bytes=8 * 1024 * 1024),
         cost_estimate=pl.CostEstimate(
             flops=blocks * 10**6, bytes_accessed=blocks * 10**5, transcendentals=0
         ),

time: 108 us -> 88 us (0.81)
  local copies, waits for them, and re-layouts: 14.3 us -> 2.89 us
  Pallas kernels: 37.2 us -> 29.3 us
    unnamed x42 -> x8, local copies, waits for them, and re-layouts: 14.3 us -> 2.86 us
    pallas_call x3, Pallas kernels: 7.96 us -> 2.3 us  [prepare_keys(): pl.pallas_call(prepare_keys_kernel, out_shape=(jax.ShapeDtypeStruct((bloc...]
    pallas_call x1, Pallas kernels: 3.2 us -> 0.99 us  [prepare_rows(): pl.pallas_call(prepare_rows_kernel, out_shape=(jax.ShapeDtypeStruct((2, r...]
  transfers between devices with their start and end apart: 12 -> 12, of which waited for: 5 -> 5; matrix products, arithmetic and copies ran while one was open for 2% -> 1% of each run, Pallas kernels for 7% -> 2%
where the time goes in v3:
time: 88 us; the launch traced here: 87.6 us
  Pallas kernels  29.3 us (33%)
  blocking collectives  29.3 us (33%)
  waiting for transfers between devices  12.4 us (14%)
  starting transfers between devices  10.3 us (12%)
  local copies, waits for them, and re-layouts  2.89 us (3%)
  other arithmetic  2.32 us (3%)
    all_to_all x1, blocking collectives, dense(): got = lax.all_to_all(block, 'seq', 0, 0, tiled=True)  29.3 us
    pallas_call x1, Pallas kernels, attend(): pl.pallas_call(attend_kernel, in_specs=[pl.BlockSpec(memory_space=pltpu.V...  26 us
    ppermute x12, waiting for transfers between devices, xor_permute(): return lax.ppermute(x, axis, [(i, i ^ mask) for i in range(n)])  12.4 us
    ppermute x12, starting transfers between devices, xor_permute(): return lax.ppermute(x, axis, [(i, i ^ mask) for i in range(n)])  10.3 us
    unnamed x8, local copies, waits for them, and re-layouts  2.86 us
    pallas_call x3, Pallas kernels, prepare_keys(): pl.pallas_call(prepare_keys_kernel, out_shape=(jax.ShapeDtypeStruct((bloc...  2.3 us
  transfers between devices with their start and end apart: 12, of which 5 were waited for; matrix products, arithmetic and copies ran while one was open for 1% of the time, Pallas kernels for 2%

profile of v3, /device:TPU:0, one launch (start us, length us, event | category | flops | bytes accessed | tf_op | source)
XLA Modules:
  0.0 87.6 jit_solution(9749885804616434585)
XLA Ops:
  0.0 0.7 convert_bitcast_fusion
  0.7 0.8 maximum_bitcast_fusion
  1.5 3.1 %collective-permute-start = (bf16[1,144,128]{2,1,0:T(8,128)(2,1)S(1)}, bf16[1,144,128]{2,1,0:T(8,128)(2,1)S(1)}, u32[]{:S(2)}, u32[]{:S(2)}) collective-permute-start(bf16[1,144,128]{2,1,0:T(8,128)(2,1)S(1)} %maximum_bitcast_fusion), channel_id=1, source_target_pairs={{0,8},{2,10},{4,12},{6,14},{8,0},{10,2},{12,4},{14,6},{16,24},{18,... | collective-permute-start | bytes 110600 | tf_op jit(solution)/shard_map/ppermute | solution.py:236
  4.5 2.6 %collective-permute-start.1 = (bf16[1,144,128]{2,1,0:T(8,128)(2,1)S(1)}, bf16[1,144,128]{2,1,0:T(8,128)(2,1)S(1)}, u32[]{:S(2)}, u32[]{:S(2)}) collective-permute-start(bf16[1,144,128]{2,1,0:T(8,128)(2,1)S(1)} %maximum_bitcast_fusion), channel_id=1, source_target_pairs={{0,16},{2,18},{4,20},{6,22},{8,24},{10,26},{12,28},{14,30},{16,0},... | collective-permute-start | bytes 110600 | tf_op jit(solution)/shard_map/ppermute | solution.py:236
  7.1 0.0 collective-permute-start.2
  7.1 0.0 collective-permute-done
  7.1 2.9 %collective-permute-done.1 = bf16[1,144,128]{2,1,0:T(8,128)(2,1)S(1)} collective-permute-done((bf16[1,144,128]{2,1,0:T(8,128)(2,1)S(1)}, bf16[1,144,128]{2,1,0:T(8,128)(2,1)S(1)}, u32[]{:S(2)}, u32[]{:S(2)}) %collective-permute-start.1) | collective-permute-done | bytes 36896 | tf_op jit(solution)/shard_map/ppermute | solution.py:236
  10.0 2.8 %collective-permute-done.2 = bf16[1,144,128]{2,1,0:T(8,128)(2,1)S(1)} collective-permute-done((bf16[1,144,128]{2,1,0:T(8,128)(2,1)S(1)}, bf16[1,144,128]{2,1,0:T(8,128)(2,1)S(1)}, u32[]{:S(2)}, u32[]{:S(2)}) %collective-permute-start.2) | collective-permute-done | bytes 36896 | tf_op jit(solution)/shard_map/ppermute | solution.py:236
  12.9 1.6 %collective-permute-start.3 = (bf16[4,144,128]{2,1,0:T(8,128)(2,1)S(1)}, bf16[4,144,128]{2,1,0:T(8,128)(2,1)S(1)}, u32[]{:S(2)}, u32[]{:S(2)}) collective-permute-start(bf16[4,144,128]{2,1,0:T(8,128)(2,1)S(1)} %pad_maximum_fusion.refs_0_), channel_id=1, source_target_pairs={{0,2},{2,0},{4,6},{6,4},{8,10},{10,8},{12,14},{14,12},{16,18},{18,... | collective-permute-start | bytes 442376 | tf_op jit(solution)/shard_map/ppermute | solution.py:236
  14.4 1.5 %collective-permute-start.4 = (bf16[4,144,128]{2,1,0:T(8,128)(2,1)S(1)}, bf16[4,144,128]{2,1,0:T(8,128)(2,1)S(1)}, u32[]{:S(2)}, u32[]{:S(2)}) collective-permute-start(bf16[4,144,128]{2,1,0:T(8,128)(2,1)S(1)} %pad_maximum_fusion.refs_0_), channel_id=1, source_target_pairs={{0,4},{2,6},{4,0},{6,2},{8,12},{10,14},{12,8},{14,10},{16,20},{18,... | collective-permute-start | bytes 442376 | tf_op jit(solution)/shard_map/ppermute | solution.py:236
  16.0 0.5 collective-permute-start.5
  16.4 0.0 collective-permute-start.6
  16.4 2.9 %collective-permute-done.3.refs_0_ = bf16[4,144,128]{2,1,0:T(8,128)(2,1)S(1)} collective-permute-done((bf16[4,144,128]{2,1,0:T(8,128)(2,1)S(1)}, bf16[4,144,128]{2,1,0:T(8,128)(2,1)S(1)}, u32[]{:S(2)}, u32[]{:S(2)}) %collective-permute-start.3) | collective-permute-done | bytes 147488 | tf_op jit(solution)/shard_map/ppermute | solution.py:236
  19.3 0.0 collective-permute-start.7
  19.3 2.8 %collective-permute-done.4.refs_1_ = bf16[4,144,128]{2,1,0:T(8,128)(2,1)S(1)} collective-permute-done((bf16[4,144,128]{2,1,0:T(8,128)(2,1)S(1)}, bf16[4,144,128]{2,1,0:T(8,128)(2,1)S(1)}, u32[]{:S(2)}, u32[]{:S(2)}) %collective-permute-start.4) | collective-permute-done | bytes 147488 | tf_op jit(solution)/shard_map/ppermute | solution.py:236
  22.1 0.0 collective-permute-start.8
  22.1 0.0 collective-permute-done.5.refs_2_
  22.1 0.5 collective-permute-start.9
  22.6 0.8 copy.8.cl_ref
  23.4 0.0 copy-start
  23.4 0.9 %copy-done = bf16[128,1024]{1,0:T(8,128)(2,1)S(1)} copy-done((bf16[128,1024]{1,0:T(8,128)(2,1)S(1)}, bf16[128,1024]{1,0:T(8,128)(2,1)}, u32[]{:S(2)}) %copy-start) | copy-done | bytes 262168
  24.4 0.0 copy-start.1
  24.4 0.9 %copy-done.1 = bf16[128,1024]{1,0:T(8,128)(2,1)S(1)} copy-done((bf16[128,1024]{1,0:T(8,128)(2,1)S(1)}, bf16[128,1024]{1,0:T(8,128)(2,1)}, u32[]{:S(2)}) %copy-start.1) | copy-done | bytes 262168
  25.3 1.0 %shard_map.55 = (bf16[2,2048,128]{2,1,0:T(8,128)(2,1)S(1)}, bf16[2048,64]{1,0:T(8,128)(2,1)S(1)}) custom-call(bf16[128,1024]{1,0:T(8,128)(2,1)S(1)} %copy-done, bf16[128,1024]{1,0:T(8,128)(2,1)S(1)} %copy-done.1, s32[128,16]{1,0:T(8,128)S(1)} %copy.8.cl_ref), custom_call_target="tpu_custom_call" | custom-call | flops 10000000 | bytes 2000000 | tf_op jit(solution)/shard_map/pallas_call | solution.py:43
  26.3 0.3 shard_map.56
  26.6 0.9 shard_map.57
  27.5 0.0 collective-permute-done.6.refs_0_
  27.5 0.0 collective-permute-done.7.refs_1_
  27.5 0.0 collective-permute-done.8.refs_2_
  27.5 0.0 collective-permute-done.9.refs_3_
  27.5 1.1 %shard_map.58 = (bf16[16,256,128]{2,1,0:T(8,128)(2,1)S(1)}, bf16[16,64,128]{2,1,0:T(8,128)(2,1)S(1)}, bf16[2048,128]{1,0:T(8,128)(2,1)S(1)}) custom-call(bf16[4,144,128]{2,1,0:T(8,128)(2,1)S(1)} %collective-permute-done.6.refs_0_, bf16[4,144,128]{2,1,0:T(8,128)(2,1)S(1)} %collective-permute-done.7.refs_1_, ...), custom_call_target="tpu_custom_call" | custom-call | flops 16000000 | bytes 1600000 | tf_op jit(solution)/shard_map/pallas_call | solution.py:93
  28.7 0.0 copy-start.2
  28.7 26.0 %shard_map.59 = bf16[128,1024]{1,0:T(8,128)(2,1)S(1)} custom-call(bf16[2,2048,128]{2,1,0:T(8,128)(2,1)S(1)} %get-tuple-element.16.lhs, bf16[2048,64]{1,0:T(8,128)(2,1)S(1)} %get-tuple-element.17.grd, bf16[4,256,128]{2,1,0:T(8,128)(2,1)S(1)} %get-tuple-element.18.refs_0_, bf16[4,64,128]{2,1,0:T(8,128)(2,1)S(1)} %get-tuple-element.19.refs_1_, ...), custom_call_target="tpu_custom_call" | custom-call | flops 3221225472 | bytes 10000000 | tf_op jit(solution)/shard_map/pallas_call | solution.py:214
  54.7 0.1 collective-permute-start.11
  54.8 0.0 copy-done.2
  54.8 0.2 copy.7
  55.1 0.5 collective-permute-start.10
  55.6 1.0 %collective-permute-done.10 = bf16[128,512]{0,1:T(8,128)(2,1)S(1)} collective-permute-done((bf16[128,512]{0,1:T(8,128)(2,1)S(1)}, bf16[128,512]{0,1:T(8,128)(2,1)S(1)}, u32[]{:S(2)}, u32[]{:S(2)}) %collective-permute-start.10) | collective-permute-done | bytes 131104 | tf_op jit(solution)/shard_map/ppermute | solution.py:236
  56.6 0.0 collective-permute-done.11
  56.6 0.4 fusion
  57.0 0.4 add_convert_fusion
  57.4 29.3 %all_to_all.5 = bf16[16,32,1024]{2,1,0:T(8,128)(2,1)S(1)} all-to-all(bf16[16,32,1024]{2,1,0:T(8,128)(2,1)S(1)} %bitcast.12), channel_id=1, replica_groups=mesh['seq'=16,'pair'=2] {'seq'}, dimensions={0} | all-to-all | bytes 2097152 | tf_op jit(solution)/shard_map/all_to_all | solution.py:270
  86.8 0.8 convert_reduce_fusion
  (2 shorter events, 0.0 us)
Async XLA Ops:
  1.5 5.6 %collective-permute-start = (bf16[1,144,128]{2,1,0:T(8,128)(2,1)S(1)}, bf16[1,144,128]{2,1,0:T(8,128)(2,1)S(1)}, u32[]{:S(2)}, u32[]{:S(2)}) collective-permute-start(bf16[1,144,128]{2,1,0:T(8,128)(2,1)S(1)} %maximum_bitcast_fusion), channel_id=1, source_target_pairs={{0,8},{2,10},{4,12},{6,14},{8,0},{10,2},{12,4},{14,6},{16,24},{18,... | collective-permute-start | bytes 110600 | tf_op jit(solution)/shard_map/ppermute | solution.py:236
  4.5 5.5 %collective-permute-start.1 = (bf16[1,144,128]{2,1,0:T(8,128)(2,1)S(1)}, bf16[1,144,128]{2,1,0:T(8,128)(2,1)S(1)}, u32[]{:S(2)}, u32[]{:S(2)}) collective-permute-start(bf16[1,144,128]{2,1,0:T(8,128)(2,1)S(1)} %maximum_bitcast_fusion), channel_id=1, source_target_pairs={{0,16},{2,18},{4,20},{6,22},{8,24},{10,26},{12,28},{14,30},{16,0},... | collective-permute-start | bytes 110600 | tf_op jit(solution)/shard_map/ppermute | solution.py:236
  7.1 5.8 %collective-permute-start.2 = (bf16[1,144,128]{2,1,0:T(8,128)(2,1)S(1)}, bf16[1,144,128]{2,1,0:T(8,128)(2,1)S(1)}, u32[]{:S(2)}, u32[]{:S(2)}) collective-permute-start(bf16[1,144,128]{2,1,0:T(8,128)(2,1)S(1)} %maximum_bitcast_fusion), channel_id=1, source_target_pairs={{0,24},{2,26},{4,28},{6,30},{8,16},{10,18},{12,20},{14,22},{16,8},... | collective-permute-start | bytes 110600 | tf_op jit(solution)/shard_map/ppermute | solution.py:236
  12.9 6.4 %collective-permute-start.3 = (bf16[4,144,128]{2,1,0:T(8,128)(2,1)S(1)}, bf16[4,144,128]{2,1,0:T(8,128)(2,1)S(1)}, u32[]{:S(2)}, u32[]{:S(2)}) collective-permute-start(bf16[4,144,128]{2,1,0:T(8,128)(2,1)S(1)} %pad_maximum_fusion.refs_0_), channel_id=1, source_target_pairs={{0,2},{2,0},{4,6},{6,4},{8,10},{10,8},{12,14},{14,12},{16,18},{18,... | collective-permute-start | bytes 442376 | tf_op jit(solution)/shard_map/ppermute | solution.py:236
  14.4 7.7 %collective-permute-start.4 = (bf16[4,144,128]{2,1,0:T(8,128)(2,1)S(1)}, bf16[4,144,128]{2,1,0:T(8,128)(2,1)S(1)}, u32[]{:S(2)}, u32[]{:S(2)}) collective-permute-start(bf16[4,144,128]{2,1,0:T(8,128)(2,1)S(1)} %pad_maximum_fusion.refs_0_), channel_id=1, source_target_pairs={{0,4},{2,6},{4,0},{6,2},{8,12},{10,14},{12,8},{14,10},{16,20},{18,... | collective-permute-start | bytes 442376 | tf_op jit(solution)/shard_map/ppermute | solution.py:236
  16.0 6.2 %collective-permute-start.5 = (bf16[4,144,128]{2,1,0:T(8,128)(2,1)S(1)}, bf16[4,144,128]{2,1,0:T(8,128)(2,1)S(1)}, u32[]{:S(2)}, u32[]{:S(2)}) collective-permute-start(bf16[4,144,128]{2,1,0:T(8,128)(2,1)S(1)} %pad_maximum_fusion.refs_0_), channel_id=1, source_target_pairs={{0,6},{2,4},{4,2},{6,0},{8,14},{10,12},{12,10},{14,8},{16,22},{18,... | collective-permute-start | bytes 442376 | tf_op jit(solution)/shard_map/ppermute | solution.py:236
  16.4 11.1 %collective-permute-start.6 = (bf16[4,144,128]{2,1,0:T(8,128)(2,1)S(1)}, bf16[4,144,128]{2,1,0:T(8,128)(2,1)S(1)}, u32[]{:S(2)}, u32[]{:S(2)}) collective-permute-start(bf16[4,144,128]{2,1,0:T(8,128)(2,1)S(1)} %pad_maximum_fusion.refs_0_), channel_id=1, source_target_pairs={{0,1},{1,0},{2,3},{3,2},{4,5},{5,4},{6,7},{7,6},{8,9},{9,8},{10,11... | collective-permute-start | bytes 442376 | tf_op jit(solution)/shard_map/ppermute | solution.py:236
  19.3 8.2 %collective-permute-start.7 = (bf16[4,144,128]{2,1,0:T(8,128)(2,1)S(1)}, bf16[4,144,128]{2,1,0:T(8,128)(2,1)S(1)}, u32[]{:S(2)}, u32[]{:S(2)}) collective-permute-start(bf16[4,144,128]{2,1,0:T(8,128)(2,1)S(1)} %collective-permute-done.3.refs_0_), channel_id=1, source_target_pairs={{0,1},{1,0},{2,3},{3,2},{4,5},{5,4},{6,7},{7,6},{8,9},{9,8},{10,11... | collective-permute-start | bytes 442376 | tf_op jit(solution)/shard_map/ppermute | solution.py:236
  22.1 5.4 %collective-permute-start.8 = (bf16[4,144,128]{2,1,0:T(8,128)(2,1)S(1)}, bf16[4,144,128]{2,1,0:T(8,128)(2,1)S(1)}, u32[]{:S(2)}, u32[]{:S(2)}) collective-permute-start(bf16[4,144,128]{2,1,0:T(8,128)(2,1)S(1)} %collective-permute-done.4.refs_1_), channel_id=1, source_target_pairs={{0,1},{1,0},{2,3},{3,2},{4,5},{5,4},{6,7},{7,6},{8,9},{9,8},{10,11... | collective-permute-start | bytes 442376 | tf_op jit(solution)/shard_map/ppermute | solution.py:236
  22.1 5.4 %collective-permute-start.9 = (bf16[4,144,128]{2,1,0:T(8,128)(2,1)S(1)}, bf16[4,144,128]{2,1,0:T(8,128)(2,1)S(1)}, u32[]{:S(2)}, u32[]{:S(2)}) collective-permute-start(bf16[4,144,128]{2,1,0:T(8,128)(2,1)S(1)} %collective-permute-done.5.refs_2_), channel_id=1, source_target_pairs={{0,1},{1,0},{2,3},{3,2},{4,5},{5,4},{6,7},{7,6},{8,9},{9,8},{10,11... | collective-permute-start | bytes 442376 | tf_op jit(solution)/shard_map/ppermute | solution.py:236
  23.4 1.0 %copy-start = (bf16[128,1024]{1,0:T(8,128)(2,1)S(1)}, bf16[128,1024]{1,0:T(8,128)(2,1)}, u32[]{:S(2)}) copy-start(bf16[128,1024]{1,0:T(8,128)(2,1)} %q_ref.1) | copy-start | bytes 786436
  24.4 0.9 %copy-start.1 = (bf16[128,1024]{1,0:T(8,128)(2,1)S(1)}, bf16[128,1024]{1,0:T(8,128)(2,1)}, u32[]{:S(2)}) copy-start(bf16[128,1024]{1,0:T(8,128)(2,1)} %g_ref.1) | copy-start | bytes 786436
  28.7 26.1 %copy-start.2 = (bf16[128,1024]{1,0:T(8,128)(2,1)S(1)}, bf16[128,1024]{1,0:T(8,128)(2,1)}, u32[]{:S(2)}) copy-start(bf16[128,1024]{1,0:T(8,128)(2,1)} %param.6) | copy-start | bytes 786436
  54.7 1.8 %collective-permute-start.11 = (bf16[128,1024]{1,0:T(8,128)(2,1)S(1)}, bf16[128,1024]{1,0:T(8,128)(2,1)S(1)}, u32[]{:S(2)}, u32[]{:S(2)}) collective-permute-start(bf16[128,1024]{1,0:T(8,128)(2,1)S(1)} %shard_map.59), channel_id=1, source_target_pairs={{0,1},{1,0},{2,3},{3,2},{4,5},{5,4},{6,7},{7,6},{8,9},{9,8},{10,11... | collective-permute-start | bytes 786440 | tf_op jit(solution)/shard_map/ppermute | solution.py:236
  55.1 1.5 %collective-permute-start.10 = (bf16[128,512]{0,1:T(8,128)(2,1)S(1)}, bf16[128,512]{0,1:T(8,128)(2,1)S(1)}, u32[]{:S(2)}, u32[]{:S(2)}) collective-permute-start(bf16[128,512]{0,1:T(8,128)(2,1)S(1)} %bitcast.15), channel_id=1, source_target_pairs={{0,1},{1,0},{2,3},{3,2},{4,5},{5,4},{6,7},{7,6},{8,9},{9,8},{10,11... | collective-permute-start | bytes 393224 | tf_op jit(solution)/shard_map/ppermute | solution.py:236

commit v4 on v3

--- a/solution.py
+++ b/solution.py
@@ -12,6 +12,8 @@
 SCALE = HD ** (-0.5)
 LOG2E = 1.4426950408889634
 TILE = 512
+LAG = 2
+GAP = 4
 
 
 def prepare_rows_kernel(q_ref, g_ref, cl_ref, lhs, grd):
@@ -158,10 +160,13 @@
         denom = jnp.sum(denom, axis=1, keepdims=True)
         inv = jnp.broadcast_to(SCALE / denom, (block, lanes))
         dot = jnp.broadcast_to(jnp.sum(dots, axis=1, keepdims=True) / denom, (block, lanes))
+        gate = None
         for i, c in enumerate(chunks):
             d = (sc[slot][at, c] * inv) * (pg[slot][at, c] - dot)
             ds[slot][i, at, :] = d.astype(jnp.bfloat16)
-        return d[0:16, :]
+            if i % GAP == GAP - 1:
+                gate = d[0:16, :] if gate is None else gate + d[0:16, :]
+        return gate
 
     def collect(slot, t, gate=None):
         g, j = places[t]
@@ -179,11 +184,11 @@
             out_ref[:, pl.ds(where, lanes)] = jnp.where(low, even, odd).astype(jnp.bfloat16)
 
     def stage(step, slot, following):
-        gate = None
+        gates = [None] * LAG
         for t in range(tiles):
-            score(following, 1 - slot, t, gate)
-            collect(1 - slot, t, gate)
-            gate = soften(slot, t)
+            score(following, 1 - slot, t, gates[t])
+            collect(1 - slot, t, gates[t])
+            gates.append(soften(slot, t))
 
         @pl.when(step > 0)
         def _():
@@ -239,36 +244,55 @@
 def dense(tokens_in, queries, key_value, out_grad, cluster_of, slot_of):
     n = lax.axis_size("seq")
     tok, width = queries.shape
+    depth = tokens_in.shape[1]
     me = lax.axis_index("pair")
     low = 1
     while low * low < n:
         low *= 2
     high = n // low
+    part, layer = lax.axis_index("seq") % low, lax.axis_index("seq") // low
+    piece = depth // (2 * n)
+    tie = lax.optimization_barrier
+
     own = jnp.concatenate([key_value, cluster_of.T.astype(jnp.bfloat16)], axis=0)[None]
-    column = jnp.concatenate([own] + [xor_permute(own, "seq", low * k) for k in range(1, high)])
+    above = [xor_permute(own, "seq", low * k) for k in range(1, high)]
+    left = prepare_rows(queries, out_grad, cluster_of)
+    x5 = tokens_in.reshape(tok, high, low, 2, piece).transpose(2, 3, 0, 1, 4)
+    x5 = x5.reshape(low, 2, tok, high * piece)
+    above[-1], left, x5 = tie((above[-1], left, x5))
+    column = jnp.concatenate([own] + above)
     near = [xor_permute(column, "seq", k) for k in range(1, low)]
-    left = prepare_rows(queries, out_grad, cluster_of)
-    groups = [
-        prepare_keys([column]),
-        prepare_keys(near),
-        prepare_keys([xor_permute(p, "pair", 1) for p in [column] + near]),
-    ]
-
-    depth = tokens_in.shape[1]
-    x4 = tokens_in.reshape(tok, n, 2, depth // (2 * n))
-    x_mine = lax.dynamic_index_in_dim(x4, me, 2, keepdims=False).reshape(tok, depth // 2)
-    x_other = lax.dynamic_index_in_dim(x4, 1 - me, 2, keepdims=False).reshape(tok, depth // 2)
-    x_got = xor_permute(x_other, "pair", 1)
+    first = prepare_keys([column])
+    near[-1], first = tie((near[-1], first))
+    far = [xor_permute(p, "pair", 1) for p in [column] + near]
+    second = prepare_keys(near)
+    far[-1], second = tie((far[-1], second))
+    groups = [first, second, prepare_keys(far)]
+
+    x_part = [lax.dynamic_index_in_dim(x5, part ^ k, 0, keepdims=False) for k in range(low)]
+    x_part = [x_part[0]] + [xor_permute(x_part[k], "seq", k) for k in range(1, low)]
+    x_part = jnp.stack(x_part)
+    x_mine = lax.dynamic_index_in_dim(x_part, me, 1, keepdims=False)
+    x_pair = xor_permute(lax.dynamic_index_in_dim(x_part, 1 - me, 1, keepdims=False), "pair", 1)
 
     mine = attend(left, groups, tok)
-    other = xor_permute(mine, "pair", 1)
-    contract = (((0,), (0,)), ((), ()))
-    block = lax.dot_general(
-        x_mine, mine, contract, preferred_element_type=jnp.float32
-    ) + lax.dot_general(x_got, other, contract, preferred_element_type=jnp.float32)
-    block = block.astype(jnp.bfloat16).reshape(n, depth // (2 * n), width)
-    got = lax.all_to_all(block, "seq", 0, 0, tiled=True)
-    return jnp.sum(got.astype(jnp.float32), axis=0)
+
+    def product(x, grad):
+        return lax.dot_general(
+            x, grad, (((0,), (0,)), ((), ())), preferred_element_type=jnp.float32
+        )
+
+    grads = [mine] + [xor_permute(mine, "seq", k) for k in range(1, low)]
+    block = sum(product(x_mine[k], grads[k]) for k in range(low))
+    grads = [xor_permute(g, "pair", 1) for g in grads]
+    block = block + sum(product(x_pair[k], grads[k]) for k in range(low))
+    block = block.reshape(high, piece, width)
+    total = lax.dynamic_index_in_dim(block, layer, 0, keepdims=False)
+    sent = block.astype(jnp.bfloat16)
+    for k in range(1, high):
+        term = lax.dynamic_index_in_dim(sent, layer ^ k, 0, keepdims=False)
+        total = total + xor_permute(term, "seq", low * k).astype(jnp.float32)
+    return total
 
 
 def cluster_grad(query_part, key_part, live_keys):

time: 88 us -> 77.7 us (0.88)
  blocking collectives: 29.3 us -> 0 us
  starting transfers between devices: 10.3 us -> 22.4 us
  waiting for transfers between devices: 12.4 us -> 20.2 us
  Pallas kernels: 29.3 us -> 28.2 us
  matrix products: 0.84 us -> 1.72 us
    all_to_all x1 -> x0, blocking collectives: 29.3 us -> none  [dense(): got = lax.all_to_all(block, 'seq', 0, 0, tiled=True)]
    ppermute x12 -> x24, starting transfers between devices: 10.3 us -> 22.4 us  [xor_permute(): return lax.ppermute(x, axis, [(i, i ^ mask) for i in range(n)])]
    ppermute x12 -> x24, waiting for transfers between devices: 12.4 us -> 20.2 us  [xor_permute(): return lax.ppermute(x, axis, [(i, i ^ mask) for i in range(n)])]
    pallas_call x1, Pallas kernels: 26 us -> 25 us  [attend(): pl.pallas_call(attend_kernel, in_specs=[pl.BlockSpec(memory_space=pltpu.V...]
    dot_general x2 -> x8, matrix products: 0.84 us -> 1.72 us  [product(): lax.dot_general(x, grad, (((0,), (0,)), ((), ())), preferred_element_type...]
  transfers between devices with their start and end apart: 12 -> 24, of which waited for: 5 -> 7; matrix products, arithmetic and copies ran while one was open for 1% -> 3% of each run, Pallas kernels for 2% -> 36%
where the time goes in v4:
time: 77.7 us; the launch traced here: 77.4 us
  Pallas kernels  28.2 us (36%)
  starting transfers between devices  22.4 us (29%)
  waiting for transfers between devices  20.2 us (26%)
  local copies, waits for them, and re-layouts  2.29 us (3%)
  other arithmetic  2.25 us (3%)
  matrix products  1.72 us (2%)
    pallas_call x1, Pallas kernels, attend(): pl.pallas_call(attend_kernel, in_specs=[pl.BlockSpec(memory_space=pltpu.V...  25 us
    ppermute x24, starting transfers between devices, xor_permute(): return lax.ppermute(x, axis, [(i, i ^ mask) for i in range(n)])  22.4 us
    ppermute x24, waiting for transfers between devices, xor_permute(): return lax.ppermute(x, axis, [(i, i ^ mask) for i in range(n)])  20.2 us
    pallas_call x3, Pallas kernels, prepare_keys(): pl.pallas_call(prepare_keys_kernel, out_shape=(jax.ShapeDtypeStruct((bloc...  2.3 us
    unnamed x8, local copies, waits for them, and re-layouts  2.21 us
    dot_general x8, matrix products, product(): lax.dot_general(x, grad, (((0,), (0,)), ((), ())), preferred_element_type...  1.72 us
  transfers between devices with their start and end apart: 24, of which 7 were waited for; matrix products, arithmetic and copies ran while one was open for 3% of the time, Pallas kernels for 36%

profile of v4, /device:TPU:0, one launch (start us, length us, event | category | flops | bytes accessed | tf_op | source)
XLA Modules:
  0.0 77.4 jit_solution(3748380942510656070)
XLA Ops:
  0.0 0.7 convert_bitcast_fusion
  0.7 0.8 %maximum_bitcast_fusion = bf16[1,144,128]{2,1,0:T(8,128)(2,1)S(1)} fusion(bf16[16,128]{1,0:T(8,128)(2,1)S(1)} %convert_bitcast_fusion, bf16[128,128]{1,0:T(8,128)(2,1)} %param.8), kind=kLoop, calls=%fused_computation.19 | loop fusion | flops 73728 | bytes 73728 | tf_op jit(solution)/shard_map/broadcast_in_dim | solution.py:257
  1.5 5.1 %collective-permute-start = (bf16[1,144,128]{2,1,0:T(8,128)(2,1)S(1)}, bf16[1,144,128]{2,1,0:T(8,128)(2,1)S(1)}, u32[]{:S(2)}, u32[]{:S(2)}) collective-permute-start(bf16[1,144,128]{2,1,0:T(8,128)(2,1)S(1)} %maximum_bitcast_fusion), channel_id=1, source_target_pairs={{0,24},{2,26},{4,28},{6,30},{8,16},{10,18},{12,20},{14,22},{16,8},... | collective-permute-start | bytes 110600 | tf_op jit(solution)/shard_map/ppermute | solution.py:241
  6.6 0.0 collective-permute-start.5
  6.6 0.6 collective-permute-start.4
  7.1 0.1 copy.7.cl_ref
  7.2 1.1 %copy.8 = bf16[128,1024]{0,1:T(8,128)(2,1)S(1)} copy(bf16[128,1024]{1,0:T(8,128)(2,1)} %param.6) | data formatting | bytes 524288 | tf_op args[0]
  8.3 0.0 copy-start
  8.4 0.0 copy-start.1
  8.4 0.9 %copy-done = bf16[128,1024]{1,0:T(8,128)(2,1)S(1)} copy-done((bf16[128,1024]{1,0:T(8,128)(2,1)S(1)}, bf16[128,1024]{1,0:T(8,128)(2,1)}, u32[]{:S(2)}) %copy-start) | copy-done | bytes 262168
  9.3 0.1 copy-done.1
  9.4 1.0 %shard_map.55 = (bf16[2,2048,128]{2,1,0:T(8,128)(2,1)S(1)}, bf16[2048,64]{1,0:T(8,128)(2,1)S(1)}) custom-call(bf16[128,1024]{1,0:T(8,128)(2,1)S(1)} %copy-done, bf16[128,1024]{1,0:T(8,128)(2,1)S(1)} %copy-done.1, s32[128,16]{1,0:T(8,128)S(1)} %copy.7.cl_ref), custom_call_target="tpu_custom_call" | custom-call | flops 10000000 | bytes 2000000 | tf_op jit(solution)/shard_map/pallas_call | solution.py:45
  10.4 0.0 collective-permute-done
  10.4 1.0 %collective-permute-done.5 = bf16[1,144,128]{2,1,0:T(8,128)(2,1)S(1)} collective-permute-done((bf16[1,144,128]{2,1,0:T(8,128)(2,1)S(1)}, bf16[1,144,128]{2,1,0:T(8,128)(2,1)S(1)}, u32[]{:S(2)}, u32[]{:S(2)}) %collective-permute-start.5) | collective-permute-done | bytes 36896 | tf_op jit(solution)/shard_map/ppermute | solution.py:241
  11.4 0.0 collective-permute-done.4
  11.4 2.5 %collective-permute-start.6 = (bf16[4,144,128]{2,1,0:T(8,128)(2,1)S(1)}, bf16[4,144,128]{2,1,0:T(8,128)(2,1)S(1)}, u32[]{:S(2)}, u32[]{:S(2)}) collective-permute-start(bf16[4,144,128]{2,1,0:T(8,128)(2,1)S(1)} %pad_maximum_fusion.1.refs_0_), channel_id=1, source_target_pairs={{0,6},{2,4},{4,2},{6,0},{8,14},{10,12},{12,10},{14,8},{16,22},{18,... | collective-permute-start | bytes 442376 | tf_op jit(solution)/shard_map/ppermute | solution.py:241
  14.0 0.5 collective-permute-start.8
  14.5 0.5 collective-permute-start.9
  15.0 0.3 shard_map.56
  15.3 2.9 %collective-permute-done.6.refs_2_ = bf16[4,144,128]{2,1,0:T(8,128)(2,1)S(1)} collective-permute-done((bf16[4,144,128]{2,1,0:T(8,128)(2,1)S(1)}, bf16[4,144,128]{2,1,0:T(8,128)(2,1)S(1)}, u32[]{:S(2)}, u32[]{:S(2)}) %collective-permute-start.6) | collective-permute-done | bytes 147488 | tf_op jit(solution)/shard_map/ppermute | solution.py:241
  18.2 0.0 collective-permute-start.7
  18.2 0.5 collective-permute-start.10
  18.7 1.2 %collective-permute-done.8.refs_0_ = bf16[4,144,128]{2,1,0:T(8,128)(2,1)S(1)} collective-permute-done((bf16[4,144,128]{2,1,0:T(8,128)(2,1)S(1)}, bf16[4,144,128]{2,1,0:T(8,128)(2,1)S(1)}, u32[]{:S(2)}, u32[]{:S(2)}) %collective-permute-start.8) | collective-permute-done | bytes 147488 | tf_op jit(solution)/shard_map/ppermute | solution.py:241
  19.8 0.0 collective-permute-start.11
  19.8 0.0 collective-permute-done.9.refs_1_
  19.8 0.5 collective-permute-start.12
  20.4 1.9 %collective-permute-start.3 = (bf16[2,128,128]{1,2,0:T(8,128)(2,1)S(1)}, bf16[2,128,128]{1,2,0:T(8,128)(2,1)S(1)}, u32[]{:S(2)}, u32[]{:S(2)}) collective-permute-start(bf16[2,128,128]{1,2,0:T(8,128)(2,1)S(1)} %get-tuple-element.55), channel_id=1, source_target_pairs={{0,6},{2,4},{4,2},{6,0},{8,14},{10,12},{12,10},{14,8},{16,22},{18,... | collective-permute-start | bytes 196616 | tf_op jit(solution)/shard_map/ppermute | solution.py:241
  22.3 0.9 %shard_map.57 = (bf16[12,256,128]{2,1,0:T(8,128)(2,1)S(1)}, bf16[12,64,128]{2,1,0:T(8,128)(2,1)S(1)}, bf16[1536,128]{1,0:T(8,128)(2,1)S(1)}) custom-call(bf16[4,144,128]{2,1,0:T(8,128)(2,1)S(1)} %collective-permute-done.8.refs_0_, bf16[4,144,128]{2,1,0:T(8,128)(2,1)S(1)} %collective-permute-done.9.refs_1_, ...), custom_call_target="tpu_custom_call" | custom-call | flops 12000000 | bytes 1200000 | tf_op jit(solution)/shard_map/pallas_call | solution.py:95
  23.1 0.0 collective-permute-done.7.refs_3_
  23.2 1.2 %collective-permute-start.2 = (bf16[2,128,128]{1,2,0:T(8,128)(2,1)S(1)}, bf16[2,128,128]{1,2,0:T(8,128)(2,1)S(1)}, u32[]{:S(2)}, u32[]{:S(2)}) collective-permute-start(bf16[2,128,128]{1,2,0:T(8,128)(2,1)S(1)} %get-tuple-element.56), channel_id=1, source_target_pairs={{0,4},{2,6},{4,0},{6,2},{8,12},{10,14},{12,8},{14,10},{16,20},{18,... | collective-permute-start | bytes 196616 | tf_op jit(solution)/shard_map/ppermute | solution.py:241
  24.3 0.5 collective-permute-start.1
  24.9 1.1 %shard_map.58 = (bf16[16,256,128]{2,1,0:T(8,128)(2,1)S(1)}, bf16[16,64,128]{2,1,0:T(8,128)(2,1)S(1)}, bf16[2048,128]{1,0:T(8,128)(2,1)S(1)}) custom-call(bf16[4,144,128]{2,1,0:T(8,128)(2,1)S(1)} %collective-permute-done.10.refs_0_, bf16[4,144,128]{2,1,0:T(8,128)(2,1)S(1)} %collective-permute-done.11.refs_1_, ...), custom_call_target="tpu_custom_call" | custom-call | flops 16000000 | bytes 1600000 | tf_op jit(solution)/shard_map/pallas_call | solution.py:95
  26.0 25.0 %shard_map.59 = bf16[128,1024]{1,0:T(8,128)(2,1)S(1)} custom-call(bf16[2,2048,128]{2,1,0:T(8,128)(2,1)S(1)} %get-tuple-element.31.lhs, bf16[2048,64]{1,0:T(8,128)(2,1)S(1)} %get-tuple-element.32.grd, bf16[4,256,128]{2,1,0:T(8,128)(2,1)S(1)} %get-tuple-element.37.refs_0_, bf16[4,64,128]{2,1,0:T(8,128)(2,1)S(1)} %get-tuple-element.38.refs_1_, ...), custom_call_target="tpu_custom_call" | custom-call | flops 3221225472 | bytes 10000000 | tf_op jit(solution)/shard_map/pallas_call | solution.py:219
  51.0 1.9 %collective-permute-start.15 = (bf16[128,1024]{1,0:T(8,128)(2,1)S(1)}, bf16[128,1024]{1,0:T(8,128)(2,1)S(1)}, u32[]{:S(2)}, u32[]{:S(2)}) collective-permute-start(bf16[128,1024]{1,0:T(8,128)(2,1)S(1)} %shard_map.59), channel_id=1, source_target_pairs={{0,6},{2,4},{4,2},{6,0},{8,14},{10,12},{12,10},{14,8},{16,22},{18,... | collective-permute-start | bytes 786440 | tf_op jit(solution)/shard_map/ppermute | solution.py:241
  52.9 0.0 collective-permute-start.17
  52.9 0.0 collective-permute-done.3
  52.9 0.5 collective-permute-start.13
  53.4 1.1 %collective-permute-start.14 = (bf16[128,1024]{1,0:T(8,128)(2,1)S(1)}, bf16[128,1024]{1,0:T(8,128)(2,1)S(1)}, u32[]{:S(2)}, u32[]{:S(2)}) collective-permute-start(bf16[128,1024]{1,0:T(8,128)(2,1)S(1)} %shard_map.59), channel_id=1, source_target_pairs={{0,4},{2,6},{4,0},{6,2},{8,12},{10,14},{12,8},{14,10},{16,20},{18,... | collective-permute-start | bytes 786440 | tf_op jit(solution)/shard_map/ppermute | solution.py:241
  54.6 0.0 collective-permute-done.1
  54.6 0.1 collective-permute-start.16
  54.7 6.4 %collective-permute-done.15 = bf16[128,1024]{1,0:T(8,128)(2,1)S(1)} collective-permute-done((bf16[128,1024]{1,0:T(8,128)(2,1)S(1)}, bf16[128,1024]{1,0:T(8,128)(2,1)S(1)}, u32[]{:S(2)}, u32[]{:S(2)}) %collective-permute-start.15) | collective-permute-done | bytes 262176 | tf_op jit(solution)/shard_map/ppermute | solution.py:241
  61.1 0.0 collective-permute-start.20
  61.1 3.8 %collective-permute-done.13 = bf16[128,1024]{1,0:T(8,128)(2,1)S(1)} collective-permute-done((bf16[128,1024]{1,0:T(8,128)(2,1)S(1)}, bf16[128,1024]{1,0:T(8,128)(2,1)S(1)}, u32[]{:S(2)}, u32[]{:S(2)}) %collective-permute-start.13) | collective-permute-done | bytes 262176 | tf_op jit(solution)/shard_map/ppermute | solution.py:241
  64.9 0.0 collective-permute-start.18
  64.9 0.0 collective-permute-done.14
  64.9 0.5 collective-permute-start.19
  65.5 0.0 collective-permute-done.16
  65.5 0.0 collective-permute-done.17
  65.5 0.2 fusion.7
  65.7 0.2 fusion.8
  65.9 0.2 fusion.9
  66.1 0.2 fusion.10
  66.3 0.2 fusion.6
  66.6 0.2 convolution_add_fusion.1
  66.8 0.0 collective-permute-done.19
  66.9 0.2 fusion.3
  67.1 0.2 fusion.2
  67.4 3.5 %collective-permute-start.23 = (bf16[32,1024]{1,0:T(8,128)(2,1)S(1)}, bf16[32,1024]{1,0:T(8,128)(2,1)S(1)}, u32[]{:S(2)}, u32[]{:S(2)}) collective-permute-start(bf16[32,1024]{1,0:T(8,128)(2,1)S(1)} %get-tuple-element.52), channel_id=1, source_target_pairs={{0,24},{2,26},{4,28},{6,30},{8,16},{10,18},{12,20},{14,22},{16,8},... | collective-permute-start | bytes 196616 | tf_op jit(solution)/shard_map/ppermute | solution.py:241
  70.9 0.0 collective-permute-start.22
  70.9 1.0 %collective-permute-start.21 = (bf16[32,1024]{1,0:T(8,128)(2,1)S(1)}, bf16[32,1024]{1,0:T(8,128)(2,1)S(1)}, u32[]{:S(2)}, u32[]{:S(2)}) collective-permute-start(bf16[32,1024]{1,0:T(8,128)(2,1)S(1)} %get-tuple-element.51), channel_id=1, source_target_pairs={{0,8},{2,10},{4,12},{6,14},{8,0},{10,2},{12,4},{14,6},{16,24},{18,... | collective-permute-start | bytes 196616 | tf_op jit(solution)/shard_map/ppermute | solution.py:241
  71.8 2.1 %collective-permute-done.23 = bf16[32,1024]{1,0:T(8,128)(2,1)S(1)} collective-permute-done((bf16[32,1024]{1,0:T(8,128)(2,1)S(1)}, bf16[32,1024]{1,0:T(8,128)(2,1)S(1)}, u32[]{:S(2)}, u32[]{:S(2)}) %collective-permute-start.23) | collective-permute-done | bytes 65568 | tf_op jit(solution)/shard_map/ppermute | solution.py:241
  74.0 2.7 %collective-permute-done.22 = bf16[32,1024]{1,0:T(8,128)(2,1)S(1)} collective-permute-done((bf16[32,1024]{1,0:T(8,128)(2,1)S(1)}, bf16[32,1024]{1,0:T(8,128)(2,1)S(1)}, u32[]{:S(2)}, u32[]{:S(2)}) %collective-permute-start.22) | collective-permute-done | bytes 65568 | tf_op jit(solution)/shard_map/ppermute | solution.py:241
  76.7 0.0 collective-permute-done.21
  76.7 0.7 fusion.5
  (15 shorter events, 0.2 us)
Async XLA Ops:
  0.7 6.4 %copy-start.2 = (s32[128,16]{0,1:T(8,128)S(1)}, s32[128,16]{0,1:T(8,128)}, u32[]{:S(2)}) copy-start(s32[128,16]{0,1:T(8,128)} %param.10) | copy-start | bytes 24580
  1.5 8.9 %collective-permute-start = (bf16[1,144,128]{2,1,0:T(8,128)(2,1)S(1)}, bf16[1,144,128]{2,1,0:T(8,128)(2,1)S(1)}, u32[]{:S(2)}, u32[]{:S(2)}) collective-permute-start(bf16[1,144,128]{2,1,0:T(8,128)(2,1)S(1)} %maximum_bitcast_fusion), channel_id=1, source_target_pairs={{0,24},{2,26},{4,28},{6,30},{8,16},{10,18},{12,20},{14,22},{16,8},... | collective-permute-start | bytes 110600 | tf_op jit(solution)/shard_map/ppermute | solution.py:241
  6.6 4.9 %collective-permute-start.5 = (bf16[1,144,128]{2,1,0:T(8,128)(2,1)S(1)}, bf16[1,144,128]{2,1,0:T(8,128)(2,1)S(1)}, u32[]{:S(2)}, u32[]{:S(2)}) collective-permute-start(bf16[1,144,128]{2,1,0:T(8,128)(2,1)S(1)} %maximum_bitcast_fusion), channel_id=1, source_target_pairs={{0,16},{2,18},{4,20},{6,22},{8,24},{10,26},{12,28},{14,30},{16,0},... | collective-permute-start | bytes 110600 | tf_op jit(solution)/shard_map/ppermute | solution.py:241
  6.6 4.9 %collective-permute-start.4 = (bf16[1,144,128]{2,1,0:T(8,128)(2,1)S(1)}, bf16[1,144,128]{2,1,0:T(8,128)(2,1)S(1)}, u32[]{:S(2)}, u32[]{:S(2)}) collective-permute-start(bf16[1,144,128]{2,1,0:T(8,128)(2,1)S(1)} %maximum_bitcast_fusion), channel_id=1, source_target_pairs={{0,8},{2,10},{4,12},{6,14},{8,0},{10,2},{12,4},{14,6},{16,24},{18,... | collective-permute-start | bytes 110600 | tf_op jit(solution)/shard_map/ppermute | solution.py:241
  8.3 1.0 %copy-start = (bf16[128,1024]{1,0:T(8,128)(2,1)S(1)}, bf16[128,1024]{1,0:T(8,128)(2,1)}, u32[]{:S(2)}) copy-start(bf16[128,1024]{1,0:T(8,128)(2,1)} %q_ref.1) | copy-start | bytes 786436
  8.4 1.0 %copy-start.1 = (bf16[128,1024]{1,0:T(8,128)(2,1)S(1)}, bf16[128,1024]{1,0:T(8,128)(2,1)}, u32[]{:S(2)}) copy-start(bf16[128,1024]{1,0:T(8,128)(2,1)} %g_ref.1) | copy-start | bytes 786436
  11.4 6.7 %collective-permute-start.6 = (bf16[4,144,128]{2,1,0:T(8,128)(2,1)S(1)}, bf16[4,144,128]{2,1,0:T(8,128)(2,1)S(1)}, u32[]{:S(2)}, u32[]{:S(2)}) collective-permute-start(bf16[4,144,128]{2,1,0:T(8,128)(2,1)S(1)} %pad_maximum_fusion.1.refs_0_), channel_id=1, source_target_pairs={{0,6},{2,4},{4,2},{6,0},{8,14},{10,12},{12,10},{14,8},{16,22},{18,... | collective-permute-start | bytes 442376 | tf_op jit(solution)/shard_map/ppermute | solution.py:241
  14.0 5.9 %collective-permute-start.8 = (bf16[4,144,128]{2,1,0:T(8,128)(2,1)S(1)}, bf16[4,144,128]{2,1,0:T(8,128)(2,1)S(1)}, u32[]{:S(2)}, u32[]{:S(2)}) collective-permute-start(bf16[4,144,128]{2,1,0:T(8,128)(2,1)S(1)} %pad_maximum_fusion.1.refs_0_), channel_id=1, source_target_pairs={{0,2},{2,0},{4,6},{6,4},{8,10},{10,8},{12,14},{14,12},{16,18},{18,... | collective-permute-start | bytes 442376 | tf_op jit(solution)/shard_map/ppermute | solution.py:241
  14.5 5.3 %collective-permute-start.9 = (bf16[4,144,128]{2,1,0:T(8,128)(2,1)S(1)}, bf16[4,144,128]{2,1,0:T(8,128)(2,1)S(1)}, u32[]{:S(2)}, u32[]{:S(2)}) collective-permute-start(bf16[4,144,128]{2,1,0:T(8,128)(2,1)S(1)} %pad_maximum_fusion.1.refs_0_), channel_id=1, source_target_pairs={{0,4},{2,6},{4,0},{6,2},{8,12},{10,14},{12,8},{14,10},{16,20},{18,... | collective-permute-start | bytes 442376 | tf_op jit(solution)/shard_map/ppermute | solution.py:241
  18.2 5.0 %collective-permute-start.7 = (bf16[4,144,128]{2,1,0:T(8,128)(2,1)S(1)}, bf16[4,144,128]{2,1,0:T(8,128)(2,1)S(1)}, u32[]{:S(2)}, u32[]{:S(2)}) collective-permute-start(bf16[4,144,128]{2,1,0:T(8,128)(2,1)S(1)} %collective-permute-done.6.refs_2_), channel_id=1, source_target_pairs={{0,1},{1,0},{2,3},{3,2},{4,5},{5,4},{6,7},{7,6},{8,9},{9,8},{10,11... | collective-permute-start | bytes 442376 | tf_op jit(solution)/shard_map/ppermute | solution.py:241
  18.2 6.2 %collective-permute-start.10 = (bf16[4,144,128]{2,1,0:T(8,128)(2,1)S(1)}, bf16[4,144,128]{2,1,0:T(8,128)(2,1)S(1)}, u32[]{:S(2)}, u32[]{:S(2)}) collective-permute-start(bf16[4,144,128]{2,1,0:T(8,128)(2,1)S(1)} %pad_maximum_fusion.1.refs_0_), channel_id=1, source_target_pairs={{0,1},{1,0},{2,3},{3,2},{4,5},{5,4},{6,7},{7,6},{8,9},{9,8},{10,11... | collective-permute-start | bytes 442376 | tf_op jit(solution)/shard_map/ppermute | solution.py:241
  19.8 5.1 %collective-permute-start.11 = (bf16[4,144,128]{2,1,0:T(8,128)(2,1)S(1)}, bf16[4,144,128]{2,1,0:T(8,128)(2,1)S(1)}, u32[]{:S(2)}, u32[]{:S(2)}) collective-permute-start(bf16[4,144,128]{2,1,0:T(8,128)(2,1)S(1)} %collective-permute-done.8.refs_0_), channel_id=1, source_target_pairs={{0,1},{1,0},{2,3},{3,2},{4,5},{5,4},{6,7},{7,6},{8,9},{9,8},{10,11... | collective-permute-start | bytes 442376 | tf_op jit(solution)/shard_map/ppermute | solution.py:241
  19.8 5.1 %collective-permute-start.12 = (bf16[4,144,128]{2,1,0:T(8,128)(2,1)S(1)}, bf16[4,144,128]{2,1,0:T(8,128)(2,1)S(1)}, u32[]{:S(2)}, u32[]{:S(2)}) collective-permute-start(bf16[4,144,128]{2,1,0:T(8,128)(2,1)S(1)} %collective-permute-done.9.refs_1_), channel_id=1, source_target_pairs={{0,1},{1,0},{2,3},{3,2},{4,5},{5,4},{6,7},{7,6},{8,9},{9,8},{10,11... | collective-permute-start | bytes 442376 | tf_op jit(solution)/shard_map/ppermute | solution.py:241
  20.4 32.5 %collective-permute-start.3 = (bf16[2,128,128]{1,2,0:T(8,128)(2,1)S(1)}, bf16[2,128,128]{1,2,0:T(8,128)(2,1)S(1)}, u32[]{:S(2)}, u32[]{:S(2)}) collective-permute-start(bf16[2,128,128]{1,2,0:T(8,128)(2,1)S(1)} %get-tuple-element.55), channel_id=1, source_target_pairs={{0,6},{2,4},{4,2},{6,0},{8,14},{10,12},{12,10},{14,8},{16,22},{18,... | collective-permute-start | bytes 196616 | tf_op jit(solution)/shard_map/ppermute | solution.py:241
  23.2 30.3 %collective-permute-start.2 = (bf16[2,128,128]{1,2,0:T(8,128)(2,1)S(1)}, bf16[2,128,128]{1,2,0:T(8,128)(2,1)S(1)}, u32[]{:S(2)}, u32[]{:S(2)}) collective-permute-start(bf16[2,128,128]{1,2,0:T(8,128)(2,1)S(1)} %get-tuple-element.56), channel_id=1, source_target_pairs={{0,4},{2,6},{4,0},{6,2},{8,12},{10,14},{12,8},{14,10},{16,20},{18,... | collective-permute-start | bytes 196616 | tf_op jit(solution)/shard_map/ppermute | solution.py:241
  24.3 30.2 %collective-permute-start.1 = (bf16[2,128,128]{1,2,0:T(8,128)(2,1)S(1)}, bf16[2,128,128]{1,2,0:T(8,128)(2,1)S(1)}, u32[]{:S(2)}, u32[]{:S(2)}) collective-permute-start(bf16[2,128,128]{1,2,0:T(8,128)(2,1)S(1)} %get-tuple-element.57), channel_id=1, source_target_pairs={{0,2},{2,0},{4,6},{6,4},{8,10},{10,8},{12,14},{14,12},{16,18},{18,... | collective-permute-start | bytes 196616 | tf_op jit(solution)/shard_map/ppermute | solution.py:241
  51.0 10.1 %collective-permute-start.15 = (bf16[128,1024]{1,0:T(8,128)(2,1)S(1)}, bf16[128,1024]{1,0:T(8,128)(2,1)S(1)}, u32[]{:S(2)}, u32[]{:S(2)}) collective-permute-start(bf16[128,1024]{1,0:T(8,128)(2,1)S(1)} %shard_map.59), channel_id=1, source_target_pairs={{0,6},{2,4},{4,2},{6,0},{8,14},{10,12},{12,10},{14,8},{16,22},{18,... | collective-permute-start | bytes 786440 | tf_op jit(solution)/shard_map/ppermute | solution.py:241
  52.9 12.6 %collective-permute-start.17 = (bf16[128,1024]{1,0:T(8,128)(2,1)S(1)}, bf16[128,1024]{1,0:T(8,128)(2,1)S(1)}, u32[]{:S(2)}, u32[]{:S(2)}) collective-permute-start(bf16[128,1024]{1,0:T(8,128)(2,1)S(1)} %shard_map.59), channel_id=1, source_target_pairs={{0,1},{1,0},{2,3},{3,2},{4,5},{5,4},{6,7},{7,6},{8,9},{9,8},{10,11... | collective-permute-start | bytes 786440 | tf_op jit(solution)/shard_map/ppermute | solution.py:241
  52.9 12.0 %collective-permute-start.13 = (bf16[128,1024]{1,0:T(8,128)(2,1)S(1)}, bf16[128,1024]{1,0:T(8,128)(2,1)S(1)}, u32[]{:S(2)}, u32[]{:S(2)}) collective-permute-start(bf16[128,1024]{1,0:T(8,128)(2,1)S(1)} %shard_map.59), channel_id=1, source_target_pairs={{0,2},{2,0},{4,6},{6,4},{8,10},{10,8},{12,14},{14,12},{16,18},{18,... | collective-permute-start | bytes 786440 | tf_op jit(solution)/shard_map/ppermute | solution.py:241
  53.4 11.5 %collective-permute-start.14 = (bf16[128,1024]{1,0:T(8,128)(2,1)S(1)}, bf16[128,1024]{1,0:T(8,128)(2,1)S(1)}, u32[]{:S(2)}, u32[]{:S(2)}) collective-permute-start(bf16[128,1024]{1,0:T(8,128)(2,1)S(1)} %shard_map.59), channel_id=1, source_target_pairs={{0,4},{2,6},{4,0},{6,2},{8,12},{10,14},{12,8},{14,10},{16,20},{18,... | collective-permute-start | bytes 786440 | tf_op jit(solution)/shard_map/ppermute | solution.py:241
  54.6 10.8 %collective-permute-start.16 = (bf16[4,128,128]{1,2,0:T(8,128)(2,1)S(1)}, bf16[4,128,128]{1,2,0:T(8,128)(2,1)S(1)}, u32[]{:S(2)}, u32[]{:S(2)}) collective-permute-start(bf16[4,128,128]{1,2,0:T(8,128)(2,1)S(1)} %dynamic-slice_bitcast_fusion), channel_id=1, source_target_pairs={{0,1},{1,0},{2,3},{3,2},{4,5},{5,4},{6,7},{7,6},{8,9},{9,8},{10,11... | collective-permute-start | bytes 393224 | tf_op jit(solution)/shard_map/ppermute | solution.py:241
  61.1 5.2 %collective-permute-start.20 = (bf16[128,1024]{1,0:T(8,128)(2,1)S(1)}, bf16[128,1024]{1,0:T(8,128)(2,1)S(1)}, u32[]{:S(2)}, u32[]{:S(2)}) collective-permute-start(bf16[128,1024]{1,0:T(8,128)(2,1)S(1)} %collective-permute-done.15), channel_id=1, source_target_pairs={{0,1},{1,0},{2,3},{3,2},{4,5},{5,4},{6,7},{7,6},{8,9},{9,8},{10,11... | collective-permute-start | bytes 786440 | tf_op jit(solution)/shard_map/ppermute | solution.py:241
  64.9 1.6 %collective-permute-start.18 = (bf16[128,1024]{1,0:T(8,128)(2,1)S(1)}, bf16[128,1024]{1,0:T(8,128)(2,1)S(1)}, u32[]{:S(2)}, u32[]{:S(2)}) collective-permute-start(bf16[128,1024]{1,0:T(8,128)(2,1)S(1)} %collective-permute-done.13), channel_id=1, source_target_pairs={{0,1},{1,0},{2,3},{3,2},{4,5},{5,4},{6,7},{7,6},{8,9},{9,8},{10,11... | collective-permute-start | bytes 786440 | tf_op jit(solution)/shard_map/ppermute | solution.py:241
  64.9 1.9 %collective-permute-start.19 = (bf16[128,1024]{1,0:T(8,128)(2,1)S(1)}, bf16[128,1024]{1,0:T(8,128)(2,1)S(1)}, u32[]{:S(2)}, u32[]{:S(2)}) collective-permute-start(bf16[128,1024]{1,0:T(8,128)(2,1)S(1)} %collective-permute-done.14), channel_id=1, source_target_pairs={{0,1},{1,0},{2,3},{3,2},{4,5},{5,4},{6,7},{7,6},{8,9},{9,8},{10,11... | collective-permute-start | bytes 786440 | tf_op jit(solution)/shard_map/ppermute | solution.py:241
  67.4 6.6 %collective-permute-start.23 = (bf16[32,1024]{1,0:T(8,128)(2,1)S(1)}, bf16[32,1024]{1,0:T(8,128)(2,1)S(1)}, u32[]{:S(2)}, u32[]{:S(2)}) collective-permute-start(bf16[32,1024]{1,0:T(8,128)(2,1)S(1)} %get-tuple-element.52), channel_id=1, source_target_pairs={{0,24},{2,26},{4,28},{6,30},{8,16},{10,18},{12,20},{14,22},{16,8},... | collective-permute-start | bytes 196616 | tf_op jit(solution)/shard_map/ppermute | solution.py:241
  70.9 5.8 %collective-permute-start.22 = (bf16[32,1024]{1,0:T(8,128)(2,1)S(1)}, bf16[32,1024]{1,0:T(8,128)(2,1)S(1)}, u32[]{:S(2)}, u32[]{:S(2)}) collective-permute-start(bf16[32,1024]{1,0:T(8,128)(2,1)S(1)} %get-tuple-element.53), channel_id=1, source_target_pairs={{0,16},{2,18},{4,20},{6,22},{8,24},{10,26},{12,28},{14,30},{16,0},... | collective-permute-start | bytes 196616 | tf_op jit(solution)/shard_map/ppermute | solution.py:241
  70.9 5.8 %collective-permute-start.21 = (bf16[32,1024]{1,0:T(8,128)(2,1)S(1)}, bf16[32,1024]{1,0:T(8,128)(2,1)S(1)}, u32[]{:S(2)}, u32[]{:S(2)}) collective-permute-start(bf16[32,1024]{1,0:T(8,128)(2,1)S(1)} %get-tuple-element.51), channel_id=1, source_target_pairs={{0,8},{2,10},{4,12},{6,14},{8,0},{10,2},{12,4},{14,6},{16,24},{18,... | collective-permute-start | bytes 196616 | tf_op jit(solution)/shard_map/ppermute | solution.py:241

commit v5 on v4

--- a/solution.py
+++ b/solution.py
@@ -12,80 +12,84 @@
 SCALE = HD ** (-0.5)
 LOG2E = 1.4426950408889634
 TILE = 512
-LAG = 2
-GAP = 4
-
-
-def prepare_rows_kernel(q_ref, g_ref, cl_ref, lhs, grd):
+LAG = 1
+LATE = 0.5
+UNITS = 8
+
+
+def prepare_rows_kernel(q_ref, g_ref, cl_ref, left, grd):
     tok, width = q_ref.shape
     lanes = 2 * HD
-    lane = lax.broadcasted_iota(jnp.int32, (tok, lanes), 1)
-    low = lane < HD
-    head = lax.broadcasted_iota(jnp.int32, (tok, H), 1)
-    for h in range(width // HD):
-        at = slice(h * tok, (h + 1) * tok)
-        two = slice((h // 2) * lanes, (h // 2 + 1) * lanes)
-        q2 = q_ref[:, two].astype(jnp.float32) * SCALE
-        g2 = g_ref[:, two].astype(jnp.float32)
-        if h % 2:
-            q2 = pltpu.roll(q2, HD, 1)
-            g2 = pltpu.roll(g2, HD, 1)
-        mine = jnp.sum(jnp.where(head == h, cl_ref[...], 0), axis=1, keepdims=True)
-        same = jnp.where(mine >= HD, mine - HD, mine)
-        first = jnp.where(lane - HD == mine, 1.0, 0.0)
-        second = jnp.where(lane == jnp.where(low, mine - HD, same + HD), 1.0, 0.0)
-        lhs[0, at, :] = jnp.where(low, q2, first).astype(jnp.bfloat16)
-        lhs[1, at, :] = second.astype(jnp.bfloat16)
-        grd[at, :] = g2[:, :HD].astype(jnp.bfloat16)
+    ids = lax.broadcasted_iota(jnp.int32, (lanes, tok), 0)
+    for i in range(width // lanes):
+        two = slice(i * lanes, (i + 1) * lanes)
+        qt = (q_ref[:, two].astype(jnp.float32) * SCALE).T.astype(jnp.bfloat16)
+        gt = g_ref[:, two].astype(jnp.float32).T.astype(jnp.bfloat16)
+        for odd in range(2):
+            h = 2 * i + odd
+            half = slice(odd * HD, (odd + 1) * HD)
+            mine = cl_ref[h : h + 1, :]
+            hot = jnp.where(ids == mine, 1.0, 0.0).astype(jnp.bfloat16)
+            same = jnp.where(ids[:HD] == jnp.bitwise_and(mine, HD - 1), 1.0, 0.0)
+            left[h, 0:HD, :] = qt[half]
+            left[h, HD : HD + lanes, :] = hot
+            left[h, HD + lanes :, :] = same.astype(jnp.bfloat16)
+            grd[h, 0:HD, :] = jnp.zeros((HD, tok), jnp.bfloat16)
+            grd[h, HD:, :] = gt[half]
 
 
 def prepare_rows(queries, out_grad, cluster_of):
     tok, width = queries.shape
-    rows = width // HD * tok
+    heads = width // HD
     return pl.pallas_call(
         prepare_rows_kernel,
         out_shape=(
-            jax.ShapeDtypeStruct((2, rows, 2 * HD), jnp.bfloat16),
-            jax.ShapeDtypeStruct((rows, HD), jnp.bfloat16),
+            jax.ShapeDtypeStruct((heads, 4 * HD, tok), jnp.bfloat16),
+            jax.ShapeDtypeStruct((heads, 2 * HD, tok), jnp.bfloat16),
         ),
         compiler_params=pltpu.CompilerParams(vmem_limit_bytes=8 * 1024 * 1024),
         cost_estimate=pl.CostEstimate(flops=10**7, bytes_accessed=2 * 10**6, transcendentals=0),
-    )(queries, out_grad, cluster_of)
+    )(queries, out_grad, cluster_of.T)
 
 
 def prepare_keys_kernel(*refs):
     kv_refs = refs[:-3]
-    rhs, val, key = refs[-3:]
-    tok = rhs.shape[2]
+    wide, key, turned = refs[-3:]
+    tok = turned.shape[2]
+    lanes = 2 * HD
     quarter = HD // 2
     ids = lax.broadcasted_iota(jnp.int32, (quarter, tok), 0)
+    low = lax.broadcasted_iota(jnp.int32, (tok, lanes), 1) < HD
     at = 0
     for kv_ref in kv_refs:
         for j in range(kv_ref.shape[0]):
+            rows = slice(at * tok, (at + 1) * tok)
             kv = kv_ref[j, 0:tok, :]
-            turned = kv.astype(jnp.float32).T.astype(jnp.bfloat16)
-            rhs[at, 0:HD, :] = turned[:HD]
-            val[at, :, :] = turned[HD:]
-            key[at * tok : (at + 1) * tok, :] = kv
+            kv32 = kv.astype(jnp.float32)
+            key[rows, :] = kv
+            turned[at, :, :] = kv32.T[:HD].astype(jnp.bfloat16)
             cl = kv_ref[j, tok : tok + H, :].astype(jnp.float32).astype(jnp.int32)
             group = jnp.bitwise_and(cl, quarter - 1)
             one = jnp.left_shift(1, 8 * jnp.right_shift(cl, 5))
             packed = jnp.zeros((quarter, tok), jnp.int32)
             for h in range(H):
                 packed += jnp.where(group[h : h + 1, :] == ids, one[h : h + 1, :], 0)
-            res = []
+            res, high = [], []
             for part in range(4):
                 count = jnp.bitwise_and(jnp.right_shift(packed, 8 * part), 255)
                 live = count > 0
                 log = jnp.log(count.astype(jnp.float32))
-                hi = jnp.where(live, log, -1e30).astype(jnp.bfloat16)
-                rhs[at, HD + part * quarter : HD + (part + 1) * quarter, :] = hi
-                res.append(jnp.where(live, log - hi.astype(jnp.float32), 0.0))
+                hi = jnp.where(live, log, -1e30).astype(jnp.bfloat16).astype(jnp.float32)
+                high.append(hi)
+                res.append(jnp.where(live, log - hi, 0.0))
+            small = []
             for part in range(2):
                 a, b = res[part], res[part + 2]
-                both = jnp.where(a == 0.0, b, jnp.where(b == 0.0, a, 0.5 * (a + b)))
-                start = 3 * HD + part * quarter
-                rhs[at, start : start + quarter, :] = both.astype(jnp.bfloat16)
+                small.append(jnp.where(a == 0.0, b, jnp.where(b == 0.0, a, 0.5 * (a + b))))
+            one = jnp.concatenate([high[0], high[1], high[0], high[1]], axis=0).T
+            two = jnp.concatenate([high[2], high[3], small[0], small[1]], axis=0).T
+            wide[0, rows, :] = jnp.where(low, kv32, one).astype(jnp.bfloat16)
+            wide[1, rows, :] = two.astype(jnp.bfloat16)
             at += 1
 
 
@@ -95,9 +99,9 @@
     return pl.pallas_call(
         prepare_keys_kernel,
         out_shape=(
-            jax.ShapeDtypeStruct((blocks, 4 * HD, tok), jnp.bfloat16),
+            jax.ShapeDtypeStruct((2, blocks * tok, 2 * HD), jnp.bfloat16),
+            jax.ShapeDtypeStruct((blocks * tok, 2 * HD), jnp.bfloat16),
             jax.ShapeDtypeStruct((blocks, HD, tok), jnp.bfloat16),
-            jax.ShapeDtypeStruct((blocks * tok, 2 * HD), jnp.bfloat16),
         ),
         compiler_params=pltpu.CompilerParams(vmem_limit_bytes=8 * 1024 * 1024),
         cost_estimate=pl.CostEstimate(
@@ -106,96 +110,109 @@
     )(*gathered)
 
 
-def attend_kernel(lhs, grd, *refs):
-    count = (len(refs) - 9) // 3
+def attend_kernel(left, grd, *refs):
+    count = (len(refs) - 10) // 3
     groups = [refs[3 * i : 3 * i + 3] for i in range(count)]
-    out_ref, sc0, sc1, pg0, pg1, ds0, ds1, acc, tot = refs[3 * count :]
-    sc, pg, ds = (sc0, sc1), (pg0, pg1), (ds0, ds1)
+    out_ref, sc0, sc1, pg0, pg1, ds0, ds1, tp0, tp1, acc = refs[3 * count :]
+    sc, pg, ds, tp = (sc0, sc1), (pg0, pg1), (ds0, ds1), (tp0, tp1)
     lanes = 2 * HD
     tok = out_ref.shape[0]
-    rows = sc0.shape[0]
-    per = TILE // lanes
-    places = [(g, j) for g, group in enumerate(groups) for j in range(group[0].shape[0] // per)]
+    rows = sc0.shape[1]
+    per = TILE // tok
+    places = [(g, j) for g, group in enumerate(groups) for j in range(group[2].shape[0] // per)]
     tiles = len(places)
-    total = tiles * TILE
-    steps = out_ref.shape[1] // HD * tok // rows
-    block = rows // tiles
-    chunks = [slice(c * lanes, (c + 1) * lanes) for c in range(total // lanes)]
-
-    def gated(x, gate):
+    steps = out_ref.shape[1] // lanes
+    unit = TILE // UNITS
+    spread = (unit // 8, 8, rows)
+
+    def tied(x, gate):
         if gate is None:
             return x
         tie = jnp.tile((gate * 0.0).astype(x.dtype), (1, x.shape[1] // gate.shape[1]))
-        pieces = []
-        for r in range(0, x.shape[0], 2 * lanes):
-            pieces += [x[r : r + 16] + tie, x[r + 16 : r + 2 * lanes]]
-        return jnp.concatenate(pieces, axis=0)
-
-    def score(step, slot, t, gate=None):
+        return jnp.concatenate([x[0:16] + tie, x[16:]], axis=0)
+
+    def score(step, slot, t, gate):
         g, j = places[t]
-        at = pl.ds(pl.multiple_of(step * rows, rows), rows)
-        span = range(j * per, (j + 1) * per)
-        right = jnp.concatenate([groups[g][0][b] for b in span], axis=1)
-        left = jnp.concatenate([lhs[0, at, :], lhs[1, at, :]], axis=1)
-        cols = slice(t * TILE, (t + 1) * TILE)
-        sc[slot][:, cols] = jnp.dot(left, gated(right, gate), preferred_element_type=jnp.float32)
-        right = jnp.concatenate([groups[g][1][b] for b in span], axis=1)
-        pg[slot][:, cols] = jnp.dot(
-            grd[at, :], gated(right, gate), preferred_element_type=jnp.float32
+        span = slice(j * TILE, (j + 1) * TILE)
+        at = slice(t * TILE, (t + 1) * TILE)
+        right = jnp.concatenate([left[2 * step], left[2 * step + 1]], axis=1)
+        wide = jnp.concatenate([groups[g][0][0, span, :], groups[g][0][1, span, :]], axis=1)
+        s = jnp.dot(wide, tied(right, gate), preferred_element_type=jnp.float32)
+        sc[slot][at, :] = s
+        top = jnp.max(s.reshape(TILE // 8, 8, rows), axis=0)
+        tp[slot][...] = top if t == 0 else jnp.maximum(tp[slot][...], top)
+        right = jnp.concatenate([grd[2 * step], grd[2 * step + 1]], axis=1)
+        pg[slot][at, :] = jnp.dot(
+            groups[g][1][span, :], tied(right, gate), preferred_element_type=jnp.float32
         )
 
-    def soften(slot, t):
-        at = slice(t * block, (t + 1) * block)
-        top = sc[slot][at, chunks[0]]
-        for c in chunks[1:]:
-            top = jnp.maximum(top, sc[slot][at, c])
-        top = jnp.broadcast_to(jnp.max(top, axis=1, keepdims=True), (block, lanes))
-        denom = jnp.zeros((block, lanes), jnp.float32)
-        dots = jnp.zeros((block, lanes), jnp.float32)
-        for c in chunks:
-            w = jnp.exp(sc[slot][at, c] - top)
-            sc[slot][at, c] = w
-            denom += w
-            dots += w * pg[slot][at, c]
-        denom = jnp.sum(denom, axis=1, keepdims=True)
-        inv = jnp.broadcast_to(SCALE / denom, (block, lanes))
-        dot = jnp.broadcast_to(jnp.sum(dots, axis=1, keepdims=True) / denom, (block, lanes))
-        gate = None
-        for i, c in enumerate(chunks):
-            d = (sc[slot][at, c] * inv) * (pg[slot][at, c] - dot)
-            ds[slot][i, at, :] = d.astype(jnp.bfloat16)
-            if i % GAP == GAP - 1:
-                gate = d[0:16, :] if gate is None else gate + d[0:16, :]
-        return gate
-
-    def collect(slot, t, gate=None):
+    def collect(slot, t, gate):
         g, j = places[t]
-        left = jnp.concatenate([ds[slot][t * per + b] for b in range(per)], axis=1)
-        right = gated(groups[g][2][j * TILE : (j + 1) * TILE, :], gate)
-        add = jnp.dot(left, right, preferred_element_type=jnp.float32)
+        at = slice(t * TILE, (t + 1) * TILE)
+        turned = jnp.concatenate([groups[g][2][j * per + b] for b in range(per)], axis=1)
+        right = jnp.concatenate([ds[slot][0, at, :], ds[slot][1, at, :]], axis=1)
+        add = jnp.dot(turned, tied(right, gate), preferred_element_type=jnp.float32)
         acc[...] = add if t == 0 else acc[...] + add
 
+    def weigh(slot, u, top):
+        at = slice(u * unit, (u + 1) * unit)
+        w = jnp.exp(sc[slot][at, :].reshape(spread) - top)
+        sc[slot][at, :] = w.reshape(unit, rows)
+        wp = w * pg[slot][at, :].reshape(spread)
+        return jnp.sum(w, axis=0), jnp.sum(wp, axis=0)
+
+    def differ(slot, u, inv, dot):
+        at = slice(u * unit, (u + 1) * unit)
+        w = sc[slot][at, :].reshape(spread)
+        d = (w * inv) * (pg[slot][at, :].reshape(spread) - dot)
+        d = d.reshape(unit, rows)
+        low = d.astype(jnp.bfloat16)
+        for b in range(rows // lanes):
+            ds[slot][b, at, :] = low[:, b * lanes : (b + 1) * lanes]
+        return d[0:8, 0:lanes]
+
     def finish(step):
-        low = lax.broadcasted_iota(jnp.int32, (tok, lanes), 1) < HD
-        for j in range(rows // (2 * tok)):
-            even = acc[2 * j * tok : (2 * j + 1) * tok, :]
-            odd = pltpu.roll(acc[(2 * j + 1) * tok : (2 * j + 2) * tok, :], HD, 1)
-            where = pl.multiple_of((step * (rows // (2 * tok)) + j) * lanes, lanes)
-            out_ref[:, pl.ds(where, lanes)] = jnp.where(low, even, odd).astype(jnp.bfloat16)
+        both = jnp.concatenate([acc[:, b * lanes : (b + 1) * lanes] for b in range(2)], axis=0)
+        where = pl.multiple_of(step * lanes, lanes)
+        out_ref[:, pl.ds(where, lanes)] = both.T.astype(jnp.bfloat16)
 
     def stage(step, slot, following):
-        gates = [None] * LAG
+        units = tiles * UNITS
+        work = [("w", u) for u in range(units)] + [("d", u) for u in range(units)]
+        cost = [6.0 if kind == "w" else 4.0 for kind, _ in work]
+        top = jnp.broadcast_to(jnp.max(tp[slot][...], axis=0, keepdims=True), (8, rows))[None]
+        denom = jnp.zeros((8, rows), jnp.float32)
+        dots = jnp.zeros((8, rows), jnp.float32)
+        inv = dot = None
+        gates, done, at = [None] * LAG, 0.0, 0
         for t in range(tiles):
             score(following, 1 - slot, t, gates[t])
             collect(1 - slot, t, gates[t])
-            gates.append(soften(slot, t))
+            gate = None
+            while at < len(work) and (t + 1 == tiles or done < sum(cost) * (t + 1) / (tiles + LATE)):
+                kind, u = work[at]
+                if kind == "w":
+                    a, b = weigh(slot, u, top)
+                    denom, dots = denom + a, dots + b
+                    gate = denom[:, :lanes]
+                else:
+                    if inv is None:
+                        whole = jnp.sum(denom, axis=0, keepdims=True)
+                        dot = jnp.sum(dots, axis=0, keepdims=True) / whole
+                        inv = jnp.broadcast_to(SCALE / whole, (8, rows))[None]
+                        dot = jnp.broadcast_to(dot, (8, rows))[None]
+                    one = differ(slot, u, inv, dot)
+                    gate = one if gate is None else gate + one
+                done += cost[at]
+                at += 1
+            gates.append(jnp.concatenate([gate, gate], axis=0))
 
         @pl.when(step > 0)
         def _():
             finish(step - 1)
 
     for t in range(tiles):
-        score(0, 0, t)
+        score(0, 0, t, None)
 
     def body(i, _):
         stage(2 * i, 0, 2 * i + 1)
@@ -204,26 +221,27 @@
 
     lax.fori_loop(0, steps // 2, body, 0)
     for t in range(tiles):
-        collect(1, t)
+        collect(1, t, None)
     finish(steps - 1)
 
 
-def attend(left, groups, tok):
-    lhs, grd = left
-    heads = grd.shape[0] // tok
-    total = sum(g[2].shape[0] for g in groups)
+def attend(rows_of, groups, tok):
+    left, grd = rows_of
+    heads = left.shape[0]
+    total = sum(g[1].shape[0] for g in groups)
     lanes = 2 * HD
     rows = 2 * tok
-    operands = [lhs, grd] + [x for g in groups for x in g]
-    work = grd.shape[0] * total
+    operands = [left, grd] + [x for g in groups for x in g]
+    work = heads * tok * total
     return pl.pallas_call(
         attend_kernel,
         in_specs=[pl.BlockSpec(memory_space=pltpu.VMEM)] * len(operands),
         out_specs=pl.BlockSpec(memory_space=pltpu.VMEM),
         out_shape=jax.ShapeDtypeStruct((tok, heads * HD), jnp.bfloat16),
-        scratch_shapes=[pltpu.VMEM((rows, total), jnp.float32)] * 4
-        + [pltpu.VMEM((total // lanes, rows, lanes), jnp.bfloat16)] * 2
-        + [pltpu.VMEM((rows, lanes), jnp.float32)] * 2,
+        scratch_shapes=[pltpu.VMEM((total, rows), jnp.float32)] * 4
+        + [pltpu.VMEM((rows // lanes, total, lanes), jnp.bfloat16)] * 2
+        + [pltpu.VMEM((8, rows), jnp.float32)] * 2
+        + [pltpu.VMEM((HD, rows), jnp.float32)],
         compiler_params=pltpu.CompilerParams(vmem_limit_bytes=40 * 1024 * 1024),
         cost_estimate=pl.CostEstimate(
             flops=work * 6 * HD, bytes_accessed=10**7, transcendentals=work
@@ -283,9 +301,14 @@
         )
 
     grads = [mine] + [xor_permute(mine, "seq", k) for k in range(1, low)]
-    block = sum(product(x_mine[k], grads[k]) for k in range(low))
-    grads = [xor_permute(g, "pair", 1) for g in grads]
-    block = block + sum(product(x_pair[k], grads[k]) for k in range(low))
+    pairs = [xor_permute(mine, "pair", 1)]
+    block = product(x_mine[0], mine) + product(x_pair[0], pairs[0])
+    grads[1], block = tie((grads[1], block))
+    pairs += [xor_permute(g, "pair", 1) for g in grads[1:]]
+    for k in range(1, low):
+        block = block + product(x_mine[k], grads[k])
+    for k in range(1, low):
+        block = block + product(x_pair[k], pairs[k])
     block = block.reshape(high, piece, width)
     total = lax.dynamic_index_in_dim(block, layer, 0, keepdims=False)
     sent = block.astype(jnp.bfloat16)

time: 77.7 us -> 75.3 us (0.969)
  Pallas kernels: 28.2 us -> 24.4 us
  waiting for transfers between devices: 20.2 us -> 21.3 us
    pallas_call x1, Pallas kernels: 25 us -> 21.1 us  [attend(): pl.pallas_call(attend_kernel, in_specs=[pl.BlockSpec(memory_space=pltpu.V...]
    ppermute x24, waiting for transfers between devices: 20.2 us -> 21.3 us  [xor_permute(): return lax.ppermute(x, axis, [(i, i ^ mask) for i in range(n)])]
    unnamed x8 -> x7, local copies, waits for them, and re-layouts: 2.21 us -> 2.12 us
  transfers between devices with their start and end apart: 24 -> 24, of which waited for: 7 -> 7; matrix products, arithmetic and copies ran while one was open for 3% -> 4% of each run, Pallas kernels for 36% -> 32%
where the time goes in v5:
time: 75.3 us; the launch traced here: 75 us
  Pallas kernels  24.4 us (32%)
  starting transfers between devices  23 us (31%)
  waiting for transfers between devices  21.3 us (28%)
  other arithmetic  2.23 us (3%)
  local copies, waits for them, and re-layouts  2.2 us (3%)
  matrix products  1.72 us (2%)
    ppermute x24, starting transfers between devices, xor_permute(): return lax.ppermute(x, axis, [(i, i ^ mask) for i in range(n)])  23 us
    ppermute x24, waiting for transfers between devices, xor_permute(): return lax.ppermute(x, axis, [(i, i ^ mask) for i in range(n)])  21.3 us
    pallas_call x1, Pallas kernels, attend(): pl.pallas_call(attend_kernel, in_specs=[pl.BlockSpec(memory_space=pltpu.V...  21.1 us
    pallas_call x3, Pallas kernels, prepare_keys(): pl.pallas_call(prepare_keys_kernel, out_shape=(jax.ShapeDtypeStruct((2, b...  2.92 us
    unnamed x7, local copies, waits for them, and re-layouts  2.12 us
    dot_general x8, matrix products, product(): lax.dot_general(x, grad, (((0,), (0,)), ((), ())), preferred_element_type...  1.72 us
  transfers between devices with their start and end apart: 24, of which 7 were waited for; matrix products, arithmetic and copies ran while one was open for 4% of the time, Pallas kernels for 32%

profile of v5, /device:TPU:0, one launch (start us, length us, event | category | flops | bytes accessed | tf_op | source)
XLA Modules:
  0.0 75.0 jit_solution(17204372279056408678)
XLA Ops:
  0.0 0.7 bitcast_convert_fusion
  0.7 0.8 %maximum_bitcast_fusion = bf16[1,144,128]{2,1,0:T(8,128)(2,1)S(1)} fusion(bf16[16,128]{1,0:T(8,128)(2,1)S(1)} %bitcast_convert_fusion, bf16[128,128]{1,0:T(8,128)(2,1)} %param.8), kind=kLoop, calls=%fused_computation.15 | loop fusion | flops 73728 | bytes 73728 | tf_op jit(solution)/shard_map/broadcast_in_dim | solution.py:275
  1.5 5.1 %collective-permute-start = (bf16[1,144,128]{2,1,0:T(8,128)(2,1)S(1)}, bf16[1,144,128]{2,1,0:T(8,128)(2,1)S(1)}, u32[]{:S(2)}, u32[]{:S(2)}) collective-permute-start(bf16[1,144,128]{2,1,0:T(8,128)(2,1)S(1)} %maximum_bitcast_fusion), channel_id=1, source_target_pairs={{0,24},{2,26},{4,28},{6,30},{8,16},{10,18},{12,20},{14,22},{16,8},... | collective-permute-start | bytes 110600 | tf_op jit(solution)/shard_map/ppermute | solution.py:259
  6.5 0.0 collective-permute-start.2
  6.5 0.6 collective-permute-start.1
  7.1 1.1 %copy.6 = bf16[128,1024]{0,1:T(8,128)(2,1)S(1)} copy(bf16[128,1024]{1,0:T(8,128)(2,1)} %param.6) | data formatting | bytes 524288 | tf_op args[0]
  8.2 0.0 copy-start
  8.3 0.0 copy-start.1
  8.3 0.9 %copy-done = bf16[128,1024]{1,0:T(8,128)(2,1)S(1)} copy-done((bf16[128,1024]{1,0:T(8,128)(2,1)S(1)}, bf16[128,1024]{1,0:T(8,128)(2,1)}, u32[]{:S(2)}) %copy-start) | copy-done | bytes 262168
  9.2 0.1 copy-done.1
  9.3 0.3 shard_map.55
  9.6 0.0 collective-permute-done
  9.6 1.8 %collective-permute-done.2 = bf16[1,144,128]{2,1,0:T(8,128)(2,1)S(1)} collective-permute-done((bf16[1,144,128]{2,1,0:T(8,128)(2,1)S(1)}, bf16[1,144,128]{2,1,0:T(8,128)(2,1)S(1)}, u32[]{:S(2)}, u32[]{:S(2)}) %collective-permute-start.2) | collective-permute-done | bytes 36896 | tf_op jit(solution)/shard_map/ppermute | solution.py:259
  11.4 0.0 collective-permute-done.1
  11.4 2.5 %collective-permute-start.3 = (bf16[4,144,128]{2,1,0:T(8,128)(2,1)S(1)}, bf16[4,144,128]{2,1,0:T(8,128)(2,1)S(1)}, u32[]{:S(2)}, u32[]{:S(2)}) collective-permute-start(bf16[4,144,128]{2,1,0:T(8,128)(2,1)S(1)} %pad_maximum_fusion.1.refs_0_), channel_id=1, source_target_pairs={{0,6},{2,4},{4,2},{6,0},{8,14},{10,12},{12,10},{14,8},{16,22},{18,... | collective-permute-start | bytes 442376 | tf_op jit(solution)/shard_map/ppermute | solution.py:259
  13.9 0.5 collective-permute-start.5
  14.5 0.5 collective-permute-start.6
  15.0 0.4 shard_map.56
  15.4 2.8 %collective-permute-done.3.refs_2_ = bf16[4,144,128]{2,1,0:T(8,128)(2,1)S(1)} collective-permute-done((bf16[4,144,128]{2,1,0:T(8,128)(2,1)S(1)}, bf16[4,144,128]{2,1,0:T(8,128)(2,1)S(1)}, u32[]{:S(2)}, u32[]{:S(2)}) %collective-permute-start.3) | collective-permute-done | bytes 147488 | tf_op jit(solution)/shard_map/ppermute | solution.py:259
  18.1 0.0 collective-permute-start.4
  18.1 0.5 collective-permute-start.7
  18.6 1.2 %collective-permute-done.5.refs_0_ = bf16[4,144,128]{2,1,0:T(8,128)(2,1)S(1)} collective-permute-done((bf16[4,144,128]{2,1,0:T(8,128)(2,1)S(1)}, bf16[4,144,128]{2,1,0:T(8,128)(2,1)S(1)}, u32[]{:S(2)}, u32[]{:S(2)}) %collective-permute-start.5) | collective-permute-done | bytes 147488 | tf_op jit(solution)/shard_map/ppermute | solution.py:259
  19.8 0.0 collective-permute-start.8
  19.8 0.0 collective-permute-done.6.refs_1_
  19.8 0.5 collective-permute-start.9
  20.3 1.9 %collective-permute-start.13 = (bf16[2,128,128]{1,2,0:T(8,128)(2,1)S(1)}, bf16[2,128,128]{1,2,0:T(8,128)(2,1)S(1)}, u32[]{:S(2)}, u32[]{:S(2)}) collective-permute-start(bf16[2,128,128]{1,2,0:T(8,128)(2,1)S(1)} %get-tuple-element.59), channel_id=1, source_target_pairs={{0,6},{2,4},{4,2},{6,0},{8,14},{10,12},{12,10},{14,8},{16,22},{18,... | collective-permute-start | bytes 196616 | tf_op jit(solution)/shard_map/ppermute | solution.py:259
  22.2 1.1 %shard_map.57 = (bf16[2,1536,128]{2,1,0:T(8,128)(2,1)S(1)}, bf16[1536,128]{1,0:T(8,128)(2,1)S(1)}, bf16[12,64,128]{2,1,0:T(8,128)(2,1)S(1)}) custom-call(bf16[4,144,128]{2,1,0:T(8,128)(2,1)S(1)} %collective-permute-done.5.refs_0_, bf16[4,144,128]{2,1,0:T(8,128)(2,1)S(1)} %collective-permute-done.6.refs_1_, ...), custom_call_target="tpu_custom_call" | custom-call | flops 12000000 | bytes 1200000 | tf_op jit(solution)/shard_map/pallas_call | solution.py:99
  23.3 0.0 collective-permute-done.4.refs_3_
  23.3 1.2 %collective-permute-start.12 = (bf16[2,128,128]{1,2,0:T(8,128)(2,1)S(1)}, bf16[2,128,128]{1,2,0:T(8,128)(2,1)S(1)}, u32[]{:S(2)}, u32[]{:S(2)}) collective-permute-start(bf16[2,128,128]{1,2,0:T(8,128)(2,1)S(1)} %get-tuple-element.60), channel_id=1, source_target_pairs={{0,4},{2,6},{4,0},{6,2},{8,12},{10,14},{12,8},{14,10},{16,20},{18,... | collective-permute-start | bytes 196616 | tf_op jit(solution)/shard_map/ppermute | solution.py:259
  24.5 0.0 collective-permute-done.7.refs_0_
  24.5 0.5 collective-permute-start.11
  25.1 1.4 %shard_map.58 = (bf16[2,2048,128]{2,1,0:T(8,128)(2,1)S(1)}, bf16[2048,128]{1,0:T(8,128)(2,1)S(1)}, bf16[16,64,128]{2,1,0:T(8,128)(2,1)S(1)}) custom-call(bf16[4,144,128]{2,1,0:T(8,128)(2,1)S(1)} %collective-permute-done.7.refs_0_, bf16[4,144,128]{2,1,0:T(8,128)(2,1)S(1)} %collective-permute-done.8.refs_1_, ...), custom_call_target="tpu_custom_call" | custom-call | flops 16000000 | bytes 1600000 | tf_op jit(solution)/shard_map/pallas_call | solution.py:99
  26.5 21.1 %shard_map.59 = bf16[128,1024]{1,0:T(8,128)(2,1)S(1)} custom-call(bf16[16,256,128]{2,1,0:T(8,128)(2,1)S(1)} %get-tuple-element.32.left, bf16[16,128,128]{2,1,0:T(8,128)(2,1)S(1)} %get-tuple-element.33.grd, bf16[2,512,128]{2,1,0:T(8,128)(2,1)S(1)} %get-tuple-element.38.refs_0_, bf16[512,128]{1,0:T(8,128)(2,1)S(1)} %get-tuple-element.39.refs_1_, ...), custom_call_target="tpu_custom_call" | custom-call | flops 3221225472 | bytes 10000000 | tf_op jit(solution)/shard_map/pallas_call | solution.py:236
  47.6 0.1 collective-permute-start.15
  47.7 0.0 collective-permute-done.13
  47.7 0.0 collective-permute-done.11
  47.8 0.5 collective-permute-start.14
  48.4 1.8 %collective-permute-start.17 = (bf16[128,1024]{1,0:T(8,128)(2,1)S(1)}, bf16[128,1024]{1,0:T(8,128)(2,1)S(1)}, u32[]{:S(2)}, u32[]{:S(2)}) collective-permute-start(bf16[128,1024]{1,0:T(8,128)(2,1)S(1)} %shard_map.59), channel_id=1, source_target_pairs={{0,6},{2,4},{4,2},{6,0},{8,14},{10,12},{12,10},{14,8},{16,22},{18,... | collective-permute-start | bytes 786440 | tf_op jit(solution)/shard_map/ppermute | solution.py:259
  50.2 1.1 %collective-permute-start.16 = (bf16[128,1024]{1,0:T(8,128)(2,1)S(1)}, bf16[128,1024]{1,0:T(8,128)(2,1)S(1)}, u32[]{:S(2)}, u32[]{:S(2)}) collective-permute-start(bf16[128,1024]{1,0:T(8,128)(2,1)S(1)} %shard_map.59), channel_id=1, source_target_pairs={{0,4},{2,6},{4,0},{6,2},{8,12},{10,14},{12,8},{14,10},{16,20},{18,... | collective-permute-start | bytes 786440 | tf_op jit(solution)/shard_map/ppermute | solution.py:259
  51.3 0.5 collective-permute-start.10
  51.9 0.0 collective-permute-done.14
  51.9 0.0 collective-permute-done.15
  51.9 0.2 fusion.8
  52.1 0.2 convolution_add_fusion.1
  52.3 10.4 %collective-permute-done.10 = bf16[128,1024]{1,0:T(8,128)(2,1)S(1)} collective-permute-done((bf16[128,1024]{1,0:T(8,128)(2,1)S(1)}, bf16[128,1024]{1,0:T(8,128)(2,1)S(1)}, u32[]{:S(2)}, u32[]{:S(2)}) %collective-permute-start.10) | collective-permute-done | bytes 262176 | tf_op jit(solution)/shard_map/ppermute | solution.py:259
  62.7 0.0 collective-permute-start.18
  62.7 0.0 collective-permute-done.17
  62.7 0.5 collective-permute-start.20
  63.2 0.2 fusion.7
  63.4 0.0 collective-permute-done.16
  63.4 0.1 collective-permute-start.19
  63.5 0.2 fusion.5
  63.7 0.2 fusion.6
  64.0 0.6 collective-permute-done.20
  64.6 0.2 fusion.3
  64.8 0.2 fusion.4
  65.1 0.0 collective-permute-done.19
  65.1 0.2 fusion
  65.4 2.7 %collective-permute-start.23 = (bf16[32,1024]{1,0:T(8,128)(2,1)S(1)}, bf16[32,1024]{1,0:T(8,128)(2,1)S(1)}, u32[]{:S(2)}, u32[]{:S(2)}) collective-permute-start(bf16[32,1024]{1,0:T(8,128)(2,1)S(1)} %get-tuple-element.56), channel_id=1, source_target_pairs={{0,24},{2,26},{4,28},{6,30},{8,16},{10,18},{12,20},{14,22},{16,8},... | collective-permute-start | bytes 196616 | tf_op jit(solution)/shard_map/ppermute | solution.py:259
  68.1 1.7 %collective-permute-start.21 = (bf16[32,1024]{1,0:T(8,128)(2,1)S(1)}, bf16[32,1024]{1,0:T(8,128)(2,1)S(1)}, u32[]{:S(2)}, u32[]{:S(2)}) collective-permute-start(bf16[32,1024]{1,0:T(8,128)(2,1)S(1)} %get-tuple-element.55), channel_id=1, source_target_pairs={{0,8},{2,10},{4,12},{6,14},{8,0},{10,2},{12,4},{14,6},{16,24},{18,... | collective-permute-start | bytes 196616 | tf_op jit(solution)/shard_map/ppermute | solution.py:259
  69.8 2.4 %collective-permute-done.23 = bf16[32,1024]{1,0:T(8,128)(2,1)S(1)} collective-permute-done((bf16[32,1024]{1,0:T(8,128)(2,1)S(1)}, bf16[32,1024]{1,0:T(8,128)(2,1)S(1)}, u32[]{:S(2)}, u32[]{:S(2)}) %collective-permute-start.23) | collective-permute-done | bytes 65568 | tf_op jit(solution)/shard_map/ppermute | solution.py:259
  72.3 2.1 %collective-permute-done.22 = bf16[32,1024]{1,0:T(8,128)(2,1)S(1)} collective-permute-done((bf16[32,1024]{1,0:T(8,128)(2,1)S(1)}, bf16[32,1024]{1,0:T(8,128)(2,1)S(1)}, u32[]{:S(2)}, u32[]{:S(2)}) %collective-permute-start.22) | collective-permute-done | bytes 65568 | tf_op jit(solution)/shard_map/ppermute | solution.py:259
  74.3 0.0 collective-permute-done.21
  74.3 0.7 fusion.2
  (14 shorter events, 0.2 us)
Async XLA Ops:
  1.5 8.2 %collective-permute-start = (bf16[1,144,128]{2,1,0:T(8,128)(2,1)S(1)}, bf16[1,144,128]{2,1,0:T(8,128)(2,1)S(1)}, u32[]{:S(2)}, u32[]{:S(2)}) collective-permute-start(bf16[1,144,128]{2,1,0:T(8,128)(2,1)S(1)} %maximum_bitcast_fusion), channel_id=1, source_target_pairs={{0,24},{2,26},{4,28},{6,30},{8,16},{10,18},{12,20},{14,22},{16,8},... | collective-permute-start | bytes 110600 | tf_op jit(solution)/shard_map/ppermute | solution.py:259
  6.5 4.9 %collective-permute-start.2 = (bf16[1,144,128]{2,1,0:T(8,128)(2,1)S(1)}, bf16[1,144,128]{2,1,0:T(8,128)(2,1)S(1)}, u32[]{:S(2)}, u32[]{:S(2)}) collective-permute-start(bf16[1,144,128]{2,1,0:T(8,128)(2,1)S(1)} %maximum_bitcast_fusion), channel_id=1, source_target_pairs={{0,16},{2,18},{4,20},{6,22},{8,24},{10,26},{12,28},{14,30},{16,0},... | collective-permute-start | bytes 110600 | tf_op jit(solution)/shard_map/ppermute | solution.py:259
  6.5 4.9 %collective-permute-start.1 = (bf16[1,144,128]{2,1,0:T(8,128)(2,1)S(1)}, bf16[1,144,128]{2,1,0:T(8,128)(2,1)S(1)}, u32[]{:S(2)}, u32[]{:S(2)}) collective-permute-start(bf16[1,144,128]{2,1,0:T(8,128)(2,1)S(1)} %maximum_bitcast_fusion), channel_id=1, source_target_pairs={{0,8},{2,10},{4,12},{6,14},{8,0},{10,2},{12,4},{14,6},{16,24},{18,... | collective-permute-start | bytes 110600 | tf_op jit(solution)/shard_map/ppermute | solution.py:259
  7.1 1.2 %copy-start.2 = (s32[128,16]{0,1:T(8,128)S(1)}, s32[128,16]{0,1:T(8,128)}, u32[]{:S(2)}) copy-start(s32[128,16]{0,1:T(8,128)} %param.10) | copy-start | bytes 24580
  8.2 1.0 %copy-start = (bf16[128,1024]{1,0:T(8,128)(2,1)S(1)}, bf16[128,1024]{1,0:T(8,128)(2,1)}, u32[]{:S(2)}) copy-start(bf16[128,1024]{1,0:T(8,128)(2,1)} %q_ref.1) | copy-start | bytes 786436
  8.3 1.0 %copy-start.1 = (bf16[128,1024]{1,0:T(8,128)(2,1)S(1)}, bf16[128,1024]{1,0:T(8,128)(2,1)}, u32[]{:S(2)}) copy-start(bf16[128,1024]{1,0:T(8,128)(2,1)} %g_ref.1) | copy-start | bytes 786436
  11.4 6.7 %collective-permute-start.3 = (bf16[4,144,128]{2,1,0:T(8,128)(2,1)S(1)}, bf16[4,144,128]{2,1,0:T(8,128)(2,1)S(1)}, u32[]{:S(2)}, u32[]{:S(2)}) collective-permute-start(bf16[4,144,128]{2,1,0:T(8,128)(2,1)S(1)} %pad_maximum_fusion.1.refs_0_), channel_id=1, source_target_pairs={{0,6},{2,4},{4,2},{6,0},{8,14},{10,12},{12,10},{14,8},{16,22},{18,... | collective-permute-start | bytes 442376 | tf_op jit(solution)/shard_map/ppermute | solution.py:259
  13.9 5.9 %collective-permute-start.5 = (bf16[4,144,128]{2,1,0:T(8,128)(2,1)S(1)}, bf16[4,144,128]{2,1,0:T(8,128)(2,1)S(1)}, u32[]{:S(2)}, u32[]{:S(2)}) collective-permute-start(bf16[4,144,128]{2,1,0:T(8,128)(2,1)S(1)} %pad_maximum_fusion.1.refs_0_), channel_id=1, source_target_pairs={{0,2},{2,0},{4,6},{6,4},{8,10},{10,8},{12,14},{14,12},{16,18},{18,... | collective-permute-start | bytes 442376 | tf_op jit(solution)/shard_map/ppermute | solution.py:259
  14.5 5.3 %collective-permute-start.6 = (bf16[4,144,128]{2,1,0:T(8,128)(2,1)S(1)}, bf16[4,144,128]{2,1,0:T(8,128)(2,1)S(1)}, u32[]{:S(2)}, u32[]{:S(2)}) collective-permute-start(bf16[4,144,128]{2,1,0:T(8,128)(2,1)S(1)} %pad_maximum_fusion.1.refs_0_), channel_id=1, source_target_pairs={{0,4},{2,6},{4,0},{6,2},{8,12},{10,14},{12,8},{14,10},{16,20},{18,... | collective-permute-start | bytes 442376 | tf_op jit(solution)/shard_map/ppermute | solution.py:259
  18.1 5.2 %collective-permute-start.4 = (bf16[4,144,128]{2,1,0:T(8,128)(2,1)S(1)}, bf16[4,144,128]{2,1,0:T(8,128)(2,1)S(1)}, u32[]{:S(2)}, u32[]{:S(2)}) collective-permute-start(bf16[4,144,128]{2,1,0:T(8,128)(2,1)S(1)} %collective-permute-done.3.refs_2_), channel_id=1, source_target_pairs={{0,1},{1,0},{2,3},{3,2},{4,5},{5,4},{6,7},{7,6},{8,9},{9,8},{10,11... | collective-permute-start | bytes 442376 | tf_op jit(solution)/shard_map/ppermute | solution.py:259
  18.1 6.4 %collective-permute-start.7 = (bf16[4,144,128]{2,1,0:T(8,128)(2,1)S(1)}, bf16[4,144,128]{2,1,0:T(8,128)(2,1)S(1)}, u32[]{:S(2)}, u32[]{:S(2)}) collective-permute-start(bf16[4,144,128]{2,1,0:T(8,128)(2,1)S(1)} %pad_maximum_fusion.1.refs_0_), channel_id=1, source_target_pairs={{0,1},{1,0},{2,3},{3,2},{4,5},{5,4},{6,7},{7,6},{8,9},{9,8},{10,11... | collective-permute-start | bytes 442376 | tf_op jit(solution)/shard_map/ppermute | solution.py:259
  19.8 5.3 %collective-permute-start.8 = (bf16[4,144,128]{2,1,0:T(8,128)(2,1)S(1)}, bf16[4,144,128]{2,1,0:T(8,128)(2,1)S(1)}, u32[]{:S(2)}, u32[]{:S(2)}) collective-permute-start(bf16[4,144,128]{2,1,0:T(8,128)(2,1)S(1)} %collective-permute-done.5.refs_0_), channel_id=1, source_target_pairs={{0,1},{1,0},{2,3},{3,2},{4,5},{5,4},{6,7},{7,6},{8,9},{9,8},{10,11... | collective-permute-start | bytes 442376 | tf_op jit(solution)/shard_map/ppermute | solution.py:259
  19.8 5.3 %collective-permute-start.9 = (bf16[4,144,128]{2,1,0:T(8,128)(2,1)S(1)}, bf16[4,144,128]{2,1,0:T(8,128)(2,1)S(1)}, u32[]{:S(2)}, u32[]{:S(2)}) collective-permute-start(bf16[4,144,128]{2,1,0:T(8,128)(2,1)S(1)} %collective-permute-done.6.refs_1_), channel_id=1, source_target_pairs={{0,1},{1,0},{2,3},{3,2},{4,5},{5,4},{6,7},{7,6},{8,9},{9,8},{10,11... | collective-permute-start | bytes 442376 | tf_op jit(solution)/shard_map/ppermute | solution.py:259
  20.3 27.4 %collective-permute-start.13 = (bf16[2,128,128]{1,2,0:T(8,128)(2,1)S(1)}, bf16[2,128,128]{1,2,0:T(8,128)(2,1)S(1)}, u32[]{:S(2)}, u32[]{:S(2)}) collective-permute-start(bf16[2,128,128]{1,2,0:T(8,128)(2,1)S(1)} %get-tuple-element.59), channel_id=1, source_target_pairs={{0,6},{2,4},{4,2},{6,0},{8,14},{10,12},{12,10},{14,8},{16,22},{18,... | collective-permute-start | bytes 196616 | tf_op jit(solution)/shard_map/ppermute | solution.py:259
  23.3 24.4 %collective-permute-start.12 = (bf16[2,128,128]{1,2,0:T(8,128)(2,1)S(1)}, bf16[2,128,128]{1,2,0:T(8,128)(2,1)S(1)}, u32[]{:S(2)}, u32[]{:S(2)}) collective-permute-start(bf16[2,128,128]{1,2,0:T(8,128)(2,1)S(1)} %get-tuple-element.60), channel_id=1, source_target_pairs={{0,4},{2,6},{4,0},{6,2},{8,12},{10,14},{12,8},{14,10},{16,20},{18,... | collective-permute-start | bytes 196616 | tf_op jit(solution)/shard_map/ppermute | solution.py:259
  24.5 23.2 %collective-permute-start.11 = (bf16[2,128,128]{1,2,0:T(8,128)(2,1)S(1)}, bf16[2,128,128]{1,2,0:T(8,128)(2,1)S(1)}, u32[]{:S(2)}, u32[]{:S(2)}) collective-permute-start(bf16[2,128,128]{1,2,0:T(8,128)(2,1)S(1)} %get-tuple-element.61), channel_id=1, source_target_pairs={{0,2},{2,0},{4,6},{6,4},{8,10},{10,8},{12,14},{14,12},{16,18},{18,... | collective-permute-start | bytes 196616 | tf_op jit(solution)/shard_map/ppermute | solution.py:259
  47.6 4.2 %collective-permute-start.15 = (bf16[128,1024]{1,0:T(8,128)(2,1)S(1)}, bf16[128,1024]{1,0:T(8,128)(2,1)S(1)}, u32[]{:S(2)}, u32[]{:S(2)}) collective-permute-start(bf16[128,1024]{1,0:T(8,128)(2,1)S(1)} %shard_map.59), channel_id=1, source_target_pairs={{0,1},{1,0},{2,3},{3,2},{4,5},{5,4},{6,7},{7,6},{8,9},{9,8},{10,11... | collective-permute-start | bytes 786440 | tf_op jit(solution)/shard_map/ppermute | solution.py:259
  47.8 4.0 %collective-permute-start.14 = (bf16[4,128,128]{1,2,0:T(8,128)(2,1)S(1)}, bf16[4,128,128]{1,2,0:T(8,128)(2,1)S(1)}, u32[]{:S(2)}, u32[]{:S(2)}) collective-permute-start(bf16[4,128,128]{1,2,0:T(8,128)(2,1)S(1)} %dynamic-slice_bitcast_fusion), channel_id=1, source_target_pairs={{0,1},{1,0},{2,3},{3,2},{4,5},{5,4},{6,7},{7,6},{8,9},{9,8},{10,11... | collective-permute-start | bytes 393224 | tf_op jit(solution)/shard_map/ppermute | solution.py:259
  48.4 14.3 %collective-permute-start.17 = (bf16[128,1024]{1,0:T(8,128)(2,1)S(1)}, bf16[128,1024]{1,0:T(8,128)(2,1)S(1)}, u32[]{:S(2)}, u32[]{:S(2)}) collective-permute-start(bf16[128,1024]{1,0:T(8,128)(2,1)S(1)} %shard_map.59), channel_id=1, source_target_pairs={{0,6},{2,4},{4,2},{6,0},{8,14},{10,12},{12,10},{14,8},{16,22},{18,... | collective-permute-start | bytes 786440 | tf_op jit(solution)/shard_map/ppermute | solution.py:259
  50.2 13.2 %collective-permute-start.16 = (bf16[128,1024]{1,0:T(8,128)(2,1)S(1)}, bf16[128,1024]{1,0:T(8,128)(2,1)S(1)}, u32[]{:S(2)}, u32[]{:S(2)}) collective-permute-start(bf16[128,1024]{1,0:T(8,128)(2,1)S(1)} %shard_map.59), channel_id=1, source_target_pairs={{0,4},{2,6},{4,0},{6,2},{8,12},{10,14},{12,8},{14,10},{16,20},{18,... | collective-permute-start | bytes 786440 | tf_op jit(solution)/shard_map/ppermute | solution.py:259
  51.3 11.4 %collective-permute-start.10 = (bf16[128,1024]{1,0:T(8,128)(2,1)S(1)}, bf16[128,1024]{1,0:T(8,128)(2,1)S(1)}, u32[]{:S(2)}, u32[]{:S(2)}) collective-permute-start(bf16[128,1024]{1,0:T(8,128)(2,1)S(1)} %shard_map.59), channel_id=1, source_target_pairs={{0,2},{2,0},{4,6},{6,4},{8,10},{10,8},{12,14},{14,12},{16,18},{18,... | collective-permute-start | bytes 786440 | tf_op jit(solution)/shard_map/ppermute | solution.py:259
  62.7 2.1 %collective-permute-start.18 = (bf16[128,1024]{1,0:T(8,128)(2,1)S(1)}, bf16[128,1024]{1,0:T(8,128)(2,1)S(1)}, u32[]{:S(2)}, u32[]{:S(2)}) collective-permute-start(bf16[128,1024]{1,0:T(8,128)(2,1)S(1)} %collective-permute-done.10), channel_id=1, source_target_pairs={{0,1},{1,0},{2,3},{3,2},{4,5},{5,4},{6,7},{7,6},{8,9},{9,8},{10,11... | collective-permute-start | bytes 786440 | tf_op jit(solution)/shard_map/ppermute | solution.py:259
  62.7 1.9 %collective-permute-start.20 = (bf16[128,1024]{1,0:T(8,128)(2,1)S(1)}, bf16[128,1024]{1,0:T(8,128)(2,1)S(1)}, u32[]{:S(2)}, u32[]{:S(2)}) collective-permute-start(bf16[128,1024]{1,0:T(8,128)(2,1)S(1)} %collective-permute-done.17), channel_id=1, source_target_pairs={{0,1},{1,0},{2,3},{3,2},{4,5},{5,4},{6,7},{7,6},{8,9},{9,8},{10,11... | collective-permute-start | bytes 786440 | tf_op jit(solution)/shard_map/ppermute | solution.py:259
  63.4 1.6 %collective-permute-start.19 = (bf16[128,1024]{1,0:T(8,128)(2,1)S(1)}, bf16[128,1024]{1,0:T(8,128)(2,1)S(1)}, u32[]{:S(2)}, u32[]{:S(2)}) collective-permute-start(bf16[128,1024]{1,0:T(8,128)(2,1)S(1)} %collective-permute-done.16), channel_id=1, source_target_pairs={{0,1},{1,0},{2,3},{3,2},{4,5},{5,4},{6,7},{7,6},{8,9},{9,8},{10,11... | collective-permute-start | bytes 786440 | tf_op jit(solution)/shard_map/ppermute | solution.py:259
  65.4 6.9 %collective-permute-start.23 = (bf16[32,1024]{1,0:T(8,128)(2,1)S(1)}, bf16[32,1024]{1,0:T(8,128)(2,1)S(1)}, u32[]{:S(2)}, u32[]{:S(2)}) collective-permute-start(bf16[32,1024]{1,0:T(8,128)(2,1)S(1)} %get-tuple-element.56), channel_id=1, source_target_pairs={{0,24},{2,26},{4,28},{6,30},{8,16},{10,18},{12,20},{14,22},{16,8},... | collective-permute-start | bytes 196616 | tf_op jit(solution)/shard_map/ppermute | solution.py:259
  68.1 6.2 %collective-permute-start.22 = (bf16[32,1024]{1,0:T(8,128)(2,1)S(1)}, bf16[32,1024]{1,0:T(8,128)(2,1)S(1)}, u32[]{:S(2)}, u32[]{:S(2)}) collective-permute-start(bf16[32,1024]{1,0:T(8,128)(2,1)S(1)} %get-tuple-element.57), channel_id=1, source_target_pairs={{0,16},{2,18},{4,20},{6,22},{8,24},{10,26},{12,28},{14,30},{16,0},... | collective-permute-start | bytes 196616 | tf_op jit(solution)/shard_map/ppermute | solution.py:259
  68.1 6.2 %collective-permute-start.21 = (bf16[32,1024]{1,0:T(8,128)(2,1)S(1)}, bf16[32,1024]{1,0:T(8,128)(2,1)S(1)}, u32[]{:S(2)}, u32[]{:S(2)}) collective-permute-start(bf16[32,1024]{1,0:T(8,128)(2,1)S(1)} %get-tuple-element.55), channel_id=1, source_target_pairs={{0,8},{2,10},{4,12},{6,14},{8,0},{10,2},{12,4},{14,6},{16,24},{18,... | collective-permute-start | bytes 196616 | tf_op jit(solution)/shard_map/ppermute | solution.py:259

commit v6 on v5

--- a/solution.py
+++ b/solution.py
@@ -5,12 +5,12 @@
 from jax.experimental.pallas import tpu as pltpu
 from jax.sharding import PartitionSpec as P
 
+
 H = 16
 HD = 64
 HALF = 512
 CL_DEV = 8
 SCALE = HD ** (-0.5)
-LOG2E = 1.4426950408889634
 TILE = 512
 LAG = 1
 LATE = 0.5
@@ -249,11 +249,6 @@
     )(*operands)
 
 
-def bench(q, g, c, *parts):
-    groups = [prepare_keys(parts[:1]), prepare_keys(parts[1:4]), prepare_keys(parts[4:])]
-    return attend(prepare_rows(q, g, c), groups, q.shape[0])
-
-
 def xor_permute(x, axis, mask):
     n = lax.axis_size(axis)
     return lax.ppermute(x, axis, [(i, i ^ mask) for i in range(n)])
@@ -291,7 +286,8 @@
     x_part = [x_part[0]] + [xor_permute(x_part[k], "seq", k) for k in range(1, low)]
     x_part = jnp.stack(x_part)
     x_mine = lax.dynamic_index_in_dim(x_part, me, 1, keepdims=False)
-    x_pair = xor_permute(lax.dynamic_index_in_dim(x_part, 1 - me, 1, keepdims=False), "pair", 1)
+    x_pair = lax.dynamic_index_in_dim(x_part, 1 - me, 1, keepdims=False)
+    x_pair = xor_permute(x_pair, "pair", 1)
 
     mine = attend(left, groups, tok)
 

time: 75.3 us -> 75.3 us (level)
  no operation moved by 1% of the time
where the time goes in v6:
time: 75.3 us; the launch traced here: 75 us
  Pallas kernels  24.4 us (32%)
  starting transfers between devices  23 us (31%)
  waiting for transfers between devices  21.3 us (28%)
  other arithmetic  2.23 us (3%)
  local copies, waits for them, and re-layouts  2.2 us (3%)
  matrix products  1.72 us (2%)
    ppermute x24, starting transfers between devices, xor_permute(): return lax.ppermute(x, axis, [(i, i ^ mask) for i in range(n)])  23 us
    ppermute x24, waiting for transfers between devices, xor_permute(): return lax.ppermute(x, axis, [(i, i ^ mask) for i in range(n)])  21.3 us
    pallas_call x1, Pallas kernels, attend(): pl.pallas_call(attend_kernel, in_specs=[pl.BlockSpec(memory_space=pltpu.V...  21.1 us
    pallas_call x3, Pallas kernels, prepare_keys(): pl.pallas_call(prepare_keys_kernel, out_shape=(jax.ShapeDtypeStruct((2, b...  2.92 us
    unnamed x7, local copies, waits for them, and re-layouts  2.12 us
    dot_general x8, matrix products, product(): lax.dot_general(x, grad, (((0,), (0,)), ((), ())), preferred_element_type...  1.72 us
  transfers between devices with their start and end apart: 24, of which 7 were waited for; matrix products, arithmetic and copies ran while one was open for 4% of the time, Pallas kernels for 32%

profile of v6, /device:TPU:0, one launch (start us, length us, event | category | flops | bytes accessed | tf_op | source)
XLA Modules:
  0.0 75.0 jit_solution(17204372279056408678)
XLA Ops:
  0.0 0.7 bitcast_convert_fusion
  0.7 0.8 %maximum_bitcast_fusion = bf16[1,144,128]{2,1,0:T(8,128)(2,1)S(1)} fusion(bf16[16,128]{1,0:T(8,128)(2,1)S(1)} %bitcast_convert_fusion, bf16[128,128]{1,0:T(8,128)(2,1)} %param.8), kind=kLoop, calls=%fused_computation.15 | loop fusion | flops 73728 | bytes 73728 | tf_op jit(solution)/shard_map/broadcast_in_dim | solution.py:270
  1.5 5.1 %collective-permute-start = (bf16[1,144,128]{2,1,0:T(8,128)(2,1)S(1)}, bf16[1,144,128]{2,1,0:T(8,128)(2,1)S(1)}, u32[]{:S(2)}, u32[]{:S(2)}) collective-permute-start(bf16[1,144,128]{2,1,0:T(8,128)(2,1)S(1)} %maximum_bitcast_fusion), channel_id=1, source_target_pairs={{0,24},{2,26},{4,28},{6,30},{8,16},{10,18},{12,20},{14,22},{16,8},... | collective-permute-start | bytes 110600 | tf_op jit(solution)/shard_map/ppermute | solution.py:254
  6.5 0.0 collective-permute-start.2
  6.5 0.6 collective-permute-start.1
  7.1 1.1 %copy.6 = bf16[128,1024]{0,1:T(8,128)(2,1)S(1)} copy(bf16[128,1024]{1,0:T(8,128)(2,1)} %param.6) | data formatting | bytes 524288 | tf_op args[0]
  8.2 0.0 copy-start
  8.3 0.0 copy-start.1
  8.3 0.9 %copy-done = bf16[128,1024]{1,0:T(8,128)(2,1)S(1)} copy-done((bf16[128,1024]{1,0:T(8,128)(2,1)S(1)}, bf16[128,1024]{1,0:T(8,128)(2,1)}, u32[]{:S(2)}) %copy-start) | copy-done | bytes 262168
  9.2 0.1 copy-done.1
  9.3 0.3 shard_map.55
  9.6 0.0 collective-permute-done
  9.6 1.8 %collective-permute-done.2 = bf16[1,144,128]{2,1,0:T(8,128)(2,1)S(1)} collective-permute-done((bf16[1,144,128]{2,1,0:T(8,128)(2,1)S(1)}, bf16[1,144,128]{2,1,0:T(8,128)(2,1)S(1)}, u32[]{:S(2)}, u32[]{:S(2)}) %collective-permute-start.2) | collective-permute-done | bytes 36896 | tf_op jit(solution)/shard_map/ppermute | solution.py:254
  11.4 0.0 collective-permute-done.1
  11.4 2.5 %collective-permute-start.3 = (bf16[4,144,128]{2,1,0:T(8,128)(2,1)S(1)}, bf16[4,144,128]{2,1,0:T(8,128)(2,1)S(1)}, u32[]{:S(2)}, u32[]{:S(2)}) collective-permute-start(bf16[4,144,128]{2,1,0:T(8,128)(2,1)S(1)} %pad_maximum_fusion.1.refs_0_), channel_id=1, source_target_pairs={{0,6},{2,4},{4,2},{6,0},{8,14},{10,12},{12,10},{14,8},{16,22},{18,... | collective-permute-start | bytes 442376 | tf_op jit(solution)/shard_map/ppermute | solution.py:254
  13.9 0.5 collective-permute-start.5
  14.5 0.5 collective-permute-start.6
  15.0 0.4 shard_map.56
  15.4 2.8 %collective-permute-done.3.refs_2_ = bf16[4,144,128]{2,1,0:T(8,128)(2,1)S(1)} collective-permute-done((bf16[4,144,128]{2,1,0:T(8,128)(2,1)S(1)}, bf16[4,144,128]{2,1,0:T(8,128)(2,1)S(1)}, u32[]{:S(2)}, u32[]{:S(2)}) %collective-permute-start.3) | collective-permute-done | bytes 147488 | tf_op jit(solution)/shard_map/ppermute | solution.py:254
  18.1 0.0 collective-permute-start.4
  18.1 0.5 collective-permute-start.7
  18.6 1.2 %collective-permute-done.5.refs_0_ = bf16[4,144,128]{2,1,0:T(8,128)(2,1)S(1)} collective-permute-done((bf16[4,144,128]{2,1,0:T(8,128)(2,1)S(1)}, bf16[4,144,128]{2,1,0:T(8,128)(2,1)S(1)}, u32[]{:S(2)}, u32[]{:S(2)}) %collective-permute-start.5) | collective-permute-done | bytes 147488 | tf_op jit(solution)/shard_map/ppermute | solution.py:254
  19.8 0.0 collective-permute-start.8
  19.8 0.0 collective-permute-done.6.refs_1_
  19.8 0.5 collective-permute-start.9
  20.3 1.9 %collective-permute-start.13 = (bf16[2,128,128]{1,2,0:T(8,128)(2,1)S(1)}, bf16[2,128,128]{1,2,0:T(8,128)(2,1)S(1)}, u32[]{:S(2)}, u32[]{:S(2)}) collective-permute-start(bf16[2,128,128]{1,2,0:T(8,128)(2,1)S(1)} %get-tuple-element.59), channel_id=1, source_target_pairs={{0,6},{2,4},{4,2},{6,0},{8,14},{10,12},{12,10},{14,8},{16,22},{18,... | collective-permute-start | bytes 196616 | tf_op jit(solution)/shard_map/ppermute | solution.py:254
  22.2 1.1 %shard_map.57 = (bf16[2,1536,128]{2,1,0:T(8,128)(2,1)S(1)}, bf16[1536,128]{1,0:T(8,128)(2,1)S(1)}, bf16[12,64,128]{2,1,0:T(8,128)(2,1)S(1)}) custom-call(bf16[4,144,128]{2,1,0:T(8,128)(2,1)S(1)} %collective-permute-done.5.refs_0_, bf16[4,144,128]{2,1,0:T(8,128)(2,1)S(1)} %collective-permute-done.6.refs_1_, ...), custom_call_target="tpu_custom_call" | custom-call | flops 12000000 | bytes 1200000 | tf_op jit(solution)/shard_map/pallas_call | solution.py:99
  23.3 0.0 collective-permute-done.4.refs_3_
  23.3 1.2 %collective-permute-start.12 = (bf16[2,128,128]{1,2,0:T(8,128)(2,1)S(1)}, bf16[2,128,128]{1,2,0:T(8,128)(2,1)S(1)}, u32[]{:S(2)}, u32[]{:S(2)}) collective-permute-start(bf16[2,128,128]{1,2,0:T(8,128)(2,1)S(1)} %get-tuple-element.60), channel_id=1, source_target_pairs={{0,4},{2,6},{4,0},{6,2},{8,12},{10,14},{12,8},{14,10},{16,20},{18,... | collective-permute-start | bytes 196616 | tf_op jit(solution)/shard_map/ppermute | solution.py:254
  24.5 0.0 collective-permute-done.7.refs_0_
  24.5 0.5 collective-permute-start.11
  25.1 0.0 collective-permute-done.8.refs_1_
  25.1 1.4 %shard_map.58 = (bf16[2,2048,128]{2,1,0:T(8,128)(2,1)S(1)}, bf16[2048,128]{1,0:T(8,128)(2,1)S(1)}, bf16[16,64,128]{2,1,0:T(8,128)(2,1)S(1)}) custom-call(bf16[4,144,128]{2,1,0:T(8,128)(2,1)S(1)} %collective-permute-done.7.refs_0_, bf16[4,144,128]{2,1,0:T(8,128)(2,1)S(1)} %collective-permute-done.8.refs_1_, ...), custom_call_target="tpu_custom_call" | custom-call | flops 16000000 | bytes 1600000 | tf_op jit(solution)/shard_map/pallas_call | solution.py:99
  26.5 21.1 %shard_map.59 = bf16[128,1024]{1,0:T(8,128)(2,1)S(1)} custom-call(bf16[16,256,128]{2,1,0:T(8,128)(2,1)S(1)} %get-tuple-element.32.left, bf16[16,128,128]{2,1,0:T(8,128)(2,1)S(1)} %get-tuple-element.33.grd, bf16[2,512,128]{2,1,0:T(8,128)(2,1)S(1)} %get-tuple-element.38.refs_0_, bf16[512,128]{1,0:T(8,128)(2,1)S(1)} %get-tuple-element.39.refs_1_, ...), custom_call_target="tpu_custom_call" | custom-call | flops 3221225472 | bytes 10000000 | tf_op jit(solution)/shard_map/pallas_call | solution.py:236
  47.6 0.1 collective-permute-start.15
  47.7 0.0 collective-permute-done.13
  47.8 0.5 collective-permute-start.14
  48.4 1.8 %collective-permute-start.17 = (bf16[128,1024]{1,0:T(8,128)(2,1)S(1)}, bf16[128,1024]{1,0:T(8,128)(2,1)S(1)}, u32[]{:S(2)}, u32[]{:S(2)}) collective-permute-start(bf16[128,1024]{1,0:T(8,128)(2,1)S(1)} %shard_map.59), channel_id=1, source_target_pairs={{0,6},{2,4},{4,2},{6,0},{8,14},{10,12},{12,10},{14,8},{16,22},{18,... | collective-permute-start | bytes 786440 | tf_op jit(solution)/shard_map/ppermute | solution.py:254
  50.2 1.1 %collective-permute-start.16 = (bf16[128,1024]{1,0:T(8,128)(2,1)S(1)}, bf16[128,1024]{1,0:T(8,128)(2,1)S(1)}, u32[]{:S(2)}, u32[]{:S(2)}) collective-permute-start(bf16[128,1024]{1,0:T(8,128)(2,1)S(1)} %shard_map.59), channel_id=1, source_target_pairs={{0,4},{2,6},{4,0},{6,2},{8,12},{10,14},{12,8},{14,10},{16,20},{18,... | collective-permute-start | bytes 786440 | tf_op jit(solution)/shard_map/ppermute | solution.py:254
  51.3 0.5 collective-permute-start.10
  51.9 0.0 collective-permute-done.14
  51.9 0.0 collective-permute-done.15
  51.9 0.2 fusion.8
  52.1 0.2 convolution_add_fusion.1
  52.3 10.4 %collective-permute-done.10 = bf16[128,1024]{1,0:T(8,128)(2,1)S(1)} collective-permute-done((bf16[128,1024]{1,0:T(8,128)(2,1)S(1)}, bf16[128,1024]{1,0:T(8,128)(2,1)S(1)}, u32[]{:S(2)}, u32[]{:S(2)}) %collective-permute-start.10) | collective-permute-done | bytes 262176 | tf_op jit(solution)/shard_map/ppermute | solution.py:254
  62.7 0.0 collective-permute-start.18
  62.7 0.0 collective-permute-done.17
  62.7 0.5 collective-permute-start.20
  63.2 0.2 fusion.7
  63.4 0.0 collective-permute-done.16
  63.4 0.1 collective-permute-start.19
  63.5 0.2 fusion.5
  63.7 0.2 fusion.6
  64.0 0.6 collective-permute-done.20
  64.6 0.2 fusion.3
  64.8 0.2 fusion.4
  65.1 0.0 collective-permute-done.19
  65.1 0.2 fusion
  65.4 2.7 %collective-permute-start.23 = (bf16[32,1024]{1,0:T(8,128)(2,1)S(1)}, bf16[32,1024]{1,0:T(8,128)(2,1)S(1)}, u32[]{:S(2)}, u32[]{:S(2)}) collective-permute-start(bf16[32,1024]{1,0:T(8,128)(2,1)S(1)} %get-tuple-element.56), channel_id=1, source_target_pairs={{0,24},{2,26},{4,28},{6,30},{8,16},{10,18},{12,20},{14,22},{16,8},... | collective-permute-start | bytes 196616 | tf_op jit(solution)/shard_map/ppermute | solution.py:254
  68.1 1.7 %collective-permute-start.21 = (bf16[32,1024]{1,0:T(8,128)(2,1)S(1)}, bf16[32,1024]{1,0:T(8,128)(2,1)S(1)}, u32[]{:S(2)}, u32[]{:S(2)}) collective-permute-start(bf16[32,1024]{1,0:T(8,128)(2,1)S(1)} %get-tuple-element.55), channel_id=1, source_target_pairs={{0,8},{2,10},{4,12},{6,14},{8,0},{10,2},{12,4},{14,6},{16,24},{18,... | collective-permute-start | bytes 196616 | tf_op jit(solution)/shard_map/ppermute | solution.py:254
  69.8 2.4 %collective-permute-done.23 = bf16[32,1024]{1,0:T(8,128)(2,1)S(1)} collective-permute-done((bf16[32,1024]{1,0:T(8,128)(2,1)S(1)}, bf16[32,1024]{1,0:T(8,128)(2,1)S(1)}, u32[]{:S(2)}, u32[]{:S(2)}) %collective-permute-start.23) | collective-permute-done | bytes 65568 | tf_op jit(solution)/shard_map/ppermute | solution.py:254
  72.3 2.1 %collective-permute-done.22 = bf16[32,1024]{1,0:T(8,128)(2,1)S(1)} collective-permute-done((bf16[32,1024]{1,0:T(8,128)(2,1)S(1)}, bf16[32,1024]{1,0:T(8,128)(2,1)S(1)}, u32[]{:S(2)}, u32[]{:S(2)}) %collective-permute-start.22) | collective-permute-done | bytes 65568 | tf_op jit(solution)/shard_map/ppermute | solution.py:254
  74.3 0.0 collective-permute-done.21
  74.3 0.7 fusion.2
  (14 shorter events, 0.2 us)
Async XLA Ops:
  1.5 8.2 %collective-permute-start = (bf16[1,144,128]{2,1,0:T(8,128)(2,1)S(1)}, bf16[1,144,128]{2,1,0:T(8,128)(2,1)S(1)}, u32[]{:S(2)}, u32[]{:S(2)}) collective-permute-start(bf16[1,144,128]{2,1,0:T(8,128)(2,1)S(1)} %maximum_bitcast_fusion), channel_id=1, source_target_pairs={{0,24},{2,26},{4,28},{6,30},{8,16},{10,18},{12,20},{14,22},{16,8},... | collective-permute-start | bytes 110600 | tf_op jit(solution)/shard_map/ppermute | solution.py:254
  6.5 4.9 %collective-permute-start.2 = (bf16[1,144,128]{2,1,0:T(8,128)(2,1)S(1)}, bf16[1,144,128]{2,1,0:T(8,128)(2,1)S(1)}, u32[]{:S(2)}, u32[]{:S(2)}) collective-permute-start(bf16[1,144,128]{2,1,0:T(8,128)(2,1)S(1)} %maximum_bitcast_fusion), channel_id=1, source_target_pairs={{0,16},{2,18},{4,20},{6,22},{8,24},{10,26},{12,28},{14,30},{16,0},... | collective-permute-start | bytes 110600 | tf_op jit(solution)/shard_map/ppermute | solution.py:254
  6.5 4.9 %collective-permute-start.1 = (bf16[1,144,128]{2,1,0:T(8,128)(2,1)S(1)}, bf16[1,144,128]{2,1,0:T(8,128)(2,1)S(1)}, u32[]{:S(2)}, u32[]{:S(2)}) collective-permute-start(bf16[1,144,128]{2,1,0:T(8,128)(2,1)S(1)} %maximum_bitcast_fusion), channel_id=1, source_target_pairs={{0,8},{2,10},{4,12},{6,14},{8,0},{10,2},{12,4},{14,6},{16,24},{18,... | collective-permute-start | bytes 110600 | tf_op jit(solution)/shard_map/ppermute | solution.py:254
  7.1 1.2 %copy-start.2 = (s32[128,16]{0,1:T(8,128)S(1)}, s32[128,16]{0,1:T(8,128)}, u32[]{:S(2)}) copy-start(s32[128,16]{0,1:T(8,128)} %param.10) | copy-start | bytes 24580
  8.2 1.0 %copy-start = (bf16[128,1024]{1,0:T(8,128)(2,1)S(1)}, bf16[128,1024]{1,0:T(8,128)(2,1)}, u32[]{:S(2)}) copy-start(bf16[128,1024]{1,0:T(8,128)(2,1)} %q_ref.1) | copy-start | bytes 786436
  8.3 1.0 %copy-start.1 = (bf16[128,1024]{1,0:T(8,128)(2,1)S(1)}, bf16[128,1024]{1,0:T(8,128)(2,1)}, u32[]{:S(2)}) copy-start(bf16[128,1024]{1,0:T(8,128)(2,1)} %g_ref.1) | copy-start | bytes 786436
  11.4 6.7 %collective-permute-start.3 = (bf16[4,144,128]{2,1,0:T(8,128)(2,1)S(1)}, bf16[4,144,128]{2,1,0:T(8,128)(2,1)S(1)}, u32[]{:S(2)}, u32[]{:S(2)}) collective-permute-start(bf16[4,144,128]{2,1,0:T(8,128)(2,1)S(1)} %pad_maximum_fusion.1.refs_0_), channel_id=1, source_target_pairs={{0,6},{2,4},{4,2},{6,0},{8,14},{10,12},{12,10},{14,8},{16,22},{18,... | collective-permute-start | bytes 442376 | tf_op jit(solution)/shard_map/ppermute | solution.py:254
  13.9 5.9 %collective-permute-start.5 = (bf16[4,144,128]{2,1,0:T(8,128)(2,1)S(1)}, bf16[4,144,128]{2,1,0:T(8,128)(2,1)S(1)}, u32[]{:S(2)}, u32[]{:S(2)}) collective-permute-start(bf16[4,144,128]{2,1,0:T(8,128)(2,1)S(1)} %pad_maximum_fusion.1.refs_0_), channel_id=1, source_target_pairs={{0,2},{2,0},{4,6},{6,4},{8,10},{10,8},{12,14},{14,12},{16,18},{18,... | collective-permute-start | bytes 442376 | tf_op jit(solution)/shard_map/ppermute | solution.py:254
  14.5 5.3 %collective-permute-start.6 = (bf16[4,144,128]{2,1,0:T(8,128)(2,1)S(1)}, bf16[4,144,128]{2,1,0:T(8,128)(2,1)S(1)}, u32[]{:S(2)}, u32[]{:S(2)}) collective-permute-start(bf16[4,144,128]{2,1,0:T(8,128)(2,1)S(1)} %pad_maximum_fusion.1.refs_0_), channel_id=1, source_target_pairs={{0,4},{2,6},{4,0},{6,2},{8,12},{10,14},{12,8},{14,10},{16,20},{18,... | collective-permute-start | bytes 442376 | tf_op jit(solution)/shard_map/ppermute | solution.py:254
  18.1 5.2 %collective-permute-start.4 = (bf16[4,144,128]{2,1,0:T(8,128)(2,1)S(1)}, bf16[4,144,128]{2,1,0:T(8,128)(2,1)S(1)}, u32[]{:S(2)}, u32[]{:S(2)}) collective-permute-start(bf16[4,144,128]{2,1,0:T(8,128)(2,1)S(1)} %collective-permute-done.3.refs_2_), channel_id=1, source_target_pairs={{0,1},{1,0},{2,3},{3,2},{4,5},{5,4},{6,7},{7,6},{8,9},{9,8},{10,11... | collective-permute-start | bytes 442376 | tf_op jit(solution)/shard_map/ppermute | solution.py:254
  18.1 6.4 %collective-permute-start.7 = (bf16[4,144,128]{2,1,0:T(8,128)(2,1)S(1)}, bf16[4,144,128]{2,1,0:T(8,128)(2,1)S(1)}, u32[]{:S(2)}, u32[]{:S(2)}) collective-permute-start(bf16[4,144,128]{2,1,0:T(8,128)(2,1)S(1)} %pad_maximum_fusion.1.refs_0_), channel_id=1, source_target_pairs={{0,1},{1,0},{2,3},{3,2},{4,5},{5,4},{6,7},{7,6},{8,9},{9,8},{10,11... | collective-permute-start | bytes 442376 | tf_op jit(solution)/shard_map/ppermute | solution.py:254
  19.8 5.3 %collective-permute-start.8 = (bf16[4,144,128]{2,1,0:T(8,128)(2,1)S(1)}, bf16[4,144,128]{2,1,0:T(8,128)(2,1)S(1)}, u32[]{:S(2)}, u32[]{:S(2)}) collective-permute-start(bf16[4,144,128]{2,1,0:T(8,128)(2,1)S(1)} %collective-permute-done.5.refs_0_), channel_id=1, source_target_pairs={{0,1},{1,0},{2,3},{3,2},{4,5},{5,4},{6,7},{7,6},{8,9},{9,8},{10,11... | collective-permute-start | bytes 442376 | tf_op jit(solution)/shard_map/ppermute | solution.py:254
  19.8 5.3 %collective-permute-start.9 = (bf16[4,144,128]{2,1,0:T(8,128)(2,1)S(1)}, bf16[4,144,128]{2,1,0:T(8,128)(2,1)S(1)}, u32[]{:S(2)}, u32[]{:S(2)}) collective-permute-start(bf16[4,144,128]{2,1,0:T(8,128)(2,1)S(1)} %collective-permute-done.6.refs_1_), channel_id=1, source_target_pairs={{0,1},{1,0},{2,3},{3,2},{4,5},{5,4},{6,7},{7,6},{8,9},{9,8},{10,11... | collective-permute-start | bytes 442376 | tf_op jit(solution)/shard_map/ppermute | solution.py:254
  20.3 27.4 %collective-permute-start.13 = (bf16[2,128,128]{1,2,0:T(8,128)(2,1)S(1)}, bf16[2,128,128]{1,2,0:T(8,128)(2,1)S(1)}, u32[]{:S(2)}, u32[]{:S(2)}) collective-permute-start(bf16[2,128,128]{1,2,0:T(8,128)(2,1)S(1)} %get-tuple-element.59), channel_id=1, source_target_pairs={{0,6},{2,4},{4,2},{6,0},{8,14},{10,12},{12,10},{14,8},{16,22},{18,... | collective-permute-start | bytes 196616 | tf_op jit(solution)/shard_map/ppermute | solution.py:254
  23.3 24.4 %collective-permute-start.12 = (bf16[2,128,128]{1,2,0:T(8,128)(2,1)S(1)}, bf16[2,128,128]{1,2,0:T(8,128)(2,1)S(1)}, u32[]{:S(2)}, u32[]{:S(2)}) collective-permute-start(bf16[2,128,128]{1,2,0:T(8,128)(2,1)S(1)} %get-tuple-element.60), channel_id=1, source_target_pairs={{0,4},{2,6},{4,0},{6,2},{8,12},{10,14},{12,8},{14,10},{16,20},{18,... | collective-permute-start | bytes 196616 | tf_op jit(solution)/shard_map/ppermute | solution.py:254
  24.5 23.2 %collective-permute-start.11 = (bf16[2,128,128]{1,2,0:T(8,128)(2,1)S(1)}, bf16[2,128,128]{1,2,0:T(8,128)(2,1)S(1)}, u32[]{:S(2)}, u32[]{:S(2)}) collective-permute-start(bf16[2,128,128]{1,2,0:T(8,128)(2,1)S(1)} %get-tuple-element.61), channel_id=1, source_target_pairs={{0,2},{2,0},{4,6},{6,4},{8,10},{10,8},{12,14},{14,12},{16,18},{18,... | collective-permute-start | bytes 196616 | tf_op jit(solution)/shard_map/ppermute | solution.py:254
  47.6 4.2 %collective-permute-start.15 = (bf16[128,1024]{1,0:T(8,128)(2,1)S(1)}, bf16[128,1024]{1,0:T(8,128)(2,1)S(1)}, u32[]{:S(2)}, u32[]{:S(2)}) collective-permute-start(bf16[128,1024]{1,0:T(8,128)(2,1)S(1)} %shard_map.59), channel_id=1, source_target_pairs={{0,1},{1,0},{2,3},{3,2},{4,5},{5,4},{6,7},{7,6},{8,9},{9,8},{10,11... | collective-permute-start | bytes 786440 | tf_op jit(solution)/shard_map/ppermute | solution.py:254
  47.8 4.0 %collective-permute-start.14 = (bf16[4,128,128]{1,2,0:T(8,128)(2,1)S(1)}, bf16[4,128,128]{1,2,0:T(8,128)(2,1)S(1)}, u32[]{:S(2)}, u32[]{:S(2)}) collective-permute-start(bf16[4,128,128]{1,2,0:T(8,128)(2,1)S(1)} %dynamic-slice_bitcast_fusion), channel_id=1, source_target_pairs={{0,1},{1,0},{2,3},{3,2},{4,5},{5,4},{6,7},{7,6},{8,9},{9,8},{10,11... | collective-permute-start | bytes 393224 | tf_op jit(solution)/shard_map/ppermute | solution.py:254
  48.4 14.3 %collective-permute-start.17 = (bf16[128,1024]{1,0:T(8,128)(2,1)S(1)}, bf16[128,1024]{1,0:T(8,128)(2,1)S(1)}, u32[]{:S(2)}, u32[]{:S(2)}) collective-permute-start(bf16[128,1024]{1,0:T(8,128)(2,1)S(1)} %shard_map.59), channel_id=1, source_target_pairs={{0,6},{2,4},{4,2},{6,0},{8,14},{10,12},{12,10},{14,8},{16,22},{18,... | collective-permute-start | bytes 786440 | tf_op jit(solution)/shard_map/ppermute | solution.py:254
  50.2 13.2 %collective-permute-start.16 = (bf16[128,1024]{1,0:T(8,128)(2,1)S(1)}, bf16[128,1024]{1,0:T(8,128)(2,1)S(1)}, u32[]{:S(2)}, u32[]{:S(2)}) collective-permute-start(bf16[128,1024]{1,0:T(8,128)(2,1)S(1)} %shard_map.59), channel_id=1, source_target_pairs={{0,4},{2,6},{4,0},{6,2},{8,12},{10,14},{12,8},{14,10},{16,20},{18,... | collective-permute-start | bytes 786440 | tf_op jit(solution)/shard_map/ppermute | solution.py:254
  51.3 11.4 %collective-permute-start.10 = (bf16[128,1024]{1,0:T(8,128)(2,1)S(1)}, bf16[128,1024]{1,0:T(8,128)(2,1)S(1)}, u32[]{:S(2)}, u32[]{:S(2)}) collective-permute-start(bf16[128,1024]{1,0:T(8,128)(2,1)S(1)} %shard_map.59), channel_id=1, source_target_pairs={{0,2},{2,0},{4,6},{6,4},{8,10},{10,8},{12,14},{14,12},{16,18},{18,... | collective-permute-start | bytes 786440 | tf_op jit(solution)/shard_map/ppermute | solution.py:254
  62.7 2.1 %collective-permute-start.18 = (bf16[128,1024]{1,0:T(8,128)(2,1)S(1)}, bf16[128,1024]{1,0:T(8,128)(2,1)S(1)}, u32[]{:S(2)}, u32[]{:S(2)}) collective-permute-start(bf16[128,1024]{1,0:T(8,128)(2,1)S(1)} %collective-permute-done.10), channel_id=1, source_target_pairs={{0,1},{1,0},{2,3},{3,2},{4,5},{5,4},{6,7},{7,6},{8,9},{9,8},{10,11... | collective-permute-start | bytes 786440 | tf_op jit(solution)/shard_map/ppermute | solution.py:254
  62.7 1.9 %collective-permute-start.20 = (bf16[128,1024]{1,0:T(8,128)(2,1)S(1)}, bf16[128,1024]{1,0:T(8,128)(2,1)S(1)}, u32[]{:S(2)}, u32[]{:S(2)}) collective-permute-start(bf16[128,1024]{1,0:T(8,128)(2,1)S(1)} %collective-permute-done.17), channel_id=1, source_target_pairs={{0,1},{1,0},{2,3},{3,2},{4,5},{5,4},{6,7},{7,6},{8,9},{9,8},{10,11... | collective-permute-start | bytes 786440 | tf_op jit(solution)/shard_map/ppermute | solution.py:254
  63.4 1.6 %collective-permute-start.19 = (bf16[128,1024]{1,0:T(8,128)(2,1)S(1)}, bf16[128,1024]{1,0:T(8,128)(2,1)S(1)}, u32[]{:S(2)}, u32[]{:S(2)}) collective-permute-start(bf16[128,1024]{1,0:T(8,128)(2,1)S(1)} %collective-permute-done.16), channel_id=1, source_target_pairs={{0,1},{1,0},{2,3},{3,2},{4,5},{5,4},{6,7},{7,6},{8,9},{9,8},{10,11... | collective-permute-start | bytes 786440 | tf_op jit(solution)/shard_map/ppermute | solution.py:254
  65.4 6.9 %collective-permute-start.23 = (bf16[32,1024]{1,0:T(8,128)(2,1)S(1)}, bf16[32,1024]{1,0:T(8,128)(2,1)S(1)}, u32[]{:S(2)}, u32[]{:S(2)}) collective-permute-start(bf16[32,1024]{1,0:T(8,128)(2,1)S(1)} %get-tuple-element.56), channel_id=1, source_target_pairs={{0,24},{2,26},{4,28},{6,30},{8,16},{10,18},{12,20},{14,22},{16,8},... | collective-permute-start | bytes 196616 | tf_op jit(solution)/shard_map/ppermute | solution.py:254
  68.1 6.2 %collective-permute-start.22 = (bf16[32,1024]{1,0:T(8,128)(2,1)S(1)}, bf16[32,1024]{1,0:T(8,128)(2,1)S(1)}, u32[]{:S(2)}, u32[]{:S(2)}) collective-permute-start(bf16[32,1024]{1,0:T(8,128)(2,1)S(1)} %get-tuple-element.57), channel_id=1, source_target_pairs={{0,16},{2,18},{4,20},{6,22},{8,24},{10,26},{12,28},{14,30},{16,0},... | collective-permute-start | bytes 196616 | tf_op jit(solution)/shard_map/ppermute | solution.py:254
  68.1 6.2 %collective-permute-start.21 = (bf16[32,1024]{1,0:T(8,128)(2,1)S(1)}, bf16[32,1024]{1,0:T(8,128)(2,1)S(1)}, u32[]{:S(2)}, u32[]{:S(2)}) collective-permute-start(bf16[32,1024]{1,0:T(8,128)(2,1)S(1)} %get-tuple-element.55), channel_id=1, source_target_pairs={{0,8},{2,10},{4,12},{6,14},{8,0},{10,2},{12,4},{14,6},{16,24},{18,... | collective-permute-start | bytes 196616 | tf_op jit(solution)/shard_map/ppermute | solution.py:254

commit v7 on v6

--- a/solution.py
+++ b/solution.py
@@ -1,3 +1,5 @@
+import functools
+
 import jax
 import jax.numpy as jnp
 from jax import lax
@@ -110,7 +112,7 @@
     )(*gathered)
 
 
-def attend_kernel(left, grd, *refs):
+def attend_kernel(begin, left, grd, *refs):
     count = (len(refs) - 10) // 3
     groups = [refs[3 * i : 3 * i + 3] for i in range(count)]
     out_ref, sc0, sc1, pg0, pg1, ds0, ds1, tp0, tp1, acc = refs[3 * count :]
@@ -135,13 +137,13 @@
         g, j = places[t]
         span = slice(j * TILE, (j + 1) * TILE)
         at = slice(t * TILE, (t + 1) * TILE)
-        right = jnp.concatenate([left[2 * step], left[2 * step + 1]], axis=1)
+        right = jnp.concatenate([left[begin + 2 * step], left[begin + 2 * step + 1]], axis=1)
         wide = jnp.concatenate([groups[g][0][0, span, :], groups[g][0][1, span, :]], axis=1)
         s = jnp.dot(wide, tied(right, gate), preferred_element_type=jnp.float32)
         sc[slot][at, :] = s
         top = jnp.max(s.reshape(TILE // 8, 8, rows), axis=0)
         tp[slot][...] = top if t == 0 else jnp.maximum(tp[slot][...], top)
-        right = jnp.concatenate([grd[2 * step], grd[2 * step + 1]], axis=1)
+        right = jnp.concatenate([grd[begin + 2 * step], grd[begin + 2 * step + 1]], axis=1)
         pg[slot][at, :] = jnp.dot(
             groups[g][1][span, :], tied(right, gate), preferred_element_type=jnp.float32
         )
@@ -225,16 +227,15 @@
     finish(steps - 1)
 
 
-def attend(rows_of, groups, tok):
+def attend(rows_of, groups, tok, begin, heads):
     left, grd = rows_of
-    heads = left.shape[0]
     total = sum(g[1].shape[0] for g in groups)
     lanes = 2 * HD
     rows = 2 * tok
     operands = [left, grd] + [x for g in groups for x in g]
     work = heads * tok * total
     return pl.pallas_call(
-        attend_kernel,
+        functools.partial(attend_kernel, begin),
         in_specs=[pl.BlockSpec(memory_space=pltpu.VMEM)] * len(operands),
         out_specs=pl.BlockSpec(memory_space=pltpu.VMEM),
         out_shape=jax.ShapeDtypeStruct((tok, heads * HD), jnp.bfloat16),
@@ -284,27 +285,36 @@
 
     x_part = [lax.dynamic_index_in_dim(x5, part ^ k, 0, keepdims=False) for k in range(low)]
     x_part = [x_part[0]] + [xor_permute(x_part[k], "seq", k) for k in range(1, low)]
+
+    def product(x, grad):
+        return lax.dot_general(
+            x, grad, (((0,), (0,)), ((), ())), preferred_element_type=jnp.float32
+        )
+
+    def spread(grad):
+        return [grad] + [xor_permute(grad, "seq", k) for k in range(1, low)]
+
+    heads = width // HD
+    cut = heads * 3 // 4
+    most = spread(attend(left, groups, tok, 0, cut))
+    rest = attend(left, groups, tok, cut, heads - cut)
+    x_part, _ = tie((x_part, rest))
     x_part = jnp.stack(x_part)
     x_mine = lax.dynamic_index_in_dim(x_part, me, 1, keepdims=False)
     x_pair = lax.dynamic_index_in_dim(x_part, 1 - me, 1, keepdims=False)
     x_pair = xor_permute(x_pair, "pair", 1)
-
-    mine = attend(left, groups, tok)
-
-    def product(x, grad):
-        return lax.dot_general(
-            x, grad, (((0,), (0,)), ((), ())), preferred_element_type=jnp.float32
-        )
-
-    grads = [mine] + [xor_permute(mine, "seq", k) for k in range(1, low)]
-    pairs = [xor_permute(mine, "pair", 1)]
-    block = product(x_mine[0], mine) + product(x_pair[0], pairs[0])
-    grads[1], block = tie((grads[1], block))
-    pairs += [xor_permute(g, "pair", 1) for g in grads[1:]]
+    rest = spread(rest)
+    pairs = [xor_permute(g, "pair", 1) for g in most]
+    block = sum(product(x_mine[k], most[k]) + product(x_pair[k], pairs[k]) for k in range(low))
+    pairs = [xor_permute(rest[0], "pair", 1)]
+    last = product(x_mine[0], rest[0]) + product(x_pair[0], pairs[0])
+    rest[1:], block, last = tie((rest[1:], block, last))
+    pairs += [xor_permute(g, "pair", 1) for g in rest[1:]]
     for k in range(1, low):
-        block = block + product(x_mine[k], grads[k])
+        last = last + product(x_mine[k], rest[k])
     for k in range(1, low):
-        block = block + product(x_pair[k], pairs[k])
+        last = last + product(x_pair[k], pairs[k])
+    block = jnp.concatenate([block, last], axis=1)
     block = block.reshape(high, piece, width)
     total = lax.dynamic_index_in_dim(block, layer, 0, keepdims=False)
     sent = block.astype(jnp.bfloat16)

time: 75.3 us -> 85.7 us (1.14)
  starting transfers between devices: 23 us -> 28.6 us
  Pallas kernels: 24.4 us -> 29.5 us
  waiting for transfers between devices: 21.3 us -> 19.9 us
  matrix products: 1.72 us -> 2.66 us
    ppermute x24 -> x31, starting transfers between devices: 23 us -> 28.6 us  [xor_permute(): return lax.ppermute(x, axis, [(i, i ^ mask) for i in range(n)])]
    pallas_call x1 -> x2, Pallas kernels: 21.1 us -> 26.2 us  [attend(): pl.pallas_call(functools.partial(attend_kernel, begin), in_specs=[pl.Bloc...]
    ppermute x24 -> x31, waiting for transfers between devices: 21.3 us -> 19.9 us  [xor_permute(): return lax.ppermute(x, axis, [(i, i ^ mask) for i in range(n)])]
    dot_general x8 -> x16, matrix products: 1.72 us -> 2.66 us  [product(): lax.dot_general(x, grad, (((0,), (0,)), ((), ())), preferred_element_type...]
  transfers between devices with their start and end apart: 24 -> 31, of which waited for: 7 -> 13; matrix products, arithmetic and copies ran while one was open for 4% -> 4% of each run, Pallas kernels for 32% -> 35%
where the time goes in v7:
time: 85.7 us; the launch traced here: 85.4 us
  Pallas kernels  29.5 us (34%)
  starting transfers between devices  28.6 us (33%)
  waiting for transfers between devices  19.9 us (23%)
  matrix products  2.66 us (3%)
  other arithmetic  2.28 us (3%)
  local copies, waits for them, and re-layouts  2.2 us (3%)
    ppermute x31, starting transfers between devices, xor_permute(): return lax.ppermute(x, axis, [(i, i ^ mask) for i in range(n)])  28.6 us
    pallas_call x2, Pallas kernels, attend(): pl.pallas_call(functools.partial(attend_kernel, begin), in_specs=[pl.Bloc...  26.2 us
    ppermute x31, waiting for transfers between devices, xor_permute(): return lax.ppermute(x, axis, [(i, i ^ mask) for i in range(n)])  19.9 us
    pallas_call x3, Pallas kernels, prepare_keys(): pl.pallas_call(prepare_keys_kernel, out_shape=(jax.ShapeDtypeStruct((2, b...  2.92 us
    dot_general x16, matrix products, product(): lax.dot_general(x, grad, (((0,), (0,)), ((), ())), preferred_element_type...  2.66 us
    unnamed x7, local copies, waits for them, and re-layouts  2.12 us
  transfers between devices with their start and end apart: 31, of which 13 were waited for; matrix products, arithmetic and copies ran while one was open for 4% of the time, Pallas kernels for 35%

profile of v7, /device:TPU:0, one launch (start us, length us, event | category | flops | bytes accessed | tf_op | source)
XLA Modules:
  0.0 85.4 jit_solution(15336918975611337248)
XLA Ops:
  0.0 0.7 bitcast_convert_fusion
  0.7 0.8 maximum_bitcast_fusion
  1.5 5.1 %collective-permute-start = (bf16[1,144,128]{2,1,0:T(8,128)(2,1)S(1)}, bf16[1,144,128]{2,1,0:T(8,128)(2,1)S(1)}, u32[]{:S(2)}, u32[]{:S(2)}) collective-permute-start(bf16[1,144,128]{2,1,0:T(8,128)(2,1)S(1)} %maximum_bitcast_fusion), channel_id=1, source_target_pairs={{0,24},{2,26},{4,28},{6,30},{8,16},{10,18},{12,20},{14,22},{16,8},... | collective-permute-start | bytes 110600 | tf_op jit(solution)/shard_map/ppermute | solution.py:255
  6.5 0.6 collective-permute-start.1
  7.1 1.1 %copy.6 = bf16[128,1024]{0,1:T(8,128)(2,1)S(1)} copy(bf16[128,1024]{1,0:T(8,128)(2,1)} %param.6) | data formatting | bytes 524288 | tf_op args[0]
  8.3 0.9 %copy-done = bf16[128,1024]{1,0:T(8,128)(2,1)S(1)} copy-done((bf16[128,1024]{1,0:T(8,128)(2,1)S(1)}, bf16[128,1024]{1,0:T(8,128)(2,1)}, u32[]{:S(2)}) %copy-start) | copy-done | bytes 262168
  9.2 0.1 copy-done.1
  9.3 0.3 shard_map.55
  9.6 1.8 %collective-permute-done.2 = bf16[1,144,128]{2,1,0:T(8,128)(2,1)S(1)} collective-permute-done((bf16[1,144,128]{2,1,0:T(8,128)(2,1)S(1)}, bf16[1,144,128]{2,1,0:T(8,128)(2,1)S(1)}, u32[]{:S(2)}, u32[]{:S(2)}) %collective-permute-start.2) | collective-permute-done | bytes 36896 | tf_op jit(solution)/shard_map/ppermute | solution.py:255
  11.4 2.5 %collective-permute-start.3 = (bf16[4,144,128]{2,1,0:T(8,128)(2,1)S(1)}, bf16[4,144,128]{2,1,0:T(8,128)(2,1)S(1)}, u32[]{:S(2)}, u32[]{:S(2)}) collective-permute-start(bf16[4,144,128]{2,1,0:T(8,128)(2,1)S(1)} %pad_maximum_fusion.2.refs_0_), channel_id=1, source_target_pairs={{0,6},{2,4},{4,2},{6,0},{8,14},{10,12},{12,10},{14,8},{16,22},{18,... | collective-permute-start | bytes 442376 | tf_op jit(solution)/shard_map/ppermute | solution.py:255
  13.9 0.5 collective-permute-start.5
  14.5 0.5 collective-permute-start.6
  15.0 0.4 shard_map.56
  15.4 2.8 %collective-permute-done.3.refs_2_ = bf16[4,144,128]{2,1,0:T(8,128)(2,1)S(1)} collective-permute-done((bf16[4,144,128]{2,1,0:T(8,128)(2,1)S(1)}, bf16[4,144,128]{2,1,0:T(8,128)(2,1)S(1)}, u32[]{:S(2)}, u32[]{:S(2)}) %collective-permute-start.3) | collective-permute-done | bytes 147488 | tf_op jit(solution)/shard_map/ppermute | solution.py:255
  18.1 0.5 collective-permute-start.7
  18.6 1.2 %collective-permute-done.5.refs_0_ = bf16[4,144,128]{2,1,0:T(8,128)(2,1)S(1)} collective-permute-done((bf16[4,144,128]{2,1,0:T(8,128)(2,1)S(1)}, bf16[4,144,128]{2,1,0:T(8,128)(2,1)S(1)}, u32[]{:S(2)}, u32[]{:S(2)}) %collective-permute-start.5) | collective-permute-done | bytes 147488 | tf_op jit(solution)/shard_map/ppermute | solution.py:255
  19.8 0.5 collective-permute-start.9
  20.3 1.6 %collective-permute-start.13 = (bf16[2,128,128]{1,2,0:T(8,128)(2,1)S(1)}, bf16[2,128,128]{1,2,0:T(8,128)(2,1)S(1)}, u32[]{:S(2)}, u32[]{:S(2)}) collective-permute-start(bf16[2,128,128]{1,2,0:T(8,128)(2,1)S(1)} %get-tuple-element.74), channel_id=1, source_target_pairs={{0,2},{2,0},{4,6},{6,4},{8,10},{10,8},{12,14},{14,12},{16,18},{18,... | collective-permute-start | bytes 196616 | tf_op jit(solution)/shard_map/ppermute | solution.py:255
  21.9 1.1 %shard_map.57 = (bf16[2,1536,128]{2,1,0:T(8,128)(2,1)S(1)}, bf16[1536,128]{1,0:T(8,128)(2,1)S(1)}, bf16[12,64,128]{2,1,0:T(8,128)(2,1)S(1)}) custom-call(bf16[4,144,128]{2,1,0:T(8,128)(2,1)S(1)} %collective-permute-done.5.refs_0_, bf16[4,144,128]{2,1,0:T(8,128)(2,1)S(1)} %collective-permute-done.6.refs_1_, ...), custom_call_target="tpu_custom_call" | custom-call | flops 12000000 | bytes 1200000 | tf_op jit(solution)/shard_map/pallas_call | solution.py:101
  23.0 1.0 %collective-permute-start.14 = (bf16[2,128,128]{1,2,0:T(8,128)(2,1)S(1)}, bf16[2,128,128]{1,2,0:T(8,128)(2,1)S(1)}, u32[]{:S(2)}, u32[]{:S(2)}) collective-permute-start(bf16[2,128,128]{1,2,0:T(8,128)(2,1)S(1)} %get-tuple-element.73), channel_id=1, source_target_pairs={{0,4},{2,6},{4,0},{6,2},{8,12},{10,14},{12,8},{14,10},{16,20},{18,... | collective-permute-start | bytes 196616 | tf_op jit(solution)/shard_map/ppermute | solution.py:255
  24.0 1.1 %collective-permute-start.15 = (bf16[2,128,128]{1,2,0:T(8,128)(2,1)S(1)}, bf16[2,128,128]{1,2,0:T(8,128)(2,1)S(1)}, u32[]{:S(2)}, u32[]{:S(2)}) collective-permute-start(bf16[2,128,128]{1,2,0:T(8,128)(2,1)S(1)} %get-tuple-element.72), channel_id=1, source_target_pairs={{0,6},{2,4},{4,2},{6,0},{8,14},{10,12},{12,10},{14,8},{16,22},{18,... | collective-permute-start | bytes 196616 | tf_op jit(solution)/shard_map/ppermute | solution.py:255
  25.1 1.4 %shard_map.58 = (bf16[2,2048,128]{2,1,0:T(8,128)(2,1)S(1)}, bf16[2048,128]{1,0:T(8,128)(2,1)S(1)}, bf16[16,64,128]{2,1,0:T(8,128)(2,1)S(1)}) custom-call(bf16[4,144,128]{2,1,0:T(8,128)(2,1)S(1)} %collective-permute-done.7.refs_0_, bf16[4,144,128]{2,1,0:T(8,128)(2,1)S(1)} %collective-permute-done.8.refs_1_, ...), custom_call_target="tpu_custom_call" | custom-call | flops 16000000 | bytes 1600000 | tf_op jit(solution)/shard_map/pallas_call | solution.py:101
  26.5 10.1 %shard_map.59 = bf16[128,256]{1,0:T(8,128)(2,1)S(1)} custom-call(bf16[16,256,128]{2,1,0:T(8,128)(2,1)S(1)} %get-tuple-element.39.left, bf16[16,128,128]{2,1,0:T(8,128)(2,1)S(1)} %get-tuple-element.40.grd, bf16[2,512,128]{2,1,0:T(8,128)(2,1)S(1)} %get-tuple-element.45.refs_0_, bf16[512,128]{1,0:T(8,128)(2,1)S(1)} %get-tuple-element.46.refs_1_, ...), custom_call_target="tpu_custom_call" | custom-call | flops 805306368 | bytes 10000000 | tf_op jit(solution)/shard_map/pallas_call | solution.py:237
  36.6 1.6 %collective-permute-start.10 = (bf16[128,256]{1,0:T(8,128)(2,1)S(1)}, bf16[128,256]{1,0:T(8,128)(2,1)S(1)}, u32[]{:S(2)}, u32[]{:S(2)}) collective-permute-start(bf16[128,256]{1,0:T(8,128)(2,1)S(1)} %shard_map.59), channel_id=1, source_target_pairs={{0,2},{2,0},{4,6},{6,4},{8,10},{10,8},{12,14},{14,12},{16,18},{18,... | collective-permute-start | bytes 196616 | tf_op jit(solution)/shard_map/ppermute | solution.py:255
  38.2 0.9 %collective-permute-start.11 = (bf16[128,256]{1,0:T(8,128)(2,1)S(1)}, bf16[128,256]{1,0:T(8,128)(2,1)S(1)}, u32[]{:S(2)}, u32[]{:S(2)}) collective-permute-start(bf16[128,256]{1,0:T(8,128)(2,1)S(1)} %shard_map.59), channel_id=1, source_target_pairs={{0,4},{2,6},{4,0},{6,2},{8,12},{10,14},{12,8},{14,10},{16,20},{18,... | collective-permute-start | bytes 196616 | tf_op jit(solution)/shard_map/ppermute | solution.py:255
  39.1 1.1 %collective-permute-start.12 = (bf16[128,256]{1,0:T(8,128)(2,1)S(1)}, bf16[128,256]{1,0:T(8,128)(2,1)S(1)}, u32[]{:S(2)}, u32[]{:S(2)}) collective-permute-start(bf16[128,256]{1,0:T(8,128)(2,1)S(1)} %shard_map.59), channel_id=1, source_target_pairs={{0,6},{2,4},{4,2},{6,0},{8,14},{10,12},{12,10},{14,8},{16,22},{18,... | collective-permute-start | bytes 196616 | tf_op jit(solution)/shard_map/ppermute | solution.py:255
  40.3 0.6 collective-permute-start.16
  40.8 16.1 %shard_map.60 = bf16[128,768]{1,0:T(8,128)(2,1)S(1)} custom-call(bf16[16,256,128]{2,1,0:T(8,128)(2,1)S(1)} %get-tuple-element.39.left, bf16[16,128,128]{2,1,0:T(8,128)(2,1)S(1)} %get-tuple-element.40.grd, bf16[2,512,128]{2,1,0:T(8,128)(2,1)S(1)} %get-tuple-element.45.refs_0_, bf16[512,128]{1,0:T(8,128)(2,1)S(1)} %get-tuple-element.46.refs_1_, ...), custom_call_target="tpu_custom_call" | custom-call | flops 2415919104 | bytes 10000000 | tf_op jit(solution)/shard_map/pallas_call | solution.py:237
  57.0 1.9 %collective-permute-start.22 = (bf16[128,768]{1,0:T(8,128)(2,1)S(1)}, bf16[128,768]{1,0:T(8,128)(2,1)S(1)}, u32[]{:S(2)}, u32[]{:S(2)}) collective-permute-start(bf16[128,768]{1,0:T(8,128)(2,1)S(1)} %shard_map.60), channel_id=1, source_target_pairs={{0,6},{2,4},{4,2},{6,0},{8,14},{10,12},{12,10},{14,8},{16,22},{18,... | collective-permute-start | bytes 589832 | tf_op jit(solution)/shard_map/ppermute | solution.py:255
  58.9 0.1 fusion.5
  59.0 0.2 convolution_add_fusion.4
  59.2 1.1 %collective-permute-done.17 = bf16[128,768]{1,0:T(8,128)(2,1)S(1)} collective-permute-done((bf16[128,768]{1,0:T(8,128)(2,1)S(1)}, bf16[128,768]{1,0:T(8,128)(2,1)S(1)}, u32[]{:S(2)}, u32[]{:S(2)}) %collective-permute-start.17) | collective-permute-done | bytes 196640 | tf_op jit(solution)/shard_map/ppermute | solution.py:255
  60.3 1.1 %collective-permute-start.20 = (bf16[128,768]{1,0:T(8,128)(2,1)S(1)}, bf16[128,768]{1,0:T(8,128)(2,1)S(1)}, u32[]{:S(2)}, u32[]{:S(2)}) collective-permute-start(bf16[128,768]{1,0:T(8,128)(2,1)S(1)} %shard_map.60), channel_id=1, source_target_pairs={{0,4},{2,6},{4,0},{6,2},{8,12},{10,14},{12,8},{14,10},{16,20},{18,... | collective-permute-start | bytes 589832 | tf_op jit(solution)/shard_map/ppermute | solution.py:255
  61.4 0.2 fusion.6
  61.6 3.2 %collective-permute-done.22 = bf16[128,768]{1,0:T(8,128)(2,1)S(1)} collective-permute-done((bf16[128,768]{1,0:T(8,128)(2,1)S(1)}, bf16[128,768]{1,0:T(8,128)(2,1)S(1)}, u32[]{:S(2)}, u32[]{:S(2)}) %collective-permute-start.22) | collective-permute-done | bytes 196640 | tf_op jit(solution)/shard_map/ppermute | solution.py:255
  64.9 1.5 %collective-permute-start.18 = (bf16[128,768]{1,0:T(8,128)(2,1)S(1)}, bf16[128,768]{1,0:T(8,128)(2,1)S(1)}, u32[]{:S(2)}, u32[]{:S(2)}) collective-permute-start(bf16[128,768]{1,0:T(8,128)(2,1)S(1)} %shard_map.60), channel_id=1, source_target_pairs={{0,2},{2,0},{4,6},{6,4},{8,10},{10,8},{12,14},{14,12},{16,18},{18,... | collective-permute-start | bytes 589832 | tf_op jit(solution)/shard_map/ppermute | solution.py:255
  66.3 0.2 fusion.15
  66.5 2.4 %collective-permute-done.20 = bf16[128,768]{1,0:T(8,128)(2,1)S(1)} collective-permute-done((bf16[128,768]{1,0:T(8,128)(2,1)S(1)}, bf16[128,768]{1,0:T(8,128)(2,1)S(1)}, u32[]{:S(2)}, u32[]{:S(2)}) %collective-permute-start.20) | collective-permute-done | bytes 196640 | tf_op jit(solution)/shard_map/ppermute | solution.py:255
  69.0 0.2 fusion.13
  69.2 1.5 %collective-permute-done.18 = bf16[128,768]{1,0:T(8,128)(2,1)S(1)} collective-permute-done((bf16[128,768]{1,0:T(8,128)(2,1)S(1)}, bf16[128,768]{1,0:T(8,128)(2,1)S(1)}, u32[]{:S(2)}, u32[]{:S(2)}) %collective-permute-start.18) | collective-permute-done | bytes 196640 | tf_op jit(solution)/shard_map/ppermute | solution.py:255
  70.7 0.2 fusion.11
  70.9 0.6 collective-permute-start.19
  71.5 0.2 convolution_add_fusion
  71.7 0.5 collective-permute-done.21
  72.2 0.2 convolution_add_fusion.1
  72.4 0.2 collective-permute-done.19
  72.6 0.2 convolution_add_fusion.2
  72.8 0.2 fusion.2
  73.0 0.4 collective-permute-start.26
  73.5 0.1 fusion.12
  73.6 0.2 collective-permute-start.25
  73.8 0.1 fusion.10
  74.0 0.1 fusion.14
  74.1 0.4 collective-permute-start.27
  74.5 0.1 fusion.8
  74.7 0.2 collective-permute-done.25
  74.9 0.1 fusion.7
  75.1 0.4 collective-permute-done.27
  75.4 0.2 add_add_fusion
  75.7 2.7 %collective-permute-start.30 = (bf16[32,1024]{1,0:T(8,128)(2,1)S(1)}, bf16[32,1024]{1,0:T(8,128)(2,1)S(1)}, u32[]{:S(2)}, u32[]{:S(2)}) collective-permute-start(bf16[32,1024]{1,0:T(8,128)(2,1)S(1)} %get-tuple-element.70), channel_id=1, source_target_pairs={{0,24},{2,26},{4,28},{6,30},{8,16},{10,18},{12,20},{14,22},{16,8},... | collective-permute-start | bytes 196616 | tf_op jit(solution)/shard_map/ppermute | solution.py:255
  78.4 1.8 %collective-permute-start.28 = (bf16[32,1024]{1,0:T(8,128)(2,1)S(1)}, bf16[32,1024]{1,0:T(8,128)(2,1)S(1)}, u32[]{:S(2)}, u32[]{:S(2)}) collective-permute-start(bf16[32,1024]{1,0:T(8,128)(2,1)S(1)} %get-tuple-element.69), channel_id=1, source_target_pairs={{0,8},{2,10},{4,12},{6,14},{8,0},{10,2},{12,4},{14,6},{16,24},{18,... | collective-permute-start | bytes 196616 | tf_op jit(solution)/shard_map/ppermute | solution.py:255
  80.2 2.4 %collective-permute-done.30 = bf16[32,1024]{1,0:T(8,128)(2,1)S(1)} collective-permute-done((bf16[32,1024]{1,0:T(8,128)(2,1)S(1)}, bf16[32,1024]{1,0:T(8,128)(2,1)S(1)}, u32[]{:S(2)}, u32[]{:S(2)}) %collective-permute-start.30) | collective-permute-done | bytes 65568 | tf_op jit(solution)/shard_map/ppermute | solution.py:255
  82.5 2.2 %collective-permute-done.29 = bf16[32,1024]{1,0:T(8,128)(2,1)S(1)} collective-permute-done((bf16[32,1024]{1,0:T(8,128)(2,1)S(1)}, bf16[32,1024]{1,0:T(8,128)(2,1)S(1)}, u32[]{:S(2)}, u32[]{:S(2)}) %collective-permute-start.29) | collective-permute-done | bytes 65568 | tf_op jit(solution)/shard_map/ppermute | solution.py:255
  84.7 0.7 fusion.4
  (38 shorter events, 0.3 us)
Async XLA Ops:
  1.5 8.2 %collective-permute-start = (bf16[1,144,128]{2,1,0:T(8,128)(2,1)S(1)}, bf16[1,144,128]{2,1,0:T(8,128)(2,1)S(1)}, u32[]{:S(2)}, u32[]{:S(2)}) collective-permute-start(bf16[1,144,128]{2,1,0:T(8,128)(2,1)S(1)} %maximum_bitcast_fusion), channel_id=1, source_target_pairs={{0,24},{2,26},{4,28},{6,30},{8,16},{10,18},{12,20},{14,22},{16,8},... | collective-permute-start | bytes 110600 | tf_op jit(solution)/shard_map/ppermute | solution.py:255
  6.5 4.9 %collective-permute-start.2 = (bf16[1,144,128]{2,1,0:T(8,128)(2,1)S(1)}, bf16[1,144,128]{2,1,0:T(8,128)(2,1)S(1)}, u32[]{:S(2)}, u32[]{:S(2)}) collective-permute-start(bf16[1,144,128]{2,1,0:T(8,128)(2,1)S(1)} %maximum_bitcast_fusion), channel_id=1, source_target_pairs={{0,16},{2,18},{4,20},{6,22},{8,24},{10,26},{12,28},{14,30},{16,0},... | collective-permute-start | bytes 110600 | tf_op jit(solution)/shard_map/ppermute | solution.py:255
  6.5 4.9 %collective-permute-start.1 = (bf16[1,144,128]{2,1,0:T(8,128)(2,1)S(1)}, bf16[1,144,128]{2,1,0:T(8,128)(2,1)S(1)}, u32[]{:S(2)}, u32[]{:S(2)}) collective-permute-start(bf16[1,144,128]{2,1,0:T(8,128)(2,1)S(1)} %maximum_bitcast_fusion), channel_id=1, source_target_pairs={{0,8},{2,10},{4,12},{6,14},{8,0},{10,2},{12,4},{14,6},{16,24},{18,... | collective-permute-start | bytes 110600 | tf_op jit(solution)/shard_map/ppermute | solution.py:255
  7.1 1.2 %copy-start.2 = (s32[128,16]{0,1:T(8,128)S(1)}, s32[128,16]{0,1:T(8,128)}, u32[]{:S(2)}) copy-start(s32[128,16]{0,1:T(8,128)} %param.10) | copy-start | bytes 24580
  8.2 1.0 %copy-start = (bf16[128,1024]{1,0:T(8,128)(2,1)S(1)}, bf16[128,1024]{1,0:T(8,128)(2,1)}, u32[]{:S(2)}) copy-start(bf16[128,1024]{1,0:T(8,128)(2,1)} %q_ref.1) | copy-start | bytes 786436
  8.3 1.0 %copy-start.1 = (bf16[128,1024]{1,0:T(8,128)(2,1)S(1)}, bf16[128,1024]{1,0:T(8,128)(2,1)}, u32[]{:S(2)}) copy-start(bf16[128,1024]{1,0:T(8,128)(2,1)} %g_ref.1) | copy-start | bytes 786436
  11.4 6.7 %collective-permute-start.3 = (bf16[4,144,128]{2,1,0:T(8,128)(2,1)S(1)}, bf16[4,144,128]{2,1,0:T(8,128)(2,1)S(1)}, u32[]{:S(2)}, u32[]{:S(2)}) collective-permute-start(bf16[4,144,128]{2,1,0:T(8,128)(2,1)S(1)} %pad_maximum_fusion.2.refs_0_), channel_id=1, source_target_pairs={{0,6},{2,4},{4,2},{6,0},{8,14},{10,12},{12,10},{14,8},{16,22},{18,... | collective-permute-start | bytes 442376 | tf_op jit(solution)/shard_map/ppermute | solution.py:255
  13.9 5.9 %collective-permute-start.5 = (bf16[4,144,128]{2,1,0:T(8,128)(2,1)S(1)}, bf16[4,144,128]{2,1,0:T(8,128)(2,1)S(1)}, u32[]{:S(2)}, u32[]{:S(2)}) collective-permute-start(bf16[4,144,128]{2,1,0:T(8,128)(2,1)S(1)} %pad_maximum_fusion.2.refs_0_), channel_id=1, source_target_pairs={{0,2},{2,0},{4,6},{6,4},{8,10},{10,8},{12,14},{14,12},{16,18},{18,... | collective-permute-start | bytes 442376 | tf_op jit(solution)/shard_map/ppermute | solution.py:255
  14.5 5.3 %collective-permute-start.6 = (bf16[4,144,128]{2,1,0:T(8,128)(2,1)S(1)}, bf16[4,144,128]{2,1,0:T(8,128)(2,1)S(1)}, u32[]{:S(2)}, u32[]{:S(2)}) collective-permute-start(bf16[4,144,128]{2,1,0:T(8,128)(2,1)S(1)} %pad_maximum_fusion.2.refs_0_), channel_id=1, source_target_pairs={{0,4},{2,6},{4,0},{6,2},{8,12},{10,14},{12,8},{14,10},{16,20},{18,... | collective-permute-start | bytes 442376 | tf_op jit(solution)/shard_map/ppermute | solution.py:255
  18.1 4.9 %collective-permute-start.4 = (bf16[4,144,128]{2,1,0:T(8,128)(2,1)S(1)}, bf16[4,144,128]{2,1,0:T(8,128)(2,1)S(1)}, u32[]{:S(2)}, u32[]{:S(2)}) collective-permute-start(bf16[4,144,128]{2,1,0:T(8,128)(2,1)S(1)} %collective-permute-done.3.refs_2_), channel_id=1, source_target_pairs={{0,1},{1,0},{2,3},{3,2},{4,5},{5,4},{6,7},{7,6},{8,9},{9,8},{10,11... | collective-permute-start | bytes 442376 | tf_op jit(solution)/shard_map/ppermute | solution.py:255
  18.1 5.8 %collective-permute-start.7 = (bf16[4,144,128]{2,1,0:T(8,128)(2,1)S(1)}, bf16[4,144,128]{2,1,0:T(8,128)(2,1)S(1)}, u32[]{:S(2)}, u32[]{:S(2)}) collective-permute-start(bf16[4,144,128]{2,1,0:T(8,128)(2,1)S(1)} %pad_maximum_fusion.2.refs_0_), channel_id=1, source_target_pairs={{0,1},{1,0},{2,3},{3,2},{4,5},{5,4},{6,7},{7,6},{8,9},{9,8},{10,11... | collective-permute-start | bytes 442376 | tf_op jit(solution)/shard_map/ppermute | solution.py:255
  19.8 5.3 %collective-permute-start.8 = (bf16[4,144,128]{2,1,0:T(8,128)(2,1)S(1)}, bf16[4,144,128]{2,1,0:T(8,128)(2,1)S(1)}, u32[]{:S(2)}, u32[]{:S(2)}) collective-permute-start(bf16[4,144,128]{2,1,0:T(8,128)(2,1)S(1)} %collective-permute-done.5.refs_0_), channel_id=1, source_target_pairs={{0,1},{1,0},{2,3},{3,2},{4,5},{5,4},{6,7},{7,6},{8,9},{9,8},{10,11... | collective-permute-start | bytes 442376 | tf_op jit(solution)/shard_map/ppermute | solution.py:255
  19.8 5.3 %collective-permute-start.9 = (bf16[4,144,128]{2,1,0:T(8,128)(2,1)S(1)}, bf16[4,144,128]{2,1,0:T(8,128)(2,1)S(1)}, u32[]{:S(2)}, u32[]{:S(2)}) collective-permute-start(bf16[4,144,128]{2,1,0:T(8,128)(2,1)S(1)} %collective-permute-done.6.refs_1_), channel_id=1, source_target_pairs={{0,1},{1,0},{2,3},{3,2},{4,5},{5,4},{6,7},{7,6},{8,9},{9,8},{10,11... | collective-permute-start | bytes 442376 | tf_op jit(solution)/shard_map/ppermute | solution.py:255
  20.3 18.7 %collective-permute-start.13 = (bf16[2,128,128]{1,2,0:T(8,128)(2,1)S(1)}, bf16[2,128,128]{1,2,0:T(8,128)(2,1)S(1)}, u32[]{:S(2)}, u32[]{:S(2)}) collective-permute-start(bf16[2,128,128]{1,2,0:T(8,128)(2,1)S(1)} %get-tuple-element.74), channel_id=1, source_target_pairs={{0,2},{2,0},{4,6},{6,4},{8,10},{10,8},{12,14},{14,12},{16,18},{18,... | collective-permute-start | bytes 196616 | tf_op jit(solution)/shard_map/ppermute | solution.py:255
  23.0 17.2 %collective-permute-start.14 = (bf16[2,128,128]{1,2,0:T(8,128)(2,1)S(1)}, bf16[2,128,128]{1,2,0:T(8,128)(2,1)S(1)}, u32[]{:S(2)}, u32[]{:S(2)}) collective-permute-start(bf16[2,128,128]{1,2,0:T(8,128)(2,1)S(1)} %get-tuple-element.73), channel_id=1, source_target_pairs={{0,4},{2,6},{4,0},{6,2},{8,12},{10,14},{12,8},{14,10},{16,20},{18,... | collective-permute-start | bytes 196616 | tf_op jit(solution)/shard_map/ppermute | solution.py:255
  24.0 16.2 %collective-permute-start.15 = (bf16[2,128,128]{1,2,0:T(8,128)(2,1)S(1)}, bf16[2,128,128]{1,2,0:T(8,128)(2,1)S(1)}, u32[]{:S(2)}, u32[]{:S(2)}) collective-permute-start(bf16[2,128,128]{1,2,0:T(8,128)(2,1)S(1)} %get-tuple-element.72), channel_id=1, source_target_pairs={{0,6},{2,4},{4,2},{6,0},{8,14},{10,12},{12,10},{14,8},{16,22},{18,... | collective-permute-start | bytes 196616 | tf_op jit(solution)/shard_map/ppermute | solution.py:255
  36.6 36.4 %collective-permute-start.10 = (bf16[128,256]{1,0:T(8,128)(2,1)S(1)}, bf16[128,256]{1,0:T(8,128)(2,1)S(1)}, u32[]{:S(2)}, u32[]{:S(2)}) collective-permute-start(bf16[128,256]{1,0:T(8,128)(2,1)S(1)} %shard_map.59), channel_id=1, source_target_pairs={{0,2},{2,0},{4,6},{6,4},{8,10},{10,8},{12,14},{14,12},{16,18},{18,... | collective-permute-start | bytes 196616 | tf_op jit(solution)/shard_map/ppermute | solution.py:255
  38.2 34.8 %collective-permute-start.11 = (bf16[128,256]{1,0:T(8,128)(2,1)S(1)}, bf16[128,256]{1,0:T(8,128)(2,1)S(1)}, u32[]{:S(2)}, u32[]{:S(2)}) collective-permute-start(bf16[128,256]{1,0:T(8,128)(2,1)S(1)} %shard_map.59), channel_id=1, source_target_pairs={{0,4},{2,6},{4,0},{6,2},{8,12},{10,14},{12,8},{14,10},{16,20},{18,... | collective-permute-start | bytes 196616 | tf_op jit(solution)/shard_map/ppermute | solution.py:255
  39.1 33.9 %collective-permute-start.12 = (bf16[128,256]{1,0:T(8,128)(2,1)S(1)}, bf16[128,256]{1,0:T(8,128)(2,1)S(1)}, u32[]{:S(2)}, u32[]{:S(2)}) collective-permute-start(bf16[128,256]{1,0:T(8,128)(2,1)S(1)} %shard_map.59), channel_id=1, source_target_pairs={{0,6},{2,4},{4,2},{6,0},{8,14},{10,12},{12,10},{14,8},{16,22},{18,... | collective-permute-start | bytes 196616 | tf_op jit(solution)/shard_map/ppermute | solution.py:255
  40.2 16.8 %collective-permute-start.24 = (bf16[128,256]{1,0:T(8,128)(2,1)S(1)}, bf16[128,256]{1,0:T(8,128)(2,1)S(1)}, u32[]{:S(2)}, u32[]{:S(2)}) collective-permute-start(bf16[128,256]{1,0:T(8,128)(2,1)S(1)} %shard_map.59), channel_id=1, source_target_pairs={{0,1},{1,0},{2,3},{3,2},{4,5},{5,4},{6,7},{7,6},{8,9},{9,8},{10,11... | collective-permute-start | bytes 196616 | tf_op jit(solution)/shard_map/ppermute | solution.py:255
  40.3 18.6 %collective-permute-start.16 = (bf16[4,128,128]{1,2,0:T(8,128)(2,1)S(1)}, bf16[4,128,128]{1,2,0:T(8,128)(2,1)S(1)}, u32[]{:S(2)}, u32[]{:S(2)}) collective-permute-start(bf16[4,128,128]{1,2,0:T(8,128)(2,1)S(1)} %dynamic-slice_bitcast_fusion), channel_id=1, source_target_pairs={{0,1},{1,0},{2,3},{3,2},{4,5},{5,4},{6,7},{7,6},{8,9},{9,8},{10,11... | collective-permute-start | bytes 393224 | tf_op jit(solution)/shard_map/ppermute | solution.py:255
  57.0 7.9 %collective-permute-start.22 = (bf16[128,768]{1,0:T(8,128)(2,1)S(1)}, bf16[128,768]{1,0:T(8,128)(2,1)S(1)}, u32[]{:S(2)}, u32[]{:S(2)}) collective-permute-start(bf16[128,768]{1,0:T(8,128)(2,1)S(1)} %shard_map.60), channel_id=1, source_target_pairs={{0,6},{2,4},{4,2},{6,0},{8,14},{10,12},{12,10},{14,8},{16,22},{18,... | collective-permute-start | bytes 589832 | tf_op jit(solution)/shard_map/ppermute | solution.py:255
  58.9 1.4 %collective-permute-start.17 = (bf16[128,768]{1,0:T(8,128)(2,1)S(1)}, bf16[128,768]{1,0:T(8,128)(2,1)S(1)}, u32[]{:S(2)}, u32[]{:S(2)}) collective-permute-start(bf16[128,768]{1,0:T(8,128)(2,1)S(1)} %shard_map.60), channel_id=1, source_target_pairs={{0,1},{1,0},{2,3},{3,2},{4,5},{5,4},{6,7},{7,6},{8,9},{9,8},{10,11... | collective-permute-start | bytes 589832 | tf_op jit(solution)/shard_map/ppermute | solution.py:255
  60.3 8.6 %collective-permute-start.20 = (bf16[128,768]{1,0:T(8,128)(2,1)S(1)}, bf16[128,768]{1,0:T(8,128)(2,1)S(1)}, u32[]{:S(2)}, u32[]{:S(2)}) collective-permute-start(bf16[128,768]{1,0:T(8,128)(2,1)S(1)} %shard_map.60), channel_id=1, source_target_pairs={{0,4},{2,6},{4,0},{6,2},{8,12},{10,14},{12,8},{14,10},{16,20},{18,... | collective-permute-start | bytes 589832 | tf_op jit(solution)/shard_map/ppermute | solution.py:255
  64.9 5.9 %collective-permute-start.18 = (bf16[128,768]{1,0:T(8,128)(2,1)S(1)}, bf16[128,768]{1,0:T(8,128)(2,1)S(1)}, u32[]{:S(2)}, u32[]{:S(2)}) collective-permute-start(bf16[128,768]{1,0:T(8,128)(2,1)S(1)} %shard_map.60), channel_id=1, source_target_pairs={{0,2},{2,0},{4,6},{6,4},{8,10},{10,8},{12,14},{14,12},{16,18},{18,... | collective-permute-start | bytes 589832 | tf_op jit(solution)/shard_map/ppermute | solution.py:255
  69.0 1.9 %collective-permute-start.23 = (bf16[128,768]{1,0:T(8,128)(2,1)S(1)}, bf16[128,768]{1,0:T(8,128)(2,1)S(1)}, u32[]{:S(2)}, u32[]{:S(2)}) collective-permute-start(bf16[128,768]{1,0:T(8,128)(2,1)S(1)} %collective-permute-done.22), channel_id=1, source_target_pairs={{0,1},{1,0},{2,3},{3,2},{4,5},{5,4},{6,7},{7,6},{8,9},{9,8},{10,11... | collective-permute-start | bytes 589832 | tf_op jit(solution)/shard_map/ppermute | solution.py:255
  70.7 1.4 %collective-permute-start.21 = (bf16[128,768]{1,0:T(8,128)(2,1)S(1)}, bf16[128,768]{1,0:T(8,128)(2,1)S(1)}, u32[]{:S(2)}, u32[]{:S(2)}) collective-permute-start(bf16[128,768]{1,0:T(8,128)(2,1)S(1)} %collective-permute-done.20), channel_id=1, source_target_pairs={{0,1},{1,0},{2,3},{3,2},{4,5},{5,4},{6,7},{7,6},{8,9},{9,8},{10,11... | collective-permute-start | bytes 589832 | tf_op jit(solution)/shard_map/ppermute | solution.py:255
  70.9 1.6 %collective-permute-start.19 = (bf16[128,768]{1,0:T(8,128)(2,1)S(1)}, bf16[128,768]{1,0:T(8,128)(2,1)S(1)}, u32[]{:S(2)}, u32[]{:S(2)}) collective-permute-start(bf16[128,768]{1,0:T(8,128)(2,1)S(1)} %collective-permute-done.18), channel_id=1, source_target_pairs={{0,1},{1,0},{2,3},{3,2},{4,5},{5,4},{6,7},{7,6},{8,9},{9,8},{10,11... | collective-permute-start | bytes 589832 | tf_op jit(solution)/shard_map/ppermute | solution.py:255
  73.0 1.5 %collective-permute-start.26 = (bf16[128,256]{1,0:T(8,128)(2,1)S(1)}, bf16[128,256]{1,0:T(8,128)(2,1)S(1)}, u32[]{:S(2)}, u32[]{:S(2)}) collective-permute-start(bf16[128,256]{1,0:T(8,128)(2,1)S(1)} %collective-permute-done.11), channel_id=1, source_target_pairs={{0,1},{1,0},{2,3},{3,2},{4,5},{5,4},{6,7},{7,6},{8,9},{9,8},{10,11... | collective-permute-start | bytes 196616 | tf_op jit(solution)/shard_map/ppermute | solution.py:255
  73.6 1.3 %collective-permute-start.25 = (bf16[128,256]{1,0:T(8,128)(2,1)S(1)}, bf16[128,256]{1,0:T(8,128)(2,1)S(1)}, u32[]{:S(2)}, u32[]{:S(2)}) collective-permute-start(bf16[128,256]{1,0:T(8,128)(2,1)S(1)} %collective-permute-done.10), channel_id=1, source_target_pairs={{0,1},{1,0},{2,3},{3,2},{4,5},{5,4},{6,7},{7,6},{8,9},{9,8},{10,11... | collective-permute-start | bytes 196616 | tf_op jit(solution)/shard_map/ppermute | solution.py:255
  74.1 1.3 %collective-permute-start.27 = (bf16[128,256]{1,0:T(8,128)(2,1)S(1)}, bf16[128,256]{1,0:T(8,128)(2,1)S(1)}, u32[]{:S(2)}, u32[]{:S(2)}) collective-permute-start(bf16[128,256]{1,0:T(8,128)(2,1)S(1)} %collective-permute-done.12), channel_id=1, source_target_pairs={{0,1},{1,0},{2,3},{3,2},{4,5},{5,4},{6,7},{7,6},{8,9},{9,8},{10,11... | collective-permute-start | bytes 196616 | tf_op jit(solution)/shard_map/ppermute | solution.py:255
  75.7 6.8 %collective-permute-start.30 = (bf16[32,1024]{1,0:T(8,128)(2,1)S(1)}, bf16[32,1024]{1,0:T(8,128)(2,1)S(1)}, u32[]{:S(2)}, u32[]{:S(2)}) collective-permute-start(bf16[32,1024]{1,0:T(8,128)(2,1)S(1)} %get-tuple-element.70), channel_id=1, source_target_pairs={{0,24},{2,26},{4,28},{6,30},{8,16},{10,18},{12,20},{14,22},{16,8},... | collective-permute-start | bytes 196616 | tf_op jit(solution)/shard_map/ppermute | solution.py:255
  78.4 6.3 %collective-permute-start.29 = (bf16[32,1024]{1,0:T(8,128)(2,1)S(1)}, bf16[32,1024]{1,0:T(8,128)(2,1)S(1)}, u32[]{:S(2)}, u32[]{:S(2)}) collective-permute-start(bf16[32,1024]{1,0:T(8,128)(2,1)S(1)} %get-tuple-element.71), channel_id=1, source_target_pairs={{0,16},{2,18},{4,20},{6,22},{8,24},{10,26},{12,28},{14,30},{16,0},... | collective-permute-start | bytes 196616 | tf_op jit(solution)/shard_map/ppermute | solution.py:255
  78.4 6.3 %collective-permute-start.28 = (bf16[32,1024]{1,0:T(8,128)(2,1)S(1)}, bf16[32,1024]{1,0:T(8,128)(2,1)S(1)}, u32[]{:S(2)}, u32[]{:S(2)}) collective-permute-start(bf16[32,1024]{1,0:T(8,128)(2,1)S(1)} %get-tuple-element.69), channel_id=1, source_target_pairs={{0,8},{2,10},{4,12},{6,14},{8,0},{10,2},{12,4},{14,6},{16,24},{18,... | collective-permute-start | bytes 196616 | tf_op jit(solution)/shard_map/ppermute | solution.py:255

commit v8 on v6

--- a/solution.py
+++ b/solution.py
@@ -77,11 +77,10 @@
             res, high = [], []
             for part in range(4):
                 count = jnp.bitwise_and(jnp.right_shift(packed, 8 * part), 255)
-                live = count > 0
-                log = jnp.log(count.astype(jnp.float32))
-                hi = jnp.where(live, log, -1e30).astype(jnp.bfloat16).astype(jnp.float32)
+                log = jnp.maximum(jnp.log(count.astype(jnp.float32)), -(2.0**100))
+                hi = log.astype(jnp.bfloat16).astype(jnp.float32)
                 high.append(hi)
-                res.append(jnp.where(live, log - hi, 0.0))
+                res.append(log - hi)
             small = []
             for part in range(2):
                 a, b = res[part], res[part + 2]

time: 75.3 us -> 75.1 us (level)
  no operation moved by 1% of the time
where the time goes in v8:
time: 75.1 us; the launch traced here: 74.8 us
  Pallas kernels  24.2 us (32%)
  starting transfers between devices  23 us (31%)
  waiting for transfers between devices  21.3 us (28%)
  other arithmetic  2.23 us (3%)
  local copies, waits for them, and re-layouts  2.2 us (3%)
  matrix products  1.72 us (2%)
    ppermute x24, starting transfers between devices, xor_permute(): return lax.ppermute(x, axis, [(i, i ^ mask) for i in range(n)])  23 us
    ppermute x24, waiting for transfers between devices, xor_permute(): return lax.ppermute(x, axis, [(i, i ^ mask) for i in range(n)])  21.3 us
    pallas_call x1, Pallas kernels, attend(): pl.pallas_call(attend_kernel, in_specs=[pl.BlockSpec(memory_space=pltpu.V...  21.1 us
    pallas_call x3, Pallas kernels, prepare_keys(): pl.pallas_call(prepare_keys_kernel, out_shape=(jax.ShapeDtypeStruct((2, b...  2.7 us
    unnamed x7, local copies, waits for them, and re-layouts  2.12 us
    dot_general x8, matrix products, product(): lax.dot_general(x, grad, (((0,), (0,)), ((), ())), preferred_element_type...  1.72 us
  transfers between devices with their start and end apart: 24, of which 7 were waited for; matrix products, arithmetic and copies ran while one was open for 4% of the time, Pallas kernels for 32%

profile of v8, /device:TPU:0, one launch (start us, length us, event | category | flops | bytes accessed | tf_op | source)
XLA Modules:
  0.0 74.8 jit_solution(1943443409094749717)
XLA Ops:
  0.0 0.7 bitcast_convert_fusion
  0.7 0.8 %maximum_bitcast_fusion = bf16[1,144,128]{2,1,0:T(8,128)(2,1)S(1)} fusion(bf16[16,128]{1,0:T(8,128)(2,1)S(1)} %bitcast_convert_fusion, bf16[128,128]{1,0:T(8,128)(2,1)} %param.8), kind=kLoop, calls=%fused_computation.15 | loop fusion | flops 73728 | bytes 73728 | tf_op jit(solution)/shard_map/broadcast_in_dim | solution.py:269
  1.5 5.1 %collective-permute-start = (bf16[1,144,128]{2,1,0:T(8,128)(2,1)S(1)}, bf16[1,144,128]{2,1,0:T(8,128)(2,1)S(1)}, u32[]{:S(2)}, u32[]{:S(2)}) collective-permute-start(bf16[1,144,128]{2,1,0:T(8,128)(2,1)S(1)} %maximum_bitcast_fusion), channel_id=1, source_target_pairs={{0,24},{2,26},{4,28},{6,30},{8,16},{10,18},{12,20},{14,22},{16,8},... | collective-permute-start | bytes 110600 | tf_op jit(solution)/shard_map/ppermute | solution.py:253
  6.5 0.0 collective-permute-start.2
  6.5 0.6 collective-permute-start.1
  7.1 1.1 %copy.6 = bf16[128,1024]{0,1:T(8,128)(2,1)S(1)} copy(bf16[128,1024]{1,0:T(8,128)(2,1)} %param.6) | data formatting | bytes 524288 | tf_op args[0]
  8.2 0.0 copy-start
  8.3 0.0 copy-start.1
  8.3 0.9 %copy-done = bf16[128,1024]{1,0:T(8,128)(2,1)S(1)} copy-done((bf16[128,1024]{1,0:T(8,128)(2,1)S(1)}, bf16[128,1024]{1,0:T(8,128)(2,1)}, u32[]{:S(2)}) %copy-start) | copy-done | bytes 262168
  9.2 0.1 copy-done.1
  9.3 0.3 shard_map.55
  9.6 0.0 collective-permute-done
  9.6 1.8 %collective-permute-done.2 = bf16[1,144,128]{2,1,0:T(8,128)(2,1)S(1)} collective-permute-done((bf16[1,144,128]{2,1,0:T(8,128)(2,1)S(1)}, bf16[1,144,128]{2,1,0:T(8,128)(2,1)S(1)}, u32[]{:S(2)}, u32[]{:S(2)}) %collective-permute-start.2) | collective-permute-done | bytes 36896 | tf_op jit(solution)/shard_map/ppermute | solution.py:253
  11.4 0.0 collective-permute-done.1
  11.4 2.5 %collective-permute-start.3 = (bf16[4,144,128]{2,1,0:T(8,128)(2,1)S(1)}, bf16[4,144,128]{2,1,0:T(8,128)(2,1)S(1)}, u32[]{:S(2)}, u32[]{:S(2)}) collective-permute-start(bf16[4,144,128]{2,1,0:T(8,128)(2,1)S(1)} %pad_maximum_fusion.1.refs_0_), channel_id=1, source_target_pairs={{0,6},{2,4},{4,2},{6,0},{8,14},{10,12},{12,10},{14,8},{16,22},{18,... | collective-permute-start | bytes 442376 | tf_op jit(solution)/shard_map/ppermute | solution.py:253
  13.9 0.5 collective-permute-start.5
  14.5 0.5 collective-permute-start.6
  15.0 0.4 shard_map.56
  15.3 2.8 %collective-permute-done.3.refs_2_ = bf16[4,144,128]{2,1,0:T(8,128)(2,1)S(1)} collective-permute-done((bf16[4,144,128]{2,1,0:T(8,128)(2,1)S(1)}, bf16[4,144,128]{2,1,0:T(8,128)(2,1)S(1)}, u32[]{:S(2)}, u32[]{:S(2)}) %collective-permute-start.3) | collective-permute-done | bytes 147488 | tf_op jit(solution)/shard_map/ppermute | solution.py:253
  18.1 0.0 collective-permute-start.4
  18.1 0.5 collective-permute-start.7
  18.6 1.2 %collective-permute-done.5.refs_0_ = bf16[4,144,128]{2,1,0:T(8,128)(2,1)S(1)} collective-permute-done((bf16[4,144,128]{2,1,0:T(8,128)(2,1)S(1)}, bf16[4,144,128]{2,1,0:T(8,128)(2,1)S(1)}, u32[]{:S(2)}, u32[]{:S(2)}) %collective-permute-start.5) | collective-permute-done | bytes 147488 | tf_op jit(solution)/shard_map/ppermute | solution.py:253
  19.8 0.0 collective-permute-start.8
  19.8 0.0 collective-permute-done.6.refs_1_
  19.8 0.5 collective-permute-start.9
  20.3 1.9 %collective-permute-start.13 = (bf16[2,128,128]{1,2,0:T(8,128)(2,1)S(1)}, bf16[2,128,128]{1,2,0:T(8,128)(2,1)S(1)}, u32[]{:S(2)}, u32[]{:S(2)}) collective-permute-start(bf16[2,128,128]{1,2,0:T(8,128)(2,1)S(1)} %get-tuple-element.59), channel_id=1, source_target_pairs={{0,6},{2,4},{4,2},{6,0},{8,14},{10,12},{12,10},{14,8},{16,22},{18,... | collective-permute-start | bytes 196616 | tf_op jit(solution)/shard_map/ppermute | solution.py:253
  22.2 1.0 %shard_map.57 = (bf16[2,1536,128]{2,1,0:T(8,128)(2,1)S(1)}, bf16[1536,128]{1,0:T(8,128)(2,1)S(1)}, bf16[12,64,128]{2,1,0:T(8,128)(2,1)S(1)}) custom-call(bf16[4,144,128]{2,1,0:T(8,128)(2,1)S(1)} %collective-permute-done.5.refs_0_, bf16[4,144,128]{2,1,0:T(8,128)(2,1)S(1)} %collective-permute-done.6.refs_1_, ...), custom_call_target="tpu_custom_call" | custom-call | flops 12000000 | bytes 1200000 | tf_op jit(solution)/shard_map/pallas_call | solution.py:98
  23.3 0.0 collective-permute-done.4.refs_3_
  23.3 1.2 %collective-permute-start.12 = (bf16[2,128,128]{1,2,0:T(8,128)(2,1)S(1)}, bf16[2,128,128]{1,2,0:T(8,128)(2,1)S(1)}, u32[]{:S(2)}, u32[]{:S(2)}) collective-permute-start(bf16[2,128,128]{1,2,0:T(8,128)(2,1)S(1)} %get-tuple-element.60), channel_id=1, source_target_pairs={{0,4},{2,6},{4,0},{6,2},{8,12},{10,14},{12,8},{14,10},{16,20},{18,... | collective-permute-start | bytes 196616 | tf_op jit(solution)/shard_map/ppermute | solution.py:253
  24.4 0.0 collective-permute-done.7.refs_0_
  24.4 0.5 collective-permute-start.11
  25.0 0.0 collective-permute-done.8.refs_1_
  25.0 0.0 collective-permute-done.9.refs_2_
  25.0 1.3 %shard_map.58 = (bf16[2,2048,128]{2,1,0:T(8,128)(2,1)S(1)}, bf16[2048,128]{1,0:T(8,128)(2,1)S(1)}, bf16[16,64,128]{2,1,0:T(8,128)(2,1)S(1)}) custom-call(bf16[4,144,128]{2,1,0:T(8,128)(2,1)S(1)} %collective-permute-done.7.refs_0_, bf16[4,144,128]{2,1,0:T(8,128)(2,1)S(1)} %collective-permute-done.8.refs_1_, ...), custom_call_target="tpu_custom_call" | custom-call | flops 16000000 | bytes 1600000 | tf_op jit(solution)/shard_map/pallas_call | solution.py:98
  26.3 21.1 %shard_map.59 = bf16[128,1024]{1,0:T(8,128)(2,1)S(1)} custom-call(bf16[16,256,128]{2,1,0:T(8,128)(2,1)S(1)} %get-tuple-element.32.left, bf16[16,128,128]{2,1,0:T(8,128)(2,1)S(1)} %get-tuple-element.33.grd, bf16[2,512,128]{2,1,0:T(8,128)(2,1)S(1)} %get-tuple-element.38.refs_0_, bf16[512,128]{1,0:T(8,128)(2,1)S(1)} %get-tuple-element.39.refs_1_, ...), custom_call_target="tpu_custom_call" | custom-call | flops 3221225472 | bytes 10000000 | tf_op jit(solution)/shard_map/pallas_call | solution.py:235
  47.5 0.1 collective-permute-start.15
  47.5 0.0 collective-permute-done.13
  47.5 0.0 collective-permute-done.12
  47.6 0.5 collective-permute-start.14
  48.2 1.8 %collective-permute-start.17 = (bf16[128,1024]{1,0:T(8,128)(2,1)S(1)}, bf16[128,1024]{1,0:T(8,128)(2,1)S(1)}, u32[]{:S(2)}, u32[]{:S(2)}) collective-permute-start(bf16[128,1024]{1,0:T(8,128)(2,1)S(1)} %shard_map.59), channel_id=1, source_target_pairs={{0,6},{2,4},{4,2},{6,0},{8,14},{10,12},{12,10},{14,8},{16,22},{18,... | collective-permute-start | bytes 786440 | tf_op jit(solution)/shard_map/ppermute | solution.py:253
  50.0 1.1 %collective-permute-start.16 = (bf16[128,1024]{1,0:T(8,128)(2,1)S(1)}, bf16[128,1024]{1,0:T(8,128)(2,1)S(1)}, u32[]{:S(2)}, u32[]{:S(2)}) collective-permute-start(bf16[128,1024]{1,0:T(8,128)(2,1)S(1)} %shard_map.59), channel_id=1, source_target_pairs={{0,4},{2,6},{4,0},{6,2},{8,12},{10,14},{12,8},{14,10},{16,20},{18,... | collective-permute-start | bytes 786440 | tf_op jit(solution)/shard_map/ppermute | solution.py:253
  51.1 0.5 collective-permute-start.10
  51.7 0.2 fusion.8
  51.9 0.2 convolution_add_fusion.1
  52.1 10.4 %collective-permute-done.10 = bf16[128,1024]{1,0:T(8,128)(2,1)S(1)} collective-permute-done((bf16[128,1024]{1,0:T(8,128)(2,1)S(1)}, bf16[128,1024]{1,0:T(8,128)(2,1)S(1)}, u32[]{:S(2)}, u32[]{:S(2)}) %collective-permute-start.10) | collective-permute-done | bytes 262176 | tf_op jit(solution)/shard_map/ppermute | solution.py:253
  62.5 0.0 collective-permute-start.18
  62.5 0.0 collective-permute-done.17
  62.5 0.5 collective-permute-start.20
  63.0 0.2 fusion.7
  63.2 0.0 collective-permute-done.16
  63.2 0.1 collective-permute-start.19
  63.3 0.2 fusion.5
  63.5 0.2 fusion.6
  63.8 0.6 collective-permute-done.20
  64.4 0.2 fusion.3
  64.6 0.0 collective-permute-done.18
  64.6 0.2 fusion.4
  64.9 0.2 fusion
  65.2 2.7 %collective-permute-start.23 = (bf16[32,1024]{1,0:T(8,128)(2,1)S(1)}, bf16[32,1024]{1,0:T(8,128)(2,1)S(1)}, u32[]{:S(2)}, u32[]{:S(2)}) collective-permute-start(bf16[32,1024]{1,0:T(8,128)(2,1)S(1)} %get-tuple-element.56), channel_id=1, source_target_pairs={{0,24},{2,26},{4,28},{6,30},{8,16},{10,18},{12,20},{14,22},{16,8},... | collective-permute-start | bytes 196616 | tf_op jit(solution)/shard_map/ppermute | solution.py:253
  67.9 1.7 %collective-permute-start.21 = (bf16[32,1024]{1,0:T(8,128)(2,1)S(1)}, bf16[32,1024]{1,0:T(8,128)(2,1)S(1)}, u32[]{:S(2)}, u32[]{:S(2)}) collective-permute-start(bf16[32,1024]{1,0:T(8,128)(2,1)S(1)} %get-tuple-element.55), channel_id=1, source_target_pairs={{0,8},{2,10},{4,12},{6,14},{8,0},{10,2},{12,4},{14,6},{16,24},{18,... | collective-permute-start | bytes 196616 | tf_op jit(solution)/shard_map/ppermute | solution.py:253
  69.6 2.4 %collective-permute-done.23 = bf16[32,1024]{1,0:T(8,128)(2,1)S(1)} collective-permute-done((bf16[32,1024]{1,0:T(8,128)(2,1)S(1)}, bf16[32,1024]{1,0:T(8,128)(2,1)S(1)}, u32[]{:S(2)}, u32[]{:S(2)}) %collective-permute-start.23) | collective-permute-done | bytes 65568 | tf_op jit(solution)/shard_map/ppermute | solution.py:253
  72.1 2.1 %collective-permute-done.22 = bf16[32,1024]{1,0:T(8,128)(2,1)S(1)} collective-permute-done((bf16[32,1024]{1,0:T(8,128)(2,1)S(1)}, bf16[32,1024]{1,0:T(8,128)(2,1)S(1)}, u32[]{:S(2)}, u32[]{:S(2)}) %collective-permute-start.22) | collective-permute-done | bytes 65568 | tf_op jit(solution)/shard_map/ppermute | solution.py:253
  74.1 0.0 collective-permute-done.21
  74.1 0.7 fusion.2
  (14 shorter events, 0.2 us)
Async XLA Ops:
  1.5 8.2 %collective-permute-start = (bf16[1,144,128]{2,1,0:T(8,128)(2,1)S(1)}, bf16[1,144,128]{2,1,0:T(8,128)(2,1)S(1)}, u32[]{:S(2)}, u32[]{:S(2)}) collective-permute-start(bf16[1,144,128]{2,1,0:T(8,128)(2,1)S(1)} %maximum_bitcast_fusion), channel_id=1, source_target_pairs={{0,24},{2,26},{4,28},{6,30},{8,16},{10,18},{12,20},{14,22},{16,8},... | collective-permute-start | bytes 110600 | tf_op jit(solution)/shard_map/ppermute | solution.py:253
  6.5 4.9 %collective-permute-start.2 = (bf16[1,144,128]{2,1,0:T(8,128)(2,1)S(1)}, bf16[1,144,128]{2,1,0:T(8,128)(2,1)S(1)}, u32[]{:S(2)}, u32[]{:S(2)}) collective-permute-start(bf16[1,144,128]{2,1,0:T(8,128)(2,1)S(1)} %maximum_bitcast_fusion), channel_id=1, source_target_pairs={{0,16},{2,18},{4,20},{6,22},{8,24},{10,26},{12,28},{14,30},{16,0},... | collective-permute-start | bytes 110600 | tf_op jit(solution)/shard_map/ppermute | solution.py:253
  6.5 4.9 %collective-permute-start.1 = (bf16[1,144,128]{2,1,0:T(8,128)(2,1)S(1)}, bf16[1,144,128]{2,1,0:T(8,128)(2,1)S(1)}, u32[]{:S(2)}, u32[]{:S(2)}) collective-permute-start(bf16[1,144,128]{2,1,0:T(8,128)(2,1)S(1)} %maximum_bitcast_fusion), channel_id=1, source_target_pairs={{0,8},{2,10},{4,12},{6,14},{8,0},{10,2},{12,4},{14,6},{16,24},{18,... | collective-permute-start | bytes 110600 | tf_op jit(solution)/shard_map/ppermute | solution.py:253
  7.1 1.2 %copy-start.2 = (s32[128,16]{0,1:T(8,128)S(1)}, s32[128,16]{0,1:T(8,128)}, u32[]{:S(2)}) copy-start(s32[128,16]{0,1:T(8,128)} %param.10) | copy-start | bytes 24580
  8.2 1.0 %copy-start = (bf16[128,1024]{1,0:T(8,128)(2,1)S(1)}, bf16[128,1024]{1,0:T(8,128)(2,1)}, u32[]{:S(2)}) copy-start(bf16[128,1024]{1,0:T(8,128)(2,1)} %q_ref.1) | copy-start | bytes 786436
  8.3 1.0 %copy-start.1 = (bf16[128,1024]{1,0:T(8,128)(2,1)S(1)}, bf16[128,1024]{1,0:T(8,128)(2,1)}, u32[]{:S(2)}) copy-start(bf16[128,1024]{1,0:T(8,128)(2,1)} %g_ref.1) | copy-start | bytes 786436
  11.4 6.7 %collective-permute-start.3 = (bf16[4,144,128]{2,1,0:T(8,128)(2,1)S(1)}, bf16[4,144,128]{2,1,0:T(8,128)(2,1)S(1)}, u32[]{:S(2)}, u32[]{:S(2)}) collective-permute-start(bf16[4,144,128]{2,1,0:T(8,128)(2,1)S(1)} %pad_maximum_fusion.1.refs_0_), channel_id=1, source_target_pairs={{0,6},{2,4},{4,2},{6,0},{8,14},{10,12},{12,10},{14,8},{16,22},{18,... | collective-permute-start | bytes 442376 | tf_op jit(solution)/shard_map/ppermute | solution.py:253
  13.9 5.9 %collective-permute-start.5 = (bf16[4,144,128]{2,1,0:T(8,128)(2,1)S(1)}, bf16[4,144,128]{2,1,0:T(8,128)(2,1)S(1)}, u32[]{:S(2)}, u32[]{:S(2)}) collective-permute-start(bf16[4,144,128]{2,1,0:T(8,128)(2,1)S(1)} %pad_maximum_fusion.1.refs_0_), channel_id=1, source_target_pairs={{0,2},{2,0},{4,6},{6,4},{8,10},{10,8},{12,14},{14,12},{16,18},{18,... | collective-permute-start | bytes 442376 | tf_op jit(solution)/shard_map/ppermute | solution.py:253
  14.5 5.3 %collective-permute-start.6 = (bf16[4,144,128]{2,1,0:T(8,128)(2,1)S(1)}, bf16[4,144,128]{2,1,0:T(8,128)(2,1)S(1)}, u32[]{:S(2)}, u32[]{:S(2)}) collective-permute-start(bf16[4,144,128]{2,1,0:T(8,128)(2,1)S(1)} %pad_maximum_fusion.1.refs_0_), channel_id=1, source_target_pairs={{0,4},{2,6},{4,0},{6,2},{8,12},{10,14},{12,8},{14,10},{16,20},{18,... | collective-permute-start | bytes 442376 | tf_op jit(solution)/shard_map/ppermute | solution.py:253
  18.1 5.1 %collective-permute-start.4 = (bf16[4,144,128]{2,1,0:T(8,128)(2,1)S(1)}, bf16[4,144,128]{2,1,0:T(8,128)(2,1)S(1)}, u32[]{:S(2)}, u32[]{:S(2)}) collective-permute-start(bf16[4,144,128]{2,1,0:T(8,128)(2,1)S(1)} %collective-permute-done.3.refs_2_), channel_id=1, source_target_pairs={{0,1},{1,0},{2,3},{3,2},{4,5},{5,4},{6,7},{7,6},{8,9},{9,8},{10,11... | collective-permute-start | bytes 442376 | tf_op jit(solution)/shard_map/ppermute | solution.py:253
  18.1 6.3 %collective-permute-start.7 = (bf16[4,144,128]{2,1,0:T(8,128)(2,1)S(1)}, bf16[4,144,128]{2,1,0:T(8,128)(2,1)S(1)}, u32[]{:S(2)}, u32[]{:S(2)}) collective-permute-start(bf16[4,144,128]{2,1,0:T(8,128)(2,1)S(1)} %pad_maximum_fusion.1.refs_0_), channel_id=1, source_target_pairs={{0,1},{1,0},{2,3},{3,2},{4,5},{5,4},{6,7},{7,6},{8,9},{9,8},{10,11... | collective-permute-start | bytes 442376 | tf_op jit(solution)/shard_map/ppermute | solution.py:253
  19.8 5.2 %collective-permute-start.8 = (bf16[4,144,128]{2,1,0:T(8,128)(2,1)S(1)}, bf16[4,144,128]{2,1,0:T(8,128)(2,1)S(1)}, u32[]{:S(2)}, u32[]{:S(2)}) collective-permute-start(bf16[4,144,128]{2,1,0:T(8,128)(2,1)S(1)} %collective-permute-done.5.refs_0_), channel_id=1, source_target_pairs={{0,1},{1,0},{2,3},{3,2},{4,5},{5,4},{6,7},{7,6},{8,9},{9,8},{10,11... | collective-permute-start | bytes 442376 | tf_op jit(solution)/shard_map/ppermute | solution.py:253
  19.8 5.2 %collective-permute-start.9 = (bf16[4,144,128]{2,1,0:T(8,128)(2,1)S(1)}, bf16[4,144,128]{2,1,0:T(8,128)(2,1)S(1)}, u32[]{:S(2)}, u32[]{:S(2)}) collective-permute-start(bf16[4,144,128]{2,1,0:T(8,128)(2,1)S(1)} %collective-permute-done.6.refs_1_), channel_id=1, source_target_pairs={{0,1},{1,0},{2,3},{3,2},{4,5},{5,4},{6,7},{7,6},{8,9},{9,8},{10,11... | collective-permute-start | bytes 442376 | tf_op jit(solution)/shard_map/ppermute | solution.py:253
  20.3 27.2 %collective-permute-start.13 = (bf16[2,128,128]{1,2,0:T(8,128)(2,1)S(1)}, bf16[2,128,128]{1,2,0:T(8,128)(2,1)S(1)}, u32[]{:S(2)}, u32[]{:S(2)}) collective-permute-start(bf16[2,128,128]{1,2,0:T(8,128)(2,1)S(1)} %get-tuple-element.59), channel_id=1, source_target_pairs={{0,6},{2,4},{4,2},{6,0},{8,14},{10,12},{12,10},{14,8},{16,22},{18,... | collective-permute-start | bytes 196616 | tf_op jit(solution)/shard_map/ppermute | solution.py:253
  23.3 24.3 %collective-permute-start.12 = (bf16[2,128,128]{1,2,0:T(8,128)(2,1)S(1)}, bf16[2,128,128]{1,2,0:T(8,128)(2,1)S(1)}, u32[]{:S(2)}, u32[]{:S(2)}) collective-permute-start(bf16[2,128,128]{1,2,0:T(8,128)(2,1)S(1)} %get-tuple-element.60), channel_id=1, source_target_pairs={{0,4},{2,6},{4,0},{6,2},{8,12},{10,14},{12,8},{14,10},{16,20},{18,... | collective-permute-start | bytes 196616 | tf_op jit(solution)/shard_map/ppermute | solution.py:253
  24.4 23.1 %collective-permute-start.11 = (bf16[2,128,128]{1,2,0:T(8,128)(2,1)S(1)}, bf16[2,128,128]{1,2,0:T(8,128)(2,1)S(1)}, u32[]{:S(2)}, u32[]{:S(2)}) collective-permute-start(bf16[2,128,128]{1,2,0:T(8,128)(2,1)S(1)} %get-tuple-element.61), channel_id=1, source_target_pairs={{0,2},{2,0},{4,6},{6,4},{8,10},{10,8},{12,14},{14,12},{16,18},{18,... | collective-permute-start | bytes 196616 | tf_op jit(solution)/shard_map/ppermute | solution.py:253
  47.5 4.2 %collective-permute-start.15 = (bf16[128,1024]{1,0:T(8,128)(2,1)S(1)}, bf16[128,1024]{1,0:T(8,128)(2,1)S(1)}, u32[]{:S(2)}, u32[]{:S(2)}) collective-permute-start(bf16[128,1024]{1,0:T(8,128)(2,1)S(1)} %shard_map.59), channel_id=1, source_target_pairs={{0,1},{1,0},{2,3},{3,2},{4,5},{5,4},{6,7},{7,6},{8,9},{9,8},{10,11... | collective-permute-start | bytes 786440 | tf_op jit(solution)/shard_map/ppermute | solution.py:253
  47.6 4.0 %collective-permute-start.14 = (bf16[4,128,128]{1,2,0:T(8,128)(2,1)S(1)}, bf16[4,128,128]{1,2,0:T(8,128)(2,1)S(1)}, u32[]{:S(2)}, u32[]{:S(2)}) collective-permute-start(bf16[4,128,128]{1,2,0:T(8,128)(2,1)S(1)} %dynamic-slice_bitcast_fusion), channel_id=1, source_target_pairs={{0,1},{1,0},{2,3},{3,2},{4,5},{5,4},{6,7},{7,6},{8,9},{9,8},{10,11... | collective-permute-start | bytes 393224 | tf_op jit(solution)/shard_map/ppermute | solution.py:253
  48.2 14.3 %collective-permute-start.17 = (bf16[128,1024]{1,0:T(8,128)(2,1)S(1)}, bf16[128,1024]{1,0:T(8,128)(2,1)S(1)}, u32[]{:S(2)}, u32[]{:S(2)}) collective-permute-start(bf16[128,1024]{1,0:T(8,128)(2,1)S(1)} %shard_map.59), channel_id=1, source_target_pairs={{0,6},{2,4},{4,2},{6,0},{8,14},{10,12},{12,10},{14,8},{16,22},{18,... | collective-permute-start | bytes 786440 | tf_op jit(solution)/shard_map/ppermute | solution.py:253
  50.0 13.2 %collective-permute-start.16 = (bf16[128,1024]{1,0:T(8,128)(2,1)S(1)}, bf16[128,1024]{1,0:T(8,128)(2,1)S(1)}, u32[]{:S(2)}, u32[]{:S(2)}) collective-permute-start(bf16[128,1024]{1,0:T(8,128)(2,1)S(1)} %shard_map.59), channel_id=1, source_target_pairs={{0,4},{2,6},{4,0},{6,2},{8,12},{10,14},{12,8},{14,10},{16,20},{18,... | collective-permute-start | bytes 786440 | tf_op jit(solution)/shard_map/ppermute | solution.py:253
  51.1 11.4 %collective-permute-start.10 = (bf16[128,1024]{1,0:T(8,128)(2,1)S(1)}, bf16[128,1024]{1,0:T(8,128)(2,1)S(1)}, u32[]{:S(2)}, u32[]{:S(2)}) collective-permute-start(bf16[128,1024]{1,0:T(8,128)(2,1)S(1)} %shard_map.59), channel_id=1, source_target_pairs={{0,2},{2,0},{4,6},{6,4},{8,10},{10,8},{12,14},{14,12},{16,18},{18,... | collective-permute-start | bytes 786440 | tf_op jit(solution)/shard_map/ppermute | solution.py:253
  62.5 2.1 %collective-permute-start.18 = (bf16[128,1024]{1,0:T(8,128)(2,1)S(1)}, bf16[128,1024]{1,0:T(8,128)(2,1)S(1)}, u32[]{:S(2)}, u32[]{:S(2)}) collective-permute-start(bf16[128,1024]{1,0:T(8,128)(2,1)S(1)} %collective-permute-done.10), channel_id=1, source_target_pairs={{0,1},{1,0},{2,3},{3,2},{4,5},{5,4},{6,7},{7,6},{8,9},{9,8},{10,11... | collective-permute-start | bytes 786440 | tf_op jit(solution)/shard_map/ppermute | solution.py:253
  62.5 1.9 %collective-permute-start.20 = (bf16[128,1024]{1,0:T(8,128)(2,1)S(1)}, bf16[128,1024]{1,0:T(8,128)(2,1)S(1)}, u32[]{:S(2)}, u32[]{:S(2)}) collective-permute-start(bf16[128,1024]{1,0:T(8,128)(2,1)S(1)} %collective-permute-done.17), channel_id=1, source_target_pairs={{0,1},{1,0},{2,3},{3,2},{4,5},{5,4},{6,7},{7,6},{8,9},{9,8},{10,11... | collective-permute-start | bytes 786440 | tf_op jit(solution)/shard_map/ppermute | solution.py:253
  63.2 1.6 %collective-permute-start.19 = (bf16[128,1024]{1,0:T(8,128)(2,1)S(1)}, bf16[128,1024]{1,0:T(8,128)(2,1)S(1)}, u32[]{:S(2)}, u32[]{:S(2)}) collective-permute-start(bf16[128,1024]{1,0:T(8,128)(2,1)S(1)} %collective-permute-done.16), channel_id=1, source_target_pairs={{0,1},{1,0},{2,3},{3,2},{4,5},{5,4},{6,7},{7,6},{8,9},{9,8},{10,11... | collective-permute-start | bytes 786440 | tf_op jit(solution)/shard_map/ppermute | solution.py:253
  65.2 6.9 %collective-permute-start.23 = (bf16[32,1024]{1,0:T(8,128)(2,1)S(1)}, bf16[32,1024]{1,0:T(8,128)(2,1)S(1)}, u32[]{:S(2)}, u32[]{:S(2)}) collective-permute-start(bf16[32,1024]{1,0:T(8,128)(2,1)S(1)} %get-tuple-element.56), channel_id=1, source_target_pairs={{0,24},{2,26},{4,28},{6,30},{8,16},{10,18},{12,20},{14,22},{16,8},... | collective-permute-start | bytes 196616 | tf_op jit(solution)/shard_map/ppermute | solution.py:253
  67.9 6.2 %collective-permute-start.22 = (bf16[32,1024]{1,0:T(8,128)(2,1)S(1)}, bf16[32,1024]{1,0:T(8,128)(2,1)S(1)}, u32[]{:S(2)}, u32[]{:S(2)}) collective-permute-start(bf16[32,1024]{1,0:T(8,128)(2,1)S(1)} %get-tuple-element.57), channel_id=1, source_target_pairs={{0,16},{2,18},{4,20},{6,22},{8,24},{10,26},{12,28},{14,30},{16,0},... | collective-permute-start | bytes 196616 | tf_op jit(solution)/shard_map/ppermute | solution.py:253
  67.9 6.2 %collective-permute-start.21 = (bf16[32,1024]{1,0:T(8,128)(2,1)S(1)}, bf16[32,1024]{1,0:T(8,128)(2,1)S(1)}, u32[]{:S(2)}, u32[]{:S(2)}) collective-permute-start(bf16[32,1024]{1,0:T(8,128)(2,1)S(1)} %get-tuple-element.55), channel_id=1, source_target_pairs={{0,8},{2,10},{4,12},{6,14},{8,0},{10,2},{12,4},{14,6},{16,24},{18,... | collective-permute-start | bytes 196616 | tf_op jit(solution)/shard_map/ppermute | solution.py:253
